TPU v7x, 128 devices: a whole 4x4x4 slice. The times are simulated.
128 devices in a mesh: dp: 16 (over y_lo, z, core), zero: 8 (over y_hi, x).
Axes of the slice: x: 4, y: 4 (y_hi: 2, y_lo: 2; y = y_hi * 2 + y_lo), z: 4, core: 2. Of those that a mesh axis runs over, the one named last changes fastest.
Arguments:
- query_rows: bfloat16 [114688, 2048], P(('dp', 'zero')), may hold values from -40 to 40
- key_rows: bfloat16 [114688, 512], P(('dp', 'zero')), may hold values from -6 to 6
- value_rows: bfloat16 [114688, 512], P(('dp', 'zero')), may hold values from -6 to 6
- output_grad: bfloat16 [114688, 2048], P(('dp', 'zero')), may hold values from -6 to 6
- home_lengths: int32 [128, 6], P(('dp', 'zero')), may hold values from 1 to 96, 384 in all within a row
- moved_lengths: int32 [128, 8], P(('dp', 'zero')), may hold values from 48 to 64, as said below
- moved_offsets: int32 [128, 8], P(('dp', 'zero')), may hold values from 0 to 448, as said below
- moved_owner: int32 [128, 8], P(('dp', 'zero')), may hold values from 0 to 15, as said below
- owner_offsets: int32 [128, 8], P(('dp', 'zero')), may hold values from 0 to 448, as said below
- layer_grad: bfloat16 [16, 8, 4096, 512], P('dp', 'zero'), may hold values from -0.59765625 to 0.59765625
Outputs:
- attention: bfloat16 [114688, 2048], P(('dp', 'zero'))
- query_grad: bfloat16 [114688, 2048], P(('dp', 'zero'))
- key_grad: bfloat16 [114688, 512], P(('dp', 'zero'))
- value_grad: bfloat16 [114688, 512], P(('dp', 'zero'))
- summed_grad: float32 [4096, 512], P('zero')
Inputs may be any that keep to these rules, and one draw needn't show every extreme that they name: `moved_lengths`: every device moves exactly 8 documents, laid end to end in its last 512 rows. `moved_offsets`: each moved document starts where the one before it ends; the first starts at 0. `moved_owner`: A receiver keeps the sender's zero index. The 8 documents of one device go to 8 different dp indices, and every device receives exactly 8 documents. `owner_offsets`: the documents that a device receives lie end to end from the start of its last 512 rows, in all at most 512 rows; in every draw some device receives exactly 512 rows. `home_lengths`: each device's home documents fill its first 384 rows.
All inputs are finite; a program needn't handle non-finite values.
Results may differ from a plain program's by a relative error of at most 0.013.
Values may be sent and summed in bfloat16 or wider, within the bound.
No kernel may reach another device: no remote copies, remote signals or barrier semaphores. Data moves between devices by JAX's collectives and lax.ppermute only.
A program may use at most 128 MiB of HBM per device.

v0:
```python
import math

import jax
import jax.numpy as jnp
from jax import lax
from jax.sharding import PartitionSpec as P

HD = 128
HOME = 384
S = 64
MOVE = 512


def attend_group(pieces, allowed):
    query_matrix, key_portion, value_portion, gradient_portion = pieces
    softmax_scale = 1.0 / math.sqrt(HD)
    scores = (
        jnp.einsum("epf,zf->pez", query_matrix, key_portion, preferred_element_type=jnp.float32)
        * softmax_scale
    )
    scores = jnp.where(allowed[None], scores, -jnp.inf)
    highest = jnp.max(scores, axis=-1, keepdims=True)
    exponent = jnp.exp(scores - highest)
    weights = exponent / jnp.sum(exponent, axis=-1, keepdims=True)
    weight_brain_float = weights.astype(jnp.bfloat16)
    attention = jnp.einsum(
        "wql,lo->qwo", weight_brain_float, value_portion, preferred_element_type=jnp.float32
    ).astype(jnp.bfloat16)
    value_grad = jnp.einsum(
        "nom,onu->mu", weight_brain_float, gradient_portion, preferred_element_type=jnp.float32
    ).astype(jnp.bfloat16)
    logit_matrix = jnp.einsum(
        "epf,zf->pez", gradient_portion, value_portion, preferred_element_type=jnp.float32
    )
    row_delta = jnp.einsum(
        "rgd,rgd->gr", gradient_portion, attention, preferred_element_type=jnp.float32
    )
    score_gradient = (weights * (logit_matrix - row_delta[:, :, None])).astype(jnp.bfloat16)
    query_grad = (
        jnp.einsum("wql,lo->qwo", score_gradient, key_portion, preferred_element_type=jnp.float32)
        * softmax_scale
    ).astype(jnp.bfloat16)
    key_grad = (
        jnp.einsum("nom,onu->mu", score_gradient, query_matrix, preferred_element_type=jnp.float32)
        * softmax_scale
    ).astype(jnp.bfloat16)
    return (attention, query_grad, key_grad, value_grad)


def attend(query_matrix, keys_in, values_in, grads_in, documents):
    length = query_matrix.shape[0]
    kv_heads = keys_in.shape[1] // HD
    per_group = query_matrix.shape[1] // keys_in.shape[1]
    position = jnp.arange(length, dtype=jnp.int32)
    allowed = (documents[:, None] == documents[None, :]) & (position[None, :] <= position[:, None])
    stacked = (
        query_matrix.reshape(length, kv_heads, per_group, HD).transpose(1, 0, 2, 3),
        keys_in.reshape(length, kv_heads, HD).transpose(1, 0, 2),
        values_in.reshape(length, kv_heads, HD).transpose(1, 0, 2),
        grads_in.reshape(length, kv_heads, per_group, HD).transpose(1, 0, 2, 3),
    )

    def one_group(pieces):
        return attend_group(pieces, allowed)

    attention, query_grad, key_grad, value_grad = lax.map(one_group, stacked)
    return (
        attention.transpose(1, 0, 2, 3).reshape(length, -1),
        query_grad.transpose(1, 0, 2, 3).reshape(length, -1),
        key_grad.transpose(1, 0, 2).reshape(length, -1),
        value_grad.transpose(1, 0, 2).reshape(length, -1),
    )


def slot_index(starts, counts, slot_rows):
    within = jnp.arange(slot_rows, dtype=jnp.int32)
    is_valid = within[None, :] < counts[:, None]
    row_index = jnp.where(is_valid, starts[:, None] + within[None, :], 0)
    return (row_index, is_valid)


def to_slots(source, row_index, is_valid):
    peer_count, slot_rows = row_index.shape
    gathered_rows = jnp.take(source, row_index.reshape(-1), axis=0).reshape(
        peer_count, slot_rows, source.shape[1]
    )
    return jnp.where(is_valid[:, :, None], gathered_rows, jnp.zeros_like(gathered_rows))


def unpack(received, landing, counts, region):
    peer_count = received[0].shape[0]
    slot_rows = received[0].shape[1]
    position = jnp.arange(region, dtype=jnp.int32)[:, None]
    senders = jnp.arange(peer_count, dtype=jnp.int32)[None, :]
    inside = (position >= landing[None, :]) & (position < (landing + counts)[None, :])
    source_row = jnp.sum(
        jnp.where(inside, senders * slot_rows + position - landing[None, :], 0), axis=1
    ).astype(jnp.int32)
    filled = jnp.any(inside, axis=1)
    documents = jnp.where(filled, jnp.sum(jnp.where(inside, senders, 0), axis=1), -1)
    arrays = []
    for member in received:
        flattened = member.reshape(peer_count * slot_rows, member.shape[2])
        gathered_rows = jnp.take(flattened, source_row, axis=0)
        arrays.append(jnp.where(filled[:, None], gathered_rows, jnp.zeros_like(gathered_rows)))
    return (tuple(arrays), documents)


def per_device(
    query_rows,
    key_rows,
    value_rows,
    output_grad,
    home_lengths,
    moved_lengths,
    moved_offsets,
    moved_owner,
    owner_offsets,
    layer_grad,
):
    peer_count = lax.axis_size("dp")
    home_ends = jnp.cumsum(home_lengths[0])
    home_position = jnp.arange(HOME, dtype=jnp.int32)
    home_docs = jnp.sum((home_position[:, None] >= home_ends[None, :]).astype(jnp.int32), axis=1)
    home = attend(
        query_rows[:HOME], key_rows[:HOME], value_rows[:HOME], output_grad[:HOME], home_docs
    )
    lengths = moved_lengths[0]
    offsets = moved_offsets[0]
    peer_ids = jnp.arange(peer_count, dtype=jnp.int32)
    matches = (moved_owner[0][None, :] == peer_ids[:, None]).astype(jnp.int32)
    starts = jnp.sum(matches * offsets[None, :], axis=1)
    counts = jnp.sum(matches * lengths[None, :], axis=1)
    landing = jnp.sum(matches * owner_offsets[0][None, :], axis=1)
    details = jnp.stack([landing, counts], axis=1)
    row_index, is_valid = slot_index(HOME + starts, counts, S)
    sent = tuple(
        (
            to_slots(source, row_index, is_valid)
            for source in (query_rows, key_rows, value_rows, output_grad)
        )
    )
    received = (
        lax.all_to_all(sent[0], "dp", split_axis=0, concat_axis=0, tiled=True),
        lax.all_to_all(sent[1], "dp", split_axis=0, concat_axis=0, tiled=True),
        lax.all_to_all(sent[2], "dp", split_axis=0, concat_axis=0, tiled=True),
        lax.all_to_all(sent[3], "dp", split_axis=0, concat_axis=0, tiled=True),
        lax.all_to_all(details, "dp", split_axis=0, concat_axis=0, tiled=True),
    )
    inputs, documents = unpack(received[:4], received[4][:, 0], received[4][:, 1], MOVE)
    moved = attend(inputs[0], inputs[1], inputs[2], inputs[3], documents)
    attention = jnp.concatenate([home[0], moved[0]], axis=0)
    query_grad = jnp.concatenate([home[1], moved[1]], axis=0)
    key_grad = jnp.concatenate([home[2], moved[2]], axis=0)
    value_grad = jnp.concatenate([home[3], moved[3]], axis=0)
    grad_term = layer_grad[0, 0].astype(jnp.float32)
    grad_share = lax.psum_scatter(
        grad_term.astype(jnp.bfloat16), "zero", scatter_dimension=0, tiled=True
    ).astype(jnp.float32)
    summed_grad = lax.psum(grad_share, "dp")
    return (attention, query_grad, key_grad, value_grad, summed_grad)


def solution(mesh):
    return jax.shard_map(
        per_device,
        mesh=mesh,
        in_specs=(
            P(("dp", "zero"), None),
            P(("dp", "zero"), None),
            P(("dp", "zero"), None),
            P(("dp", "zero"), None),
            P(("dp", "zero"), None),
            P(("dp", "zero"), None),
            P(("dp", "zero"), None),
            P(("dp", "zero"), None),
            P(("dp", "zero"), None),
            P("dp", "zero", None, None),
        ),
        out_specs=(
            P(("dp", "zero"), None),
            P(("dp", "zero"), None),
            P(("dp", "zero"), None),
            P(("dp", "zero"), None),
            P("zero", None),
        ),
        check_vma=False,
    )
```

profile of v0, /device:TPU:1, one launch (start us, length us, event | category | flops | bytes accessed | tf_op | source)
XLA Modules:
  0.0 438.1 jit_solution(514064132955999020)
XLA Ops:
  8.7 7.8 %all-to-all-start = ((s32[16,1,2]{2,1,0:T(1,128)}), s32[16,1,2]{2,1,0:T(1,128)S(1)}, u32[]{:S(2)}, u32[]{:S(2)}) async-start(s32[16,1,2]{2,1,0:T(1,128)} %copy.108), calls=%async_computation | async-start | bytes 16384 | tf_op jit(solution)/shard_map/all_to_all | solution.py:148
  16.7 5.4 %gather_fusion.2 = bf16[1024,512]{1,0:T(8,128)(2,1)S(1)} fusion(bf16[896,512]{1,0:T(8,128)(2,1)} %param.23, s32[1024]{0:T(1024)S(1)} %fusion.106), kind=kCustom, calls=%fused_computation.6.clone | custom fusion | bytes 2101248 | tf_op jit(solution)/shard_map/jit(_take)/gather | solution.py:84
  22.1 4.0 gather_fusion
  27.9 5.7 %all-to-all-start.2 = ((bf16[16,64,512]{2,1,0:T(8,128)(2,1)}), bf16[16,64,512]{2,1,0:T(8,128)(2,1)S(1)}, u32[]{:S(2)}, u32[]{:S(2)}) async-start(bf16[16,64,512]{2,1,0:T(8,128)(2,1)} %get-tuple-element.258), calls=%async_computation.2 | async-start | bytes 2097152 | tf_op jit(solution)/shard_map/all_to_all | solution.py:145
  33.7 11.4 %gather_fusion.4 = bf16[1024,2048]{1,0:T(8,128)(2,1)} fusion(bf16[896,2048]{1,0:T(8,128)(2,1)} %param.22, s32[1024]{0:T(1024)S(1)} %fusion.106), kind=kCustom, calls=%fused_computation.clone | custom fusion | bytes 8392704 | tf_op jit(solution)/shard_map/jit(_take)/gather | solution.py:84
  45.0 11.3 %gather_fusion.6 = bf16[1024,2048]{1,0:T(8,128)(2,1)} fusion(bf16[896,2048]{1,0:T(8,128)(2,1)} %param.25, s32[1024]{0:T(1024)S(1)} %fusion.106), kind=kCustom, calls=%fused_computation.4.clone | custom fusion | bytes 8392704 | tf_op jit(solution)/shard_map/jit(_take)/gather | solution.py:84
  56.4 5.7 %all-to-all-start.1 = ((bf16[16,64,512]{2,1,0:T(8,128)(2,1)}), bf16[16,64,512]{2,1,0:T(8,128)(2,1)S(1)}, u32[]{:S(2)}, u32[]{:S(2)}) async-start(bf16[16,64,512]{2,1,0:T(8,128)(2,1)} %get-tuple-element.259), calls=%async_computation.1 | async-start | bytes 2097152 | tf_op jit(solution)/shard_map/all_to_all | solution.py:146
  62.1 4.1 broadcast_select_fusion
  66.2 3.6 broadcast_select_fusion.2
  69.8 8.1 %all-to-all-done.1 = bf16[16,64,512]{2,1,0:T(8,128)(2,1)S(1)} async-done(((bf16[16,64,512]{2,1,0:T(8,128)(2,1)}), bf16[16,64,512]{2,1,0:T(8,128)(2,1)S(1)}, u32[]{:S(2)}, u32[]{:S(2)}) %all-to-all-start.1) | async-done | bytes 1048608 | tf_op jit(solution)/shard_map/all_to_all | solution.py:146
  78.9 5.1 %all-to-all-start.3 = ((bf16[16,64,2048]{2,1,0:T(8,128)(2,1)}), bf16[16,64,2048]{2,1,0:T(8,128)(2,1)}, u32[]{:S(2)}, u32[]{:S(2)}) async-start(bf16[16,64,2048]{2,1,0:T(8,128)(2,1)} %get-tuple-element.257), calls=%async_computation.3 | async-start | bytes 8388608 | tf_op jit(solution)/shard_map/all_to_all | solution.py:144
  91.5 59.1 %all-to-all-done.3 = bf16[16,64,2048]{2,1,0:T(8,128)(2,1)} async-done(((bf16[16,64,2048]{2,1,0:T(8,128)(2,1)}), bf16[16,64,2048]{2,1,0:T(8,128)(2,1)}, u32[]{:S(2)}, u32[]{:S(2)}) %all-to-all-start.3) | async-done | bytes 4194336 | tf_op jit(solution)/shard_map/all_to_all | solution.py:144
  150.6 9.9 %all-to-all-start.4 = ((bf16[16,64,2048]{2,1,0:T(8,128)(2,1)}), bf16[16,64,2048]{2,1,0:T(8,128)(2,1)}, u32[]{:S(2)}, u32[]{:S(2)}) async-start(bf16[16,64,2048]{2,1,0:T(8,128)(2,1)} %get-tuple-element.256), calls=%async_computation.4 | async-start | bytes 8388608 | tf_op jit(solution)/shard_map/all_to_all | solution.py:147
  160.5 60.1 %while.34 = (s32[]{:T(128)}, bf16[4,384,4,128]{1,3,2,0:T(8,128)(2,1)}, bf16[4,384,4,128]{1,3,2,0:T(8,128)(2,1)}, bf16[4,384,128]{2,1,0:T(8,128)(2,1)}, bf16[4,38...) while((s32[]{:T(128)}, ...), condition=%wide.region_5.6_spmd.clone, body=%wide.region_2.5_spmd.clone.sunk | while | flops 913832832 | bytes 34346664 | solution.py:66
  220.7 2.8 copy.141
  231.9 7.1 %gather_fusion.5 = bf16[512,2048]{1,0:T(8,128)(2,1)S(1)} fusion(bf16[1024,2048]{1,0:T(8,128)(2,1)} %bitcast.34, s32[1024]{0:T(1024)S(1)} %pad_clamp_fusion), kind=kCustom, calls=%fused_computation.1.clone | custom fusion | bytes 4196352 | tf_op jit(solution)/shard_map/jit(_take)/gather | solution.py:104
  239.0 8.0 %gather_fusion.7 = bf16[512,2048]{1,0:T(8,128)(2,1)} fusion(bf16[1024,2048]{1,0:T(8,128)(2,1)} %bitcast.37, s32[1024]{0:T(1024)S(1)} %pad_clamp_fusion), kind=kCustom, calls=%fused_computation.5.clone | custom fusion | bytes 4196352 | tf_op jit(solution)/shard_map/jit(_take)/gather | solution.py:104
  247.0 3.7 select_select_fusion
  250.7 4.6 %reshape.215 = bf16[512,4,4,128]{3,2,1,0:T(4,128)(2,1)} reshape(bf16[512,2048]{1,0:T(8,128)(2,1)} %get-tuple-element.261) | data formatting | bytes 4194304 | tf_op jit(solution)/shard_map/reshape | solution.py:57
  255.3 2.7 reshape.218
  258.0 5.3 %copy_bitcast_fusion = (bf16[4,512,4,128]{3,1,2,0:T(8,128)(2,1)}, bf16[4,512,4,128]{3,1,2,0:T(8,128)(2,1)}) fusion(bf16[512,4,4,128]{3,2,1,0:T(4,128)(2,1)} %reshape.218, bf16[512,4,4,128]{3,2,1,0:T(4,128)(2,1)} %reshape.215), kind=kLoop, calls=%fused_computation.129 | loop fusion | bytes 8388608 | tf_op jit(solution)/shard_map/transpose | solution.py:60
  263.3 88.2 %while.35 = (s32[]{:T(128)}, bf16[4,512,4,128]{1,3,2,0:T(8,128)(2,1)}, bf16[4,512,4,128]{1,3,2,0:T(8,128)(2,1)}, bf16[4,512,128]{2,1,0:T(8,128)(2,1)}, bf16[4,51...) while((s32[]{:T(128)}, ...), condition=%wide.region_15.20_spmd.clone, body=%wide.region_12.19_spmd.clone.sunk | while | flops 1626012160 | bytes 68993272 | solution.py:66
  276.0 3.2 fusion.195
  282.9 2.5 fusion.198
  298.0 3.2 fusion.195
  320.1 3.2 fusion.195
  327.0 2.5 fusion.198
  342.2 3.2 fusion.195
  349.0 2.5 fusion.198
  351.5 3.9 copy.143
  355.4 3.0 copy.145
  367.3 64.0 %all-reduce.1 = f32[512,512]{1,0:T(8,128)} all-reduce(bf16[512,512]{1,0:T(8,128)(2,1)} %reduce-scatter.2.cloned.1.call-done), channel_id=1, replica_groups=mesh['dp'=16,'zero'=8] {'dp'}, use_global_device_ids=true, to_apply=%region_17.22 | all-reduce | flops 262144 | bytes 1572864 | tf_op jit(solution)/shard_map/psum | solution.py:160
  (242 shorter events, 156.7 us)
Async XLA Ops:
  8.7 19.3 %all-to-all-start = ((s32[16,1,2]{2,1,0:T(1,128)}), s32[16,1,2]{2,1,0:T(1,128)S(1)}, u32[]{:S(2)}, u32[]{:S(2)}) async-start(s32[16,1,2]{2,1,0:T(1,128)} %copy.108), calls=%async_computation | async-start | bytes 16384 | tf_op jit(solution)/shard_map/all_to_all | solution.py:148
  16.7 5.4 %copy-start.1 = (bf16[896,512]{1,0:T(8,128)(2,1)S(1)}, bf16[896,512]{1,0:T(8,128)(2,1)}, u32[]{:S(2)}) copy-start(bf16[896,512]{1,0:T(8,128)(2,1)} %param.24) | copy-start | bytes 2752516
  27.9 17.1 %copy-start.19 = (s32[16,1,2]{2,1,0:T(1,128)}, s32[16,1,2]{2,1,0:T(1,128)S(1)}, u32[]{:S(2)}) copy-start(s32[16,1,2]{2,1,0:T(1,128)S(1)} %all-to-all-done) | copy-start | bytes 388
  27.9 28.4 %all-to-all-start.2 = ((bf16[16,64,512]{2,1,0:T(8,128)(2,1)}), bf16[16,64,512]{2,1,0:T(8,128)(2,1)S(1)}, u32[]{:S(2)}, u32[]{:S(2)}) async-start(bf16[16,64,512]{2,1,0:T(8,128)(2,1)} %get-tuple-element.258), calls=%async_computation.2 | async-start | bytes 2097152 | tf_op jit(solution)/shard_map/all_to_all | solution.py:145
  56.4 9.8 %copy-start.4 = (bf16[16,64,512]{2,1,0:T(8,128)(2,1)}, bf16[16,64,512]{2,1,0:T(8,128)(2,1)S(1)}, u32[]{:S(2)}) copy-start(bf16[16,64,512]{2,1,0:T(8,128)(2,1)S(1)} %all-to-all-done.2) | copy-start | bytes 3145732
  56.4 21.6 %all-to-all-start.1 = ((bf16[16,64,512]{2,1,0:T(8,128)(2,1)}), bf16[16,64,512]{2,1,0:T(8,128)(2,1)S(1)}, u32[]{:S(2)}, u32[]{:S(2)}) async-start(bf16[16,64,512]{2,1,0:T(8,128)(2,1)} %get-tuple-element.259), calls=%async_computation.1 | async-start | bytes 2097152 | tf_op jit(solution)/shard_map/all_to_all | solution.py:146
  78.9 71.7 %all-to-all-start.3 = ((bf16[16,64,2048]{2,1,0:T(8,128)(2,1)}), bf16[16,64,2048]{2,1,0:T(8,128)(2,1)}, u32[]{:S(2)}, u32[]{:S(2)}) async-start(bf16[16,64,2048]{2,1,0:T(8,128)(2,1)} %get-tuple-element.257), calls=%async_computation.3 | async-start | bytes 8388608 | tf_op jit(solution)/shard_map/all_to_all | solution.py:144
  84.1 283.2 %reduce-scatter.2.cloned.1.call-start = ((), (), s32[]{:S(2)}) async-start(), calls=%async_computation.6 | async-start | bytes 4718592 | tf_op jit(solution)/shard_map/reduce_scatter | solution.py:157
  84.8 3.0 slice-start.1
  87.8 2.5 slice-start.3
  87.8 3.4 copy-start.21
  150.6 88.4 %all-to-all-start.4 = ((bf16[16,64,2048]{2,1,0:T(8,128)(2,1)}), bf16[16,64,2048]{2,1,0:T(8,128)(2,1)}, u32[]{:S(2)}, u32[]{:S(2)}) async-start(bf16[16,64,2048]{2,1,0:T(8,128)(2,1)} %get-tuple-element.256), calls=%async_computation.4 | async-start | bytes 8388608 | tf_op jit(solution)/shard_map/all_to_all | solution.py:147
  162.7 2.5 copy-start.2
  177.7 2.5 copy-start.2
  192.7 2.5 copy-start.2
  207.8 2.5 copy-start.2
  220.7 2.8 copy-start.16
  223.5 3.6 copy-start.20
  223.5 3.9 copy-start.5
  250.7 4.6 %copy-start.9 = (bf16[512,2048]{1,0:T(8,128)(2,1)S(1)}, bf16[512,2048]{1,0:T(8,128)(2,1)}, u32[]{:S(2)}) copy-start(bf16[512,2048]{1,0:T(8,128)(2,1)} %get-tuple-element.260) | copy-start | bytes 6291460
  263.3 6.4 %copy-start.14 = (bf16[4,512,128]{1,2,0:T(8,128)(2,1)}, bf16[4,512,128]{1,2,0:T(8,128)(2,1)S(1)}, u32[]{:S(2)}) copy-start(bf16[4,512,128]{1,2,0:T(8,128)(2,1)S(1)} %get-tuple-element.435) | copy-start | bytes 1572868 | tf_op jit(solution)/shard_map/while
  276.0 3.2 copy-start.11
  285.3 6.4 %copy-start.14 = (bf16[4,512,128]{1,2,0:T(8,128)(2,1)}, bf16[4,512,128]{1,2,0:T(8,128)(2,1)S(1)}, u32[]{:S(2)}) copy-start(bf16[4,512,128]{1,2,0:T(8,128)(2,1)S(1)} %get-tuple-element.435) | copy-start | bytes 1572868 | tf_op jit(solution)/shard_map/while
  298.0 3.2 copy-start.11
  307.4 6.4 %copy-start.14 = (bf16[4,512,128]{1,2,0:T(8,128)(2,1)}, bf16[4,512,128]{1,2,0:T(8,128)(2,1)S(1)}, u32[]{:S(2)}) copy-start(bf16[4,512,128]{1,2,0:T(8,128)(2,1)S(1)} %get-tuple-element.435) | copy-start | bytes 1572868 | tf_op jit(solution)/shard_map/while
  320.1 3.2 copy-start.11
  327.0 2.5 copy-start.15
  329.4 6.4 %copy-start.14 = (bf16[4,512,128]{1,2,0:T(8,128)(2,1)}, bf16[4,512,128]{1,2,0:T(8,128)(2,1)S(1)}, u32[]{:S(2)}) copy-start(bf16[4,512,128]{1,2,0:T(8,128)(2,1)S(1)} %get-tuple-element.435) | copy-start | bytes 1572868 | tf_op jit(solution)/shard_map/while
  342.1 3.2 copy-start.11
  355.4 4.1 copy-start.17
  359.5 3.5 copy-start.8
  359.5 3.5 copy-start.13
  (21 other events, 40.1 us)
Sparse Core Ops, SparseCore 0:
  88.8 111.3 reduce-scatter.1
where the time goes:
time: 444 us; the launch traced here: 438 us
  local copies, waits for them, and re-layouts  106 us (24%)
  matrix products  103 us (23%)
  waiting for transfers between devices  68 us (15%)
  blocking collectives  64 us (14%)
  other arithmetic  48.1 us (11%)
  starting transfers between devices  34.4 us (8%)
  between operations  14.3 us (3%)
    psum x1, blocking collectives, per_device(): summed_grad = lax.psum(grad_share, 'dp')  64 us
    all_to_all x1, waiting for transfers between devices, per_device(): lax.all_to_all(sent[0], 'dp', split_axis=0, concat_axis=0, tiled=True)  59.1 us
    gather x4, local copies, waits for them, and re-layouts, to_slots(): jnp.take(source, row_index.reshape(-1), axis=0)  32 us
    dot_general x8, matrix products, attend_group(): jnp.einsum('epf,zf->pez', gradient_portion, value_portion, preferred_elem...  22.2 us
    gather x4, local copies, waits for them, and re-layouts, unpack(): gathered_rows = jnp.take(flattened, source_row, axis=0)  19.1 us
    dot_general x8, matrix products, attend_group(): jnp.einsum('nom,onu->mu', weight_brain_float, gradient_portion, preferred...  18.2 us
    dot_general x8, matrix products, attend_group(): jnp.einsum('nom,onu->mu', score_gradient, query_matrix, preferred_element...  18 us
    dot_general x8, matrix products, attend_group(): jnp.einsum('wql,lo->qwo', weight_brain_float, value_portion, preferred_el...  14.8 us
  transfers between devices with their start and end apart: 6, of which 2 were waited for; matrix products, arithmetic and copies ran while one was open for 57% of the time, Pallas kernels for 0%

commit v1 on v0

v1 whole, which is shorter than its diff:
```python
import functools
import math

import jax
import jax.numpy as jnp
from jax import lax
from jax.experimental import pallas as pl
from jax.experimental.pallas import tpu as pltpu
from jax.sharding import Mesh
from jax.sharding import PartitionSpec as P

HD = 128
HOME = 384
S = 64
MOVE = 512
NDOC = 8
GROUP = 4
KV = 4
WIN = 80
NSLOT = 16
KVROWS = 6 * S
META = 8
SCALE = 1.0 / math.sqrt(HD)
EXP2_SCALE = SCALE * math.log2(math.e)
FINE = ("ylo", "z", "core", "yhi", "x")
DP = ("ylo", "z", "core")
BF = jnp.bfloat16
F32 = jnp.float32


def dot(a, b, dims):
    return lax.dot_general(a, b, (dims, ((), ())), preferred_element_type=F32)


NN = ((1,), (0,))
NT = ((1,), (1,))
TN = ((0,), (0,))


def heads_to_rows(x):
    return jnp.concatenate([x[:, HD * h : HD * (h + 1)] for h in range(GROUP)], axis=0)


def transposed_softmax(scores, allowed):
    scores = jnp.where(allowed, scores * EXP2_SCALE, -1e30)
    highest = jnp.max(scores, axis=0, keepdims=True)
    exponent = jnp.where(allowed, jnp.exp2(scores - highest), 0.0)
    total = jnp.sum(exponent, axis=0, keepdims=True)
    return exponent * (1.0 / jnp.maximum(total, 1e-30))


def send_kernel(kvs, with_meta, table, q_hbm, k_hbm, v_hbm, g_hbm, out_hbm, q, k, v, g, slot, meta, in_sem, out_sem, meta_sem):
    c0, nc = kvs[0], len(kvs)
    wide, narrow = pl.ds(GROUP * HD * c0, GROUP * HD * nc), pl.ds(HD * c0, HD * nc)
    rows = pl.ds(HOME, MOVE)
    loads = [
        pltpu.make_async_copy(k_hbm.at[rows, narrow], k, in_sem.at[0]),
        pltpu.make_async_copy(v_hbm.at[rows, narrow], v, in_sem.at[1]),
        pltpu.make_async_copy(q_hbm.at[rows, wide], q, in_sem.at[2]),
        pltpu.make_async_copy(g_hbm.at[rows, wide], g, in_sem.at[3]),
    ]
    for load in loads:
        load.start()
    if with_meta:
        lane = lax.broadcasted_iota(jnp.int32, (META, HD), 1)
        for s in range(NSLOT):
            code = jnp.int32(0)
            for d in range(NDOC):
                code = code + jnp.where(table[2, d] == s, table[3, d] + 1, 0)
            high = lax.shift_right_logical(code, 5)
            meta[s] = jnp.where(lane < S, high, code & 31).astype(F32).astype(BF)
        meta_copy = pltpu.make_async_copy(meta, out_hbm.at[:, pl.ds(KVROWS * nc, META), :], meta_sem)
        meta_copy.start()
    for load in loads:
        load.wait()

    def store(d):
        return pltpu.make_async_copy(slot.at[d % 2], out_hbm.at[table[2, d], pl.ds(0, KVROWS * nc), :], out_sem.at[d % 2])

    for d in range(NDOC):
        length, offset, landing = table[0, d], table[1, d], table[3, d]
        start = pl.multiple_of(jnp.minimum(lax.shift_right_logical(offset, 4) * 16, MOVE - WIN), 16)
        place = lax.broadcasted_iota(jnp.int32, (S, WIN), 0)
        inside = (place - landing) & (S - 1)
        source = lax.broadcasted_iota(jnp.int32, (S, WIN), 1)
        pick = jnp.where((source - (offset - start) == inside) & (inside < length), 1.0, 0.0).astype(BF)
        key_place = (lax.broadcasted_iota(jnp.int32, (S, GROUP * S), 0) - landing) & (S - 1)
        query_place = (lax.broadcasted_iota(jnp.int32, (S, GROUP * S), 1) - landing) & (S - 1)
        causal = key_place <= query_place
        allowed = causal & (query_place < length)
        window = pl.ds(start, WIN)
        all_k = dot(pick, k[window, :], NN).astype(BF)
        all_v = dot(pick, v[window, :], NN).astype(BF)
        if d >= 2:
            store(d - 2).wait()
        here = slot.at[d % 2]
        for n in range(nc):
            kd = all_k[:, HD * n : HD * (n + 1)]
            vd = all_v[:, HD * n : HD * (n + 1)]
            cols = slice(GROUP * HD * n, GROUP * HD * (n + 1))
            qs = heads_to_rows(dot(pick, q[window, cols], NN).astype(BF))
            gs = heads_to_rows(dot(pick, g[window, cols], NN).astype(BF))
            weights = transposed_softmax(dot(kd, qs, NT), allowed)
            logits = dot(vd, gs, NT)
            delta = jnp.sum(weights * logits, axis=0, keepdims=True)
            grad = (weights * (logits - delta)).astype(BF)
            weights = weights.astype(BF)
            dv = dot(weights, gs, NN).astype(BF)
            dk = (dot(grad, qs, NN) * SCALE).astype(BF)
            grad32 = grad.astype(F32)
            turned = jnp.concatenate([grad32[:, S * h : S * (h + 1)].T for h in range(GROUP)], axis=1)
            square = jnp.where(causal, weights.astype(F32), turned).astype(BF)
            base = KVROWS * n
            here[base : base + S, :] = square[:, :HD]
            here[base + S : base + 2 * S, :] = square[:, HD:]
            here[base + 2 * S : base + 3 * S, :] = kd
            here[base + 3 * S : base + 4 * S, :] = vd
            here[base + 4 * S : base + 5 * S, :] = dk
            here[base + 5 * S : base + 6 * S, :] = dv
        store(d).start()
    store(NDOC - 2).wait()
    store(NDOC - 1).wait()
    if with_meta:
        meta_copy.wait()


def send(table, q, k, v, g, kvs, with_meta):
    nc = len(kvs)
    height = KVROWS * nc + (META if with_meta else 0)
    any_spec = pl.BlockSpec(memory_space=pl.ANY)
    return pl.pallas_call(
        functools.partial(send_kernel, kvs, with_meta),
        out_shape=jax.ShapeDtypeStruct((NSLOT, height, HD), BF),
        in_specs=[pl.BlockSpec(memory_space=pltpu.SMEM)] + [any_spec] * 4,
        out_specs=any_spec,
        scratch_shapes=[
            pltpu.VMEM((MOVE, GROUP * HD * nc), BF),
            pltpu.VMEM((MOVE, HD * nc), BF),
            pltpu.VMEM((MOVE, HD * nc), BF),
            pltpu.VMEM((MOVE, GROUP * HD * nc), BF),
            pltpu.VMEM((2, KVROWS * nc, HD), BF),
            pltpu.VMEM((NSLOT, META, HD), BF),
            pltpu.SemaphoreType.DMA((4,)),
            pltpu.SemaphoreType.DMA((2,)),
            pltpu.SemaphoreType.DMA,
        ],
        compiler_params=pltpu.CompilerParams(vmem_limit_bytes=40 << 20),
        cost_estimate=pl.CostEstimate(flops=4_000_000_000 * nc // 4, bytes_accessed=10_000_000 * nc // 4, transcendentals=1_000_000),
        name="send",
    )(table, q, k, v, g)


def home_kernel(lengths, q, k, v, g, out, dq, dk, dv, acc_k, acc_v):
    block = 128
    ends = []
    total = jnp.int32(0)
    for i in range(6):
        total = total + lengths[0, i]
        ends.append(total)
    acc_k[...] = jnp.zeros_like(acc_k)
    acc_v[...] = jnp.zeros_like(acc_v)
    for b in range(3):
        low = max(0, block * (b - 1))
        span = block * (b + 1) - low
        rows = slice(block * b, block * (b + 1))
        keys = slice(low, low + span)
        position = block * b + (lax.broadcasted_iota(jnp.int32, (1, GROUP * block), 1) & (block - 1))
        start = jnp.zeros_like(position)
        for end in ends:
            start = jnp.where(position >= end, end, start)
        key_position = low + lax.broadcasted_iota(jnp.int32, (span, GROUP * block), 0)
        allowed = (key_position <= position) & (key_position >= start)
        qs, gs = heads_to_rows(q[rows, :]), heads_to_rows(g[rows, :])
        kb, vb = k[keys, :], v[keys, :]
        weights = transposed_softmax(dot(kb, qs, NT), allowed)
        logits = dot(vb, gs, NT)
        delta = jnp.sum(weights * logits, axis=0, keepdims=True)
        grad = (weights * (logits - delta)).astype(BF)
        weights = weights.astype(BF)
        acc_v[keys, :] += dot(weights, gs, NN)
        acc_k[keys, :] += dot(grad, qs, NN)
        turned_out = dot(vb, weights, TN)
        turned_dq = dot(kb, grad, TN) * SCALE
        for h in range(GROUP):
            lanes = slice(block * h, block * (h + 1))
            out[rows, HD * h : HD * (h + 1)] = turned_out[:, lanes].T.astype(BF)
            dq[rows, HD * h : HD * (h + 1)] = turned_dq[:, lanes].T.astype(BF)
    dk[...] = (acc_k[...] * SCALE).astype(BF)
    dv[...] = acc_v[...].astype(BF)


def home(lengths, q, k, v, g):
    total = q.shape[0]
    wide = pl.BlockSpec((HOME, GROUP * HD), lambda c: (0, c))
    narrow = pl.BlockSpec((HOME, HD), lambda c: (0, c))
    return pl.pallas_call(
        home_kernel,
        out_shape=[
            jax.ShapeDtypeStruct((total, KV * GROUP * HD), BF),
            jax.ShapeDtypeStruct((total, KV * GROUP * HD), BF),
            jax.ShapeDtypeStruct((total, KV * HD), BF),
            jax.ShapeDtypeStruct((total, KV * HD), BF),
        ],
        grid=(KV,),
        in_specs=[pl.BlockSpec(memory_space=pltpu.SMEM), wide, narrow, narrow, wide],
        out_specs=[wide, wide, narrow, narrow],
        scratch_shapes=[pltpu.VMEM((HOME, HD), F32), pltpu.VMEM((HOME, HD), F32)],
        compiler_params=pltpu.CompilerParams(vmem_limit_bytes=40 << 20),
        cost_estimate=pl.CostEstimate(flops=10_000_000_000, bytes_accessed=10_000_000, transcendentals=2_000_000),
        name="home",
    )(lengths, q, k, v, g)


def receive_kernel(kvs, sources, landings, recv, out_in, dq_in, dk_in, dv_in, out, dq, dk, dv, slot, o_buf, q_buf, k_buf, v_buf, in_sem, out_sem):
    nc = len(kvs)

    def load(d):
        return pltpu.make_async_copy(recv.at[sources[d], pl.ds(0, KVROWS * nc), :], slot.at[d], in_sem.at[d])

    for d in range(NDOC):
        load(d).start()
    o_buf[...] = jnp.zeros_like(o_buf)
    q_buf[...] = jnp.zeros_like(q_buf)
    k_buf[...] = jnp.zeros_like(k_buf)
    v_buf[...] = jnp.zeros_like(v_buf)
    wide_row = lax.broadcasted_iota(jnp.int32, (GROUP * S, GROUP * HD), 0) // S
    wide_col = lax.broadcasted_iota(jnp.int32, (GROUP * S, GROUP * HD), 1) // HD
    diagonal = wide_row == wide_col
    ones = jnp.where(diagonal, 1.0, 0.0).astype(BF)
    for d in range(NDOC):
        load(d).wait()
        landing = landings[d]
        shift = landing & (S - 1)
        first = pl.multiple_of(landing - shift, S)
        key_place = (lax.broadcasted_iota(jnp.int32, (S, GROUP * S), 0) - landing) & (S - 1)
        query_place = (lax.broadcasted_iota(jnp.int32, (S, GROUP * S), 1) - landing) & (S - 1)
        causal = key_place <= query_place

        def put(buf, cols, value):
            kept = lax.broadcasted_iota(jnp.int32, value.shape, 0) >= shift
            here, after = pl.ds(first, S), pl.ds(first + S, S)
            buf[here, cols] = jnp.where(kept, value, buf[here, cols].astype(F32)).astype(BF)
            buf[after, cols] = jnp.where(kept, buf[after, cols].astype(F32), value).astype(BF)

        for n in range(nc):
            base = KVROWS * n
            square = jnp.concatenate([slot[d, base : base + S, :], slot[d, base + S : base + 2 * S, :]], axis=1).astype(F32)
            weights = jnp.where(causal, square, 0.0).astype(BF)
            grad = jnp.where(causal, 0.0, square).astype(BF)
            kd = slot[d, base + 2 * S : base + 3 * S, :]
            vd = slot[d, base + 3 * S : base + 4 * S, :]
            attended = dot(weights, vd, TN)
            attended = jnp.concatenate([attended[S * h : S * (h + 1)] for h in range(GROUP)], axis=1)
            k4 = jnp.concatenate([kd.astype(F32)] * GROUP, axis=1)
            k16 = jnp.where(diagonal, jnp.concatenate([k4] * GROUP, axis=0), 0.0).astype(BF)
            query = (dot(grad, k16, NN) - dot(grad, ones, NN) * k4) * SCALE
            wide, narrow = slice(GROUP * HD * n, GROUP * HD * (n + 1)), slice(HD * n, HD * (n + 1))
            put(o_buf, wide, attended)
            put(q_buf, wide, query)
            put(k_buf, narrow, slot[d, base + 4 * S : base + 5 * S, :].astype(F32))
            put(v_buf, narrow, slot[d, base + 5 * S : base + 6 * S, :].astype(F32))
    rows, filled = pl.ds(HOME, MOVE), pl.ds(0, MOVE)
    wide, narrow = pl.ds(GROUP * HD * kvs[0], GROUP * HD * nc), pl.ds(HD * kvs[0], HD * nc)
    stores = [
        pltpu.make_async_copy(o_buf.at[filled, :], out.at[rows, wide], out_sem.at[0]),
        pltpu.make_async_copy(q_buf.at[filled, :], dq.at[rows, wide], out_sem.at[1]),
        pltpu.make_async_copy(k_buf.at[filled, :], dk.at[rows, narrow], out_sem.at[2]),
        pltpu.make_async_copy(v_buf.at[filled, :], dv.at[rows, narrow], out_sem.at[3]),
    ]
    for copy in stores:
        copy.start()
    for copy in stores:
        copy.wait()


def receive(sources, landings, recv, outs, kvs):
    nc = len(kvs)
    any_spec = pl.BlockSpec(memory_space=pl.ANY)
    smem = pl.BlockSpec(memory_space=pltpu.SMEM)
    padded = MOVE + S
    return pl.pallas_call(
        functools.partial(receive_kernel, kvs),
        out_shape=[jax.ShapeDtypeStruct(o.shape, o.dtype) for o in outs],
        in_specs=[smem, smem] + [any_spec] * 5,
        out_specs=[any_spec] * 4,
        input_output_aliases={3: 0, 4: 1, 5: 2, 6: 3},
        scratch_shapes=[
            pltpu.VMEM((NDOC, KVROWS * nc, HD), BF),
            pltpu.VMEM((padded, GROUP * HD * nc), BF),
            pltpu.VMEM((padded, GROUP * HD * nc), BF),
            pltpu.VMEM((padded, HD * nc), BF),
            pltpu.VMEM((padded, HD * nc), BF),
            pltpu.SemaphoreType.DMA((NDOC,)),
            pltpu.SemaphoreType.DMA((4,)),
        ],
        compiler_params=pltpu.CompilerParams(vmem_limit_bytes=40 << 20),
        cost_estimate=pl.CostEstimate(flops=4_000_000_000 * nc // 4, bytes_accessed=10_000_000 * nc // 4, transcendentals=0),
        name="receive",
    )(sources, landings, recv, *outs)


def placement(codes):
    valid = codes > 0
    rank = jnp.sum((valid[None, :] & (codes[None, :] < codes[:, None])).astype(jnp.int32), axis=1)
    order = jnp.arange(NDOC, dtype=jnp.int32)
    chosen = (valid[None, :] & (rank[None, :] == order[:, None])).astype(jnp.int32)
    sources = jnp.sum(chosen * jnp.arange(NSLOT, dtype=jnp.int32)[None, :], axis=1)
    landings = jnp.sum(chosen * (codes - 1)[None, :], axis=1)
    return sources, landings


def codes_of(meta):
    pairs = meta.astype(F32).astype(jnp.int32)
    return pairs[:, 0] * 32 + pairs[:, S]


def swap(x, axis, size, mask):
    return lax.ppermute(x, axis, [(i, i ^ mask) for i in range(size)])


def add(*terms):
    total = terms[0].astype(F32)
    for term in terms[1:]:
        total = total + term.astype(F32)
    return total


def reduce_x(layer_grad):
    columns = layer_grad.shape[-1]
    grad = layer_grad.reshape(2, 4, 2, 256, columns)
    core, x = lax.axis_index("core"), lax.axis_index("x")
    mine = lax.dynamic_index_in_dim(grad, core, 2, keepdims=False)
    other = lax.dynamic_index_in_dim(grad, 1 - core, 2, keepdims=False)
    part = add(mine, swap(other, "core", 2, 1)).astype(BF)

    def block(step):
        return lax.dynamic_index_in_dim(part, (x + step) % 4, 1, keepdims=False)

    received = [lax.ppermute(block(step), "x", [(i, (i + step) % 4) for i in range(4)]) for step in (1, 2, 3)]
    return add(block(0), *received).astype(BF)


def reduce_rest(part):
    yhi = lax.axis_index("yhi")
    mine = lax.dynamic_index_in_dim(part, yhi, 0, keepdims=False)
    other = lax.dynamic_index_in_dim(part, 1 - yhi, 0, keepdims=False)
    total = add(mine, swap(other, "yhi", 2, 1))
    for axis, size, mask in (("ylo", 2, 1), ("z", 4, 1), ("z", 4, 2)):
        total = total.astype(BF)
        total = add(total, swap(total, axis, size, mask))
    total = total.astype(BF)
    twin = swap(total, "core", 2, 1)
    core = lax.axis_index("core")
    first = jnp.where(core == 0, total, twin)
    second = jnp.where(core == 0, twin, total)
    return jnp.concatenate([first, second], axis=0).astype(F32)


def exchange(slots):
    return lax.all_to_all(slots, DP, split_axis=0, concat_axis=0, tiled=True)


def per_device(q, k, v, g, home_lengths, moved_lengths, moved_offsets, moved_owner, owner_offsets, layer_grad):
    table = jnp.concatenate([moved_lengths, moved_offsets, moved_owner, owner_offsets], axis=0)
    everything = tuple(range(KV))
    part = reduce_x(layer_grad)
    received = exchange(send(table, q, k, v, g, everything, True))
    outs = home(home_lengths, q, k, v, g)
    sources, landings = placement(codes_of(received[:, KVROWS * KV, :]))
    outs = receive(sources, landings, received, outs, everything)
    part, received = lax.optimization_barrier((part, received))
    return (*outs, reduce_rest(part))


def solution(mesh):
    fine = Mesh(mesh.devices.reshape(2, 4, 2, 2, 4), FINE)
    rows = P(FINE, None)
    return jax.shard_map(
        per_device,
        mesh=fine,
        in_specs=(rows,) * 9 + (P(DP, ("yhi", "x"), None, None),),
        out_specs=(rows, rows, rows, rows, P(("yhi", "x"), None)),
        check_vma=False,
    )
```

time: 444 us -> 180 us (0.41); the launches traced: 438 us -> 179 us
  matrix products: 103 us -> 0 us
  local copies, waits for them, and re-layouts: 106 us -> 15 us
  blocking collectives: 64 us -> 0 us
  other arithmetic: 48.1 us -> 7.4 us
  Pallas kernels: 0 us -> 34.4 us
  waiting for transfers between devices: 68 us -> 91.7 us
  between operations: 14.3 us -> 0.77 us
    dot_general x44 -> x0, matrix products: 94.9 us -> none  [the longest x8 22.2 us: attend_group(): jnp.einsum('epf,zf->pez', gradient_portion, value_portion, preferred_elem...]
    psum x1 -> x0, blocking collectives: 64 us -> none  [per_device(): summed_grad = lax.psum(grad_share, 'dp')]
    gather x8 -> x0, local copies, waits for them, and re-layouts: 51.1 us -> none  [the longest x4 32 us: to_slots(): jnp.take(source, row_index.reshape(-1), axis=0)]
    ppermute x0 -> x9, waiting for transfers between devices: none -> 44.6 us  [the longest x3 25.6 us: reduce_x(): lax.ppermute(block(step), 'x', [(i, (i + step) % 4) for i in range(4)])]
    pallas_call x0 -> x3, Pallas kernels: none -> 34.4 us  [the longest x1 15.6 us: send(): pl.pallas_call(functools.partial(send_kernel, kvs, with_meta), out_shape=...]
    all_to_all x5 -> x1, starting transfers between devices: 34.3 us -> 7.88 us  [exchange(): return lax.all_to_all(slots, DP, split_axis=0, concat_axis=0, tiled=True)]
    reshape x12 -> x0, local copies, waits for them, and re-layouts: 23.5 us -> none  [the longest x2 6.72 us: attend(): attention.transpose(1, 0, 2, 3).reshape(length, -1)]
    ppermute x0 -> x9, starting transfers between devices: none -> 22.3 us  [the longest x6 18.6 us: swap(): return lax.ppermute(x, axis, [(i, i ^ mask) for i in range(size)])]
  transfers between devices with their start and end apart: 6 -> 10, of which waited for: 2 -> 7; matrix products, arithmetic and copies ran while one was open for 57% -> 5% of each run, Pallas kernels for 0% -> 10%
where the time goes in v1:
time: 180 us; the launch traced here: 179 us
  waiting for transfers between devices  91.7 us (51%)
  Pallas kernels  34.4 us (19%)
  starting transfers between devices  30.2 us (17%)
  local copies, waits for them, and re-layouts  15 us (8%)
  other arithmetic  7.4 us (4%)
    all_to_all x1, waiting for transfers between devices, exchange(): return lax.all_to_all(slots, DP, split_axis=0, concat_axis=0, tiled=True)  47 us
    ppermute x3, waiting for transfers between devices, reduce_x(): lax.ppermute(block(step), 'x', [(i, (i + step) % 4) for i in range(4)])  25.6 us
    ppermute x6, waiting for transfers between devices, swap(): return lax.ppermute(x, axis, [(i, i ^ mask) for i in range(size)])  19.1 us
    ppermute x6, starting transfers between devices, swap(): return lax.ppermute(x, axis, [(i, i ^ mask) for i in range(size)])  18.6 us
    pallas_call x1, Pallas kernels, send(): pl.pallas_call(functools.partial(send_kernel, kvs, with_meta), out_shape=...  15.6 us
    unnamed x20, local copies, waits for them, and re-layouts  11.8 us
    pallas_call x1, Pallas kernels, home(): pl.pallas_call(home_kernel, out_shape=[jax.ShapeDtypeStruct((total, KV *...  9.94 us
    pallas_call x1, Pallas kernels, receive(): pl.pallas_call(functools.partial(receive_kernel, kvs), out_shape=[jax.Sha...  8.89 us
  transfers between devices with their start and end apart: 10, of which 7 were waited for; matrix products, arithmetic and copies ran while one was open for 5% of the time, Pallas kernels for 10%

profile of v1, /device:TPU:1, one launch (start us, length us, event | category | flops | bytes accessed | tf_op | source)
XLA Modules:
  0.0 179.4 jit_solution(15836484396857411903)
XLA Ops:
  0.6 0.7 pad_add_fusion.table
  1.4 2.0 %copy-done = bf16[896,2048]{1,0:T(8,128)(2,1)S(1)} copy-done((bf16[896,2048]{1,0:T(8,128)(2,1)S(1)}, bf16[896,2048]{1,0:T(8,128)(2,1)}, u32[]{:S(2)}) %copy-start) | copy-done | bytes 3670040
  3.4 2.0 %copy-done.2 = bf16[896,2048]{1,0:T(8,128)(2,1)S(1)} copy-done((bf16[896,2048]{1,0:T(8,128)(2,1)S(1)}, bf16[896,2048]{1,0:T(8,128)(2,1)}, u32[]{:S(2)}) %copy-start.2) | copy-done | bytes 3670040
  5.4 1.2 copy-done.4
  6.6 1.2 copy-done.6
  7.8 15.6 %send.1 = bf16[16,1544,128]{2,1,0:T(8,128)(2,1)} custom-call(s32[4,8]{1,0:T(4,128)S(1)} %pad_add_fusion.table, bf16[896,2048]{1,0:T(8,128)(2,1)S(1)} %copy-done, bf16[896,512]{1,0:T(8,128)(2,1)S(1)} %copy-done.4, bf16[896,512]{1,0:T(8,128)(2,1)S(1)} %copy-done.6, bf16[896,2048]{1,0:T(8,128)(2,1)S(1)} %copy-done.2), custom_call_target="tpu_custom_call" | custom-call | flops 4000000000 | bytes 10000000 | tf_op jit(solution)/shard_map/send/pallas_call | solution.py:131
  23.4 7.9 %all-to-all-start = ((bf16[16,1544,128]{2,1,0:T(8,128)(2,1)}), bf16[16,1544,128]{2,1,0:T(8,128)(2,1)}, u32[]{:S(2)}, u32[]{:S(2)}) async-start(bf16[16,1544,128]{2,1,0:T(8,128)(2,1)} %send.1), calls=%async_computation | async-start | bytes 12648448 | tf_op jit(solution)/shard_map/all_to_all | solution.py:360
  31.2 3.0 %dynamic-slice_bitcast_fusion = bf16[2,4,256,512]{3,2,1,0:T(8,128)(2,1)} fusion(bf16[2,4,2,256,512]{4,3,2,1,0:T(8,128)(2,1)} %bitcast.21, s32[]{:T(128)S(6)} %select_n.60), kind=kLoop, calls=%fused_computation.2 | loop fusion | bytes 4194308 | tf_op jit(solution)/shard_map/jit(dynamic_index_in_dim)/squeeze | solution.py:333
  34.4 4.2 %collective-permute-done = bf16[2,4,256,512]{3,2,1,0:T(8,128)(2,1)S(1)} collective-permute-done((bf16[2,4,256,512]{3,2,1,0:T(8,128)(2,1)}, bf16[2,4,256,512]{3,2,1,0:T(8,128)(2,1)S(1)}, u32[]{:S(2)}, u32[]{:S(2)}) %collective-permute-start) | collective-permute-done | bytes 2097184 | tf_op jit(solution)/shard_map/ppermute | solution.py:318
  38.6 2.2 %fusion = bf16[2,4,256,512]{3,2,1,0:T(8,128)(2,1)S(1)} fusion(bf16[2,4,256,512]{3,2,1,0:T(8,128)(2,1)S(1)} %collective-permute-done, bf16[2,4,2,256,512]{4,3,2,1,0:T(8,128)(2,1)} %bitcast.22, s32[]{:T(128)S(6)} %select_n.59), kind=kLoop, calls=%fused_computation.1 | loop fusion | flops 4194304 | bytes 6291460 | tf_op jit(solution)/shard_map/convert_element_type | solution.py:334
  40.8 1.3 copy-done.9
  42.3 2.5 %collective-permute-start.3 = (bf16[2,256,512]{2,1,0:T(8,128)(2,1)S(1)}, bf16[2,256,512]{2,1,0:T(8,128)(2,1)}, u32[]{:S(2)}, u32[]{:S(2)}) collective-permute-start(bf16[2,256,512]{2,1,0:T(8,128)(2,1)S(1)} %get-tuple-element.26), channel_id=1, source_target_pairs={{0,3},{1,0},{2,1},{3,2},{4,7},{5,4},{6,5},{7,6},{8,11},{9,8},{10,9... | collective-permute-start | bytes 1572872 | tf_op jit(solution)/shard_map/ppermute | solution.py:339
  44.8 0.5 collective-permute-start.2
  45.3 0.6 collective-permute-start.1
  45.9 21.1 %collective-permute-done.3 = bf16[2,256,512]{2,1,0:T(8,128)(2,1)} collective-permute-done((bf16[2,256,512]{2,1,0:T(8,128)(2,1)S(1)}, bf16[2,256,512]{2,1,0:T(8,128)(2,1)}, u32[]{:S(2)}, u32[]{:S(2)}) %collective-permute-start.3) | collective-permute-done | bytes 524320 | tf_op jit(solution)/shard_map/ppermute | solution.py:339
  67.1 4.4 %collective-permute-done.1 = bf16[2,256,512]{2,1,0:T(8,128)(2,1)} collective-permute-done((bf16[2,256,512]{2,1,0:T(8,128)(2,1)S(1)}, bf16[2,256,512]{2,1,0:T(8,128)(2,1)}, u32[]{:S(2)}, u32[]{:S(2)}) %collective-permute-start.1) | collective-permute-done | bytes 524320 | tf_op jit(solution)/shard_map/ppermute | solution.py:339
  71.5 1.8 fusion.3
  73.3 47.0 %all-to-all-done.recv = bf16[16,1544,128]{2,1,0:T(8,128)(2,1)} async-done(((bf16[16,1544,128]{2,1,0:T(8,128)(2,1)}), bf16[16,1544,128]{2,1,0:T(8,128)(2,1)}, u32[]{:S(2)}, u32[]{:S(2)}) %all-to-all-start) | async-done | bytes 6324256 | tf_op jit(solution)/shard_map/all_to_all | solution.py:360
  120.4 2.7 %collective-permute-start.4 = (bf16[256,512]{1,0:T(8,128)(2,1)S(1)}, bf16[256,512]{1,0:T(8,128)(2,1)S(1)}, u32[]{:S(2)}, u32[]{:S(2)}) collective-permute-start(bf16[256,512]{1,0:T(8,128)(2,1)S(1)} %dynamic-slice_bitcast_fusion.4), channel_id=1, source_target_pairs={{0,4},{4,0},{1,5},{5,1},{2,6},{6,2},{3,7},{7,3},{8,12},{12,8},{9,1... | collective-permute-start | bytes 786440 | tf_op jit(solution)/shard_map/ppermute | solution.py:318
  123.0 5.8 %collective-permute-done.4 = bf16[256,512]{1,0:T(8,128)(2,1)S(1)} collective-permute-done((bf16[256,512]{1,0:T(8,128)(2,1)S(1)}, bf16[256,512]{1,0:T(8,128)(2,1)S(1)}, u32[]{:S(2)}, u32[]{:S(2)}) %collective-permute-start.4) | collective-permute-done | bytes 262176 | tf_op jit(solution)/shard_map/ppermute | solution.py:318
  128.9 0.3 collective-permute-start.5
  129.2 2.0 %copy-done.1 = bf16[896,2048]{1,0:T(8,128)(2,1)S(1)} copy-done((bf16[896,2048]{1,0:T(8,128)(2,1)S(1)}, bf16[896,2048]{1,0:T(8,128)(2,1)}, u32[]{:S(2)}) %copy-start.1) | copy-done | bytes 3670040
  131.3 2.0 %copy-done.3 = bf16[896,2048]{1,0:T(8,128)(2,1)S(1)} copy-done((bf16[896,2048]{1,0:T(8,128)(2,1)S(1)}, bf16[896,2048]{1,0:T(8,128)(2,1)}, u32[]{:S(2)}) %copy-start.3) | copy-done | bytes 3670040
  133.3 9.9 %home.1 = (bf16[896,2048]{1,0:T(8,128)(2,1)}, bf16[896,2048]{1,0:T(8,128)(2,1)}, bf16[896,512]{1,0:T(8,128)(2,1)}, bf16[896,512]{1,0:T(8,128)(2,1)}) custom-call(s32[1,6]{1,0:T(1,128)S(1)} %copy-done.8, bf16[896,2048]{1,0:T(8,128)(2,1)S(1)} %copy-done.1, bf16[896,512]{1,0:T(8,128)(2,1)S(1)} %copy-done.5, bf16[896,512]{1,0:T(8,128)(2,1)S(1)} %copy-done.7, ...), custom_call_target="tpu_custom_call" | custom-call | flops 10000000000 | bytes 10000000 | tf_op jit(solution)/shard_map/home/pallas_call | solution.py:196
  143.3 0.8 fusion.6
  144.1 5.7 %collective-permute-start.6 = (bf16[256,512]{1,0:T(8,128)(2,1)S(1)}, bf16[256,512]{1,0:T(8,128)(2,1)S(1)}, u32[]{:S(2)}, u32[]{:S(2)}) collective-permute-start(bf16[256,512]{1,0:T(8,128)(2,1)S(1)} %add_convert_fusion.2), channel_id=1, source_target_pairs={{0,16},{16,0},{32,48},{48,32},{1,17},{17,1},{33,49},{49,33},{2,18}... | collective-permute-start | bytes 786440 | tf_op jit(solution)/shard_map/ppermute | solution.py:318
  150.0 4.4 %collective-permute-done.6 = bf16[256,512]{1,0:T(8,128)(2,1)S(1)} collective-permute-done((bf16[256,512]{1,0:T(8,128)(2,1)S(1)}, bf16[256,512]{1,0:T(8,128)(2,1)S(1)}, u32[]{:S(2)}, u32[]{:S(2)}) %collective-permute-start.6) | collective-permute-done | bytes 262176 | tf_op jit(solution)/shard_map/ppermute | solution.py:318
  154.5 7.3 %collective-permute-start.7 = (bf16[256,512]{1,0:T(8,128)(2,1)S(1)}, bf16[256,512]{1,0:T(8,128)(2,1)S(1)}, u32[]{:S(2)}, u32[]{:S(2)}) collective-permute-start(bf16[256,512]{1,0:T(8,128)(2,1)S(1)} %add_convert_fusion.1), channel_id=1, source_target_pairs={{0,32},{16,48},{32,0},{48,16},{1,33},{17,49},{33,1},{49,17},{2,34}... | collective-permute-start | bytes 786440 | tf_op jit(solution)/shard_map/ppermute | solution.py:318
  162.1 4.6 %collective-permute-done.7 = bf16[256,512]{1,0:T(8,128)(2,1)S(1)} collective-permute-done((bf16[256,512]{1,0:T(8,128)(2,1)S(1)}, bf16[256,512]{1,0:T(8,128)(2,1)S(1)}, u32[]{:S(2)}, u32[]{:S(2)}) %collective-permute-start.7) | collective-permute-done | bytes 262176 | tf_op jit(solution)/shard_map/ppermute | solution.py:318
  166.8 2.5 %collective-permute-start.8 = (bf16[256,512]{1,0:T(8,128)(2,1)S(1)}, bf16[256,512]{1,0:T(8,128)(2,1)S(1)}, u32[]{:S(2)}, u32[]{:S(2)}) collective-permute-start(bf16[256,512]{1,0:T(8,128)(2,1)S(1)} %add_convert_fusion), channel_id=1, source_target_pairs={{0,8},{8,0},{1,9},{9,1},{2,10},{10,2},{3,11},{11,3},{4,12},{12,4},... | collective-permute-start | bytes 786440 | tf_op jit(solution)/shard_map/ppermute | solution.py:318
  169.4 8.9 %receive.1 = (bf16[896,2048]{1,0:T(8,128)(2,1)}, bf16[896,2048]{1,0:T(8,128)(2,1)}, bf16[896,512]{1,0:T(8,128)(2,1)}, bf16[896,512]{1,0:T(8,128)(2,1)}) custom-call(s32[8]{0:T(128)S(1)} %get-tuple-element.24.sources, s32[8]{0:T(128)S(1)} %get-tuple-element.23.landings, ...), custom_call_target="tpu_custom_call", output_to_operand_aliasing={{0}: (3, {}), {1}: (4, {}), {2}: (5, {}), {3}: (6, {})} | custom-call | flops 4000000000 | bytes 10000000 | tf_op jit(solution)/shard_map/receive/pallas_call | solution.py:281
  178.3 1.1 maximum_convert_fusion
  (29 shorter events, 1.2 us)
Async XLA Ops:
  1.3 2.0 %copy-start = (bf16[896,2048]{1,0:T(8,128)(2,1)S(1)}, bf16[896,2048]{1,0:T(8,128)(2,1)}, u32[]{:S(2)}) copy-start(bf16[896,2048]{1,0:T(8,128)(2,1)} %q.1) | copy-start | bytes 11010052
  3.4 2.0 %copy-start.2 = (bf16[896,2048]{1,0:T(8,128)(2,1)S(1)}, bf16[896,2048]{1,0:T(8,128)(2,1)}, u32[]{:S(2)}) copy-start(bf16[896,2048]{1,0:T(8,128)(2,1)} %g.1) | copy-start | bytes 11010052
  5.4 1.2 copy-start.4
  6.6 1.2 copy-start.6
  23.4 97.0 %all-to-all-start = ((bf16[16,1544,128]{2,1,0:T(8,128)(2,1)}), bf16[16,1544,128]{2,1,0:T(8,128)(2,1)}, u32[]{:S(2)}, u32[]{:S(2)}) async-start(bf16[16,1544,128]{2,1,0:T(8,128)(2,1)} %send.1), calls=%async_computation | async-start | bytes 12648448 | tf_op jit(solution)/shard_map/all_to_all | solution.py:360
  34.3 4.4 %collective-permute-start = (bf16[2,4,256,512]{3,2,1,0:T(8,128)(2,1)}, bf16[2,4,256,512]{3,2,1,0:T(8,128)(2,1)S(1)}, u32[]{:S(2)}, u32[]{:S(2)}) collective-permute-start(bf16[2,4,256,512]{3,2,1,0:T(8,128)(2,1)} %dynamic-slice_bitcast_fusion), channel_id=1, source_target_pairs={{0,8},{8,0},{1,9},{9,1},{2,10},{10,2},{3,11},{11,3},{4,12},{12,4},... | collective-permute-start | bytes 6291464 | tf_op jit(solution)/shard_map/ppermute | solution.py:318
  40.8 1.3 copy-start.9
  42.2 87.1 %copy-start.5 = (bf16[896,512]{1,0:T(8,128)(2,1)S(1)}, bf16[896,512]{1,0:T(8,128)(2,1)}, u32[]{:S(2)}) copy-start(bf16[896,512]{1,0:T(8,128)(2,1)} %k.1) | copy-start | bytes 2752516
  42.2 87.1 %copy-start.7 = (bf16[896,512]{1,0:T(8,128)(2,1)S(1)}, bf16[896,512]{1,0:T(8,128)(2,1)}, u32[]{:S(2)}) copy-start(bf16[896,512]{1,0:T(8,128)(2,1)} %v.1) | copy-start | bytes 2752516
  42.2 87.1 %copy-start.8 = (s32[1,6]{1,0:T(1,128)S(1)}, s32[1,6]{1,0:T(1,128)}, u32[]{:S(2)}) copy-start(s32[1,6]{1,0:T(1,128)} %lengths.1) | copy-start | bytes 76
  42.3 24.8 %collective-permute-start.3 = (bf16[2,256,512]{2,1,0:T(8,128)(2,1)S(1)}, bf16[2,256,512]{2,1,0:T(8,128)(2,1)}, u32[]{:S(2)}, u32[]{:S(2)}) collective-permute-start(bf16[2,256,512]{2,1,0:T(8,128)(2,1)S(1)} %get-tuple-element.26), channel_id=1, source_target_pairs={{0,3},{1,0},{2,1},{3,2},{4,7},{5,4},{6,5},{7,6},{8,11},{9,8},{10,9... | collective-permute-start | bytes 1572872 | tf_op jit(solution)/shard_map/ppermute | solution.py:339
  44.8 22.3 %collective-permute-start.2 = (bf16[2,256,512]{2,1,0:T(8,128)(2,1)S(1)}, bf16[2,256,512]{2,1,0:T(8,128)(2,1)}, u32[]{:S(2)}, u32[]{:S(2)}) collective-permute-start(bf16[2,256,512]{2,1,0:T(8,128)(2,1)S(1)} %get-tuple-element.27), channel_id=1, source_target_pairs={{0,2},{1,3},{2,0},{3,1},{4,6},{5,7},{6,4},{7,5},{8,10},{9,11},{10,... | collective-permute-start | bytes 1572872 | tf_op jit(solution)/shard_map/ppermute | solution.py:339
  45.3 26.2 %collective-permute-start.1 = (bf16[2,256,512]{2,1,0:T(8,128)(2,1)S(1)}, bf16[2,256,512]{2,1,0:T(8,128)(2,1)}, u32[]{:S(2)}, u32[]{:S(2)}) collective-permute-start(bf16[2,256,512]{2,1,0:T(8,128)(2,1)S(1)} %get-tuple-element.25), channel_id=1, source_target_pairs={{0,1},{1,2},{2,3},{3,0},{4,5},{5,6},{6,7},{7,4},{8,9},{9,10},{10,1... | collective-permute-start | bytes 1572872 | tf_op jit(solution)/shard_map/ppermute | solution.py:339
  120.4 8.5 %collective-permute-start.4 = (bf16[256,512]{1,0:T(8,128)(2,1)S(1)}, bf16[256,512]{1,0:T(8,128)(2,1)S(1)}, u32[]{:S(2)}, u32[]{:S(2)}) collective-permute-start(bf16[256,512]{1,0:T(8,128)(2,1)S(1)} %dynamic-slice_bitcast_fusion.4), channel_id=1, source_target_pairs={{0,4},{4,0},{1,5},{5,1},{2,6},{6,2},{3,7},{7,3},{8,12},{12,8},{9,1... | collective-permute-start | bytes 786440 | tf_op jit(solution)/shard_map/ppermute | solution.py:318
  128.9 15.1 %collective-permute-start.5 = (bf16[256,512]{1,0:T(8,128)(2,1)S(1)}, bf16[256,512]{1,0:T(8,128)(2,1)S(1)}, u32[]{:S(2)}, u32[]{:S(2)}) collective-permute-start(bf16[256,512]{1,0:T(8,128)(2,1)S(1)} %fusion.4), channel_id=1, source_target_pairs={{0,64},{64,0},{1,65},{65,1},{2,66},{66,2},{3,67},{67,3},{4,68},{68... | collective-permute-start | bytes 786440 | tf_op jit(solution)/shard_map/ppermute | solution.py:318
  129.2 2.0 %copy-start.1 = (bf16[896,2048]{1,0:T(8,128)(2,1)S(1)}, bf16[896,2048]{1,0:T(8,128)(2,1)}, u32[]{:S(2)}) copy-start(bf16[896,2048]{1,0:T(8,128)(2,1)} %q.1) | copy-start | bytes 11010052
  131.3 2.0 %copy-start.3 = (bf16[896,2048]{1,0:T(8,128)(2,1)S(1)}, bf16[896,2048]{1,0:T(8,128)(2,1)}, u32[]{:S(2)}) copy-start(bf16[896,2048]{1,0:T(8,128)(2,1)} %g.1) | copy-start | bytes 11010052
  144.1 10.4 %collective-permute-start.6 = (bf16[256,512]{1,0:T(8,128)(2,1)S(1)}, bf16[256,512]{1,0:T(8,128)(2,1)S(1)}, u32[]{:S(2)}, u32[]{:S(2)}) collective-permute-start(bf16[256,512]{1,0:T(8,128)(2,1)S(1)} %add_convert_fusion.2), channel_id=1, source_target_pairs={{0,16},{16,0},{32,48},{48,32},{1,17},{17,1},{33,49},{49,33},{2,18}... | collective-permute-start | bytes 786440 | tf_op jit(solution)/shard_map/ppermute | solution.py:318
  154.5 12.2 %collective-permute-start.7 = (bf16[256,512]{1,0:T(8,128)(2,1)S(1)}, bf16[256,512]{1,0:T(8,128)(2,1)S(1)}, u32[]{:S(2)}, u32[]{:S(2)}) collective-permute-start(bf16[256,512]{1,0:T(8,128)(2,1)S(1)} %add_convert_fusion.1), channel_id=1, source_target_pairs={{0,32},{16,48},{32,0},{48,16},{1,33},{17,49},{33,1},{49,17},{2,34}... | collective-permute-start | bytes 786440 | tf_op jit(solution)/shard_map/ppermute | solution.py:318
  166.8 11.4 %collective-permute-start.8 = (bf16[256,512]{1,0:T(8,128)(2,1)S(1)}, bf16[256,512]{1,0:T(8,128)(2,1)S(1)}, u32[]{:S(2)}, u32[]{:S(2)}) collective-permute-start(bf16[256,512]{1,0:T(8,128)(2,1)S(1)} %add_convert_fusion), channel_id=1, source_target_pairs={{0,8},{8,0},{1,9},{9,1},{2,10},{10,2},{3,11},{11,3},{4,12},{12,4},... | collective-permute-start | bytes 786440 | tf_op jit(solution)/shard_map/ppermute | solution.py:318

commit v2 on v1

v2 whole, which is shorter than its diff:
```python
import functools
import math

import jax
import jax.numpy as jnp
from jax import lax
from jax.experimental import pallas as pl
from jax.experimental.pallas import tpu as pltpu
from jax.sharding import Mesh
from jax.sharding import PartitionSpec as P

HD = 128
HOME = 384
S = 64
MOVE = 512
NDOC = 8
GROUP = 4
KV = 4
WIN = 80
NSLOT = 16
KVROWS = 6 * S
META = 8
SCALE = 1.0 / math.sqrt(HD)
EXP2_SCALE = SCALE * math.log2(math.e)
FINE = ("ylo", "z", "core", "yhi", "x")
DP = ("ylo", "z", "core")
BF = jnp.bfloat16
F32 = jnp.float32


def dot(a, b, dims):
    return lax.dot_general(a, b, (dims, ((), ())), preferred_element_type=F32)


NN = ((1,), (0,))
NT = ((1,), (1,))
TN = ((0,), (0,))


def heads_to_rows(x):
    return jnp.concatenate([x[:, HD * h : HD * (h + 1)] for h in range(GROUP)], axis=0)


def transposed_softmax(scores, allowed, filled=None):
    scores = jnp.where(allowed, scores * EXP2_SCALE, -1e30)
    highest = jnp.max(scores, axis=0, keepdims=True)
    exponent = jnp.exp2(scores - highest)
    inverse = 1.0 / jnp.sum(exponent, axis=0, keepdims=True)
    if filled is not None:
        inverse = jnp.where(filled, inverse, 0.0)
    return exponent * inverse


def send_kernel(table, q_hbm, k_hbm, v_hbm, g_hbm, *refs):
    out, q, k, v, g, slot, meta, in_sem, out_sem, meta_sem = refs
    chunk = 128
    pairs = ((q_hbm, q), (g_hbm, g), (k_hbm, k), (v_hbm, v))

    def load(a, b):
        source, target = pairs[a]
        return pltpu.make_async_copy(source.at[pl.ds(HOME + chunk * b, chunk), :], target.at[pl.ds(chunk * b, chunk), :], in_sem.at[a, b])

    for b in range(MOVE // chunk):
        for a in range(4):
            load(a, b).start()
    lane = lax.broadcasted_iota(jnp.int32, (META, HD), 1)
    for s in range(NSLOT):
        code = jnp.int32(0)
        for d in range(NDOC):
            code = code + jnp.where(table[2, d] == s, table[3, d] + 1, 0)
        meta[s] = jnp.where(lane < S, lax.shift_right_logical(code, 5), code & 31).astype(F32).astype(BF)

    meta_copy = pltpu.make_async_copy(meta, out.at[:, pl.ds(KVROWS * KV, META), :], meta_sem)
    meta_copy.start()

    def store(d):
        return pltpu.make_async_copy(slot.at[d % 2], out.at[table[2, d], pl.ds(0, KVROWS * KV), :], out_sem.at[d % 2])

    same = (lax.broadcasted_iota(jnp.int32, (HD, HD), 0) & (S - 1)) == (lax.broadcasted_iota(jnp.int32, (HD, HD), 1) & (S - 1))
    loaded = -1
    for d in range(NDOC):
        last = min((S * d + WIN - 1) // chunk, MOVE // chunk - 1)
        while loaded < last:
            loaded += 1
            for a in range(4):
                load(a, loaded).wait()
        length, offset, landing = table[0, d], table[1, d], table[3, d]
        start = pl.multiple_of(jnp.minimum(lax.shift_right_logical(offset, 4) * 16, MOVE - WIN), 16)
        inside = (lax.broadcasted_iota(jnp.int32, (S, WIN), 0) - landing) & (S - 1)
        source = lax.broadcasted_iota(jnp.int32, (S, WIN), 1)
        pick = jnp.where((source - (offset - start) == inside) & (inside < length), 1.0, 0.0).astype(BF)
        key_place = (lax.broadcasted_iota(jnp.int32, (S, 1), 0) - landing) & (S - 1)
        query_place = (lax.broadcasted_iota(jnp.int32, (1, GROUP * S), 1) - landing) & (S - 1)
        filled = query_place < length
        allowed = key_place <= jnp.where(filled, query_place, -1)
        window = pl.ds(start, WIN)
        all_k = dot(pick, k[window, :], NN).astype(BF)
        all_v = dot(pick, v[window, :], NN).astype(BF)
        if d >= 2:
            store(d - 2).wait()
        here = slot.at[d % 2]
        for n in range(KV):
            kd = all_k[:, HD * n : HD * (n + 1)]
            vd = all_v[:, HD * n : HD * (n + 1)]
            cols = slice(GROUP * HD * n, GROUP * HD * (n + 1))
            qs = heads_to_rows(dot(pick, q[window, cols], NN).astype(BF))
            gs = heads_to_rows(dot(pick, g[window, cols], NN).astype(BF))
            weights = transposed_softmax(dot(kd, qs, NT), allowed, filled)
            logits = dot(vd, gs, NT)
            delta = jnp.sum(weights * logits, axis=0, keepdims=True)
            grad = weights * (logits - delta)
            dv = dot(weights.astype(BF), gs, NN).astype(BF)
            dk = (dot(grad.astype(BF), qs, NN) * SCALE).astype(BF)
            turned = jnp.concatenate([grad[:, :HD], grad[:, HD:]], axis=0).T
            square = jnp.concatenate([weights[:, :HD], weights[:, HD:]], axis=0) + jnp.where(same, 0.0, turned)
            base = KVROWS * n
            here[base : base + 2 * S, :] = square.astype(BF)
            here[base + 2 * S : base + 3 * S, :] = kd
            here[base + 3 * S : base + 4 * S, :] = vd
            here[base + 4 * S : base + 5 * S, :] = dk
            here[base + 5 * S : base + 6 * S, :] = dv
        store(d).start()
    store(NDOC - 2).wait()
    store(NDOC - 1).wait()
    meta_copy.wait()


def send(table, q, k, v, g):
    hbm = pl.BlockSpec(memory_space=pltpu.HBM)
    return pl.pallas_call(
        send_kernel,
        out_shape=jax.ShapeDtypeStruct((NSLOT, KVROWS * KV + META, HD), BF),
        in_specs=[pl.BlockSpec(memory_space=pltpu.SMEM)] + [hbm] * 4,
        out_specs=hbm,
        scratch_shapes=[
            pltpu.VMEM((MOVE, KV * GROUP * HD), BF),
            pltpu.VMEM((MOVE, KV * HD), BF),
            pltpu.VMEM((MOVE, KV * HD), BF),
            pltpu.VMEM((MOVE, KV * GROUP * HD), BF),
            pltpu.VMEM((2, KVROWS * KV, HD), BF),
            pltpu.VMEM((NSLOT, META, HD), BF),
            pltpu.SemaphoreType.DMA((4, 4)),
            pltpu.SemaphoreType.DMA((2,)),
            pltpu.SemaphoreType.DMA,
        ],
        cost_estimate=pl.CostEstimate(flops=4_000_000_000, bytes_accessed=10_000_000, transcendentals=1_000_000),
        name="send",
    )(table, q, k, v, g)


def home_kernel(lengths, q, k, v, g, out, dq, dk, dv, acc_k, acc_v):
    block = 128
    ends = []
    total = jnp.int32(0)
    for i in range(6):
        total = total + lengths[0, i]
        ends.append(total)
    acc_k[...] = jnp.zeros_like(acc_k)
    acc_v[...] = jnp.zeros_like(acc_v)
    for b in range(3):
        low = max(0, block * (b - 1))
        span = block * (b + 1) - low
        rows = slice(block * b, block * (b + 1))
        keys = slice(low, low + span)
        position = block * b + (lax.broadcasted_iota(jnp.int32, (1, GROUP * block), 1) & (block - 1))
        start = jnp.zeros_like(position)
        for end in ends:
            start = jnp.where(position >= end, end, start)
        key_position = low + lax.broadcasted_iota(jnp.int32, (span, GROUP * block), 0)
        allowed = (key_position <= position) & (key_position >= start)
        qs, gs = heads_to_rows(q[rows, :]), heads_to_rows(g[rows, :])
        kb, vb = k[keys, :], v[keys, :]
        weights = transposed_softmax(dot(kb, qs, NT), allowed)
        logits = dot(vb, gs, NT)
        delta = jnp.sum(weights * logits, axis=0, keepdims=True)
        grad = (weights * (logits - delta)).astype(BF)
        weights = weights.astype(BF)
        acc_v[keys, :] += dot(weights, gs, NN)
        acc_k[keys, :] += dot(grad, qs, NN)
        turned_out = dot(vb, weights, TN)
        turned_dq = dot(kb, grad, TN) * SCALE
        for h in range(GROUP):
            lanes = slice(block * h, block * (h + 1))
            out[rows, HD * h : HD * (h + 1)] = turned_out[:, lanes].T.astype(BF)
            dq[rows, HD * h : HD * (h + 1)] = turned_dq[:, lanes].T.astype(BF)
    dk[...] = (acc_k[...] * SCALE).astype(BF)
    dv[...] = acc_v[...].astype(BF)


def home(lengths, q, k, v, g):
    total = q.shape[0]
    wide = pl.BlockSpec((HOME, GROUP * HD), lambda c: (0, c))
    narrow = pl.BlockSpec((HOME, HD), lambda c: (0, c))
    return pl.pallas_call(
        home_kernel,
        out_shape=[
            jax.ShapeDtypeStruct((total, KV * GROUP * HD), BF),
            jax.ShapeDtypeStruct((total, KV * GROUP * HD), BF),
            jax.ShapeDtypeStruct((total, KV * HD), BF),
            jax.ShapeDtypeStruct((total, KV * HD), BF),
        ],
        grid=(KV,),
        in_specs=[pl.BlockSpec(memory_space=pltpu.SMEM), wide, narrow, narrow, wide],
        out_specs=[wide, wide, narrow, narrow],
        scratch_shapes=[pltpu.VMEM((HOME, HD), F32), pltpu.VMEM((HOME, HD), F32)],
        cost_estimate=pl.CostEstimate(flops=10_000_000_000, bytes_accessed=10_000_000, transcendentals=2_000_000),
        name="home",
    )(lengths, q, k, v, g)


def receive_kernel(sources, landings, recv, *refs):
    out, dq, dk, dv = refs[4:8]
    slot, o_buf, q_buf, k_buf, v_buf, o_out, q_out, k_out, v_out, in_sem, out_sem = refs[8:]

    def load(d, n):
        rows = pl.ds(KVROWS * n, KVROWS)
        return pltpu.make_async_copy(recv.at[sources[d], rows, :], slot.at[d, rows, :], in_sem.at[d, n])

    for n in range(KV):
        for d in range(NDOC):
            load(d, n).start()

    def stores(n):
        rows, wide, narrow = pl.ds(HOME, MOVE), pl.ds(GROUP * HD * n, GROUP * HD), pl.ds(HD * n, HD)
        return [
            pltpu.make_async_copy(o_out.at[n % 2], out.at[rows, wide], out_sem.at[0, n % 2]),
            pltpu.make_async_copy(q_out.at[n % 2], dq.at[rows, wide], out_sem.at[1, n % 2]),
            pltpu.make_async_copy(k_out.at[n % 2], dk.at[rows, narrow], out_sem.at[2, n % 2]),
            pltpu.make_async_copy(v_out.at[n % 2], dv.at[rows, narrow], out_sem.at[3, n % 2]),
        ]

    zeros = jnp.zeros((S, HD), BF)
    one = jnp.ones((S, HD), BF)
    ones = jnp.concatenate([jnp.concatenate([one, zeros], axis=1), jnp.concatenate([zeros, one], axis=1)], axis=0)

    def twice(x):
        return jnp.concatenate([jnp.concatenate([x, zeros], axis=1), jnp.concatenate([zeros, x], axis=1)], axis=0)

    def spread_heads(x):
        return jnp.concatenate([x[:S, :HD], x[S:, :HD], x[:S, HD:], x[S:, HD:]], axis=1)

    row = lax.broadcasted_iota(jnp.int32, (HD, 1), 0)
    column = lax.broadcasted_iota(jnp.int32, (1, HD), 1)
    shared = 6 * S
    for buf in (o_buf, q_buf, k_buf, v_buf):
        buf[shared:, :] = jnp.zeros((MOVE + S - shared, buf.shape[1]), F32)
    for n in range(KV):
        for d in range(NDOC):
            load(d, n).wait()
            landing = landings[d]
            shift = landing & (S - 1)
            first = pl.multiple_of(landing - shift, S)
            causal = ((row - landing) & (S - 1)) <= ((column - landing) & (S - 1))
            base = KVROWS * n
            square = slot[d, base : base + 2 * S, :].astype(F32)
            weights = jnp.where(causal, square, 0.0)
            grad = (square - weights).astype(BF)
            kd = slot[d, base + 2 * S : base + 3 * S, :]
            vd = slot[d, base + 3 * S : base + 4 * S, :]
            attended = dot(weights.T.astype(BF), twice(vd), NN)
            k32 = kd.astype(F32)
            k22 = jnp.concatenate([jnp.concatenate([k32, k32], axis=1)] * 2, axis=0)
            query = (dot(grad, twice(kd), NN) - dot(grad, ones, NN) * k22) * SCALE

            def put(buf, value):
                kept = lax.broadcasted_iota(jnp.int32, value.shape, 0) >= shift
                pltpu.store(buf.at[pl.ds(first, S), :], value, mask=kept)
                pltpu.store(buf.at[pl.ds(first + S, S), :], value, mask=jnp.logical_not(kept))

            put(o_buf, spread_heads(attended))
            put(q_buf, spread_heads(query))
            put(k_buf, slot[d, base + 4 * S : base + 5 * S, :].astype(F32))
            put(v_buf, slot[d, base + 5 * S : base + 6 * S, :].astype(F32))
        if n >= 2:
            for copy in stores(n - 2):
                copy.wait()
        for buf, final in ((o_buf, o_out), (q_buf, q_out), (k_buf, k_out), (v_buf, v_out)):
            final[n % 2] = buf[:MOVE, :].astype(BF)
        for copy in stores(n):
            copy.start()
    for n in (KV - 2, KV - 1):
        for copy in stores(n):
            copy.wait()


def receive(sources, landings, recv, outs):
    hbm = pl.BlockSpec(memory_space=pltpu.HBM)
    smem = pl.BlockSpec(memory_space=pltpu.SMEM)
    padded = MOVE + S
    wide, narrow = GROUP * HD, HD
    return pl.pallas_call(
        receive_kernel,
        out_shape=[jax.ShapeDtypeStruct(o.shape, o.dtype) for o in outs],
        in_specs=[smem, smem] + [hbm] * 5,
        out_specs=[hbm] * 4,
        input_output_aliases={3 + i: i for i in range(4)},
        scratch_shapes=[
            pltpu.VMEM((NDOC, KVROWS * KV, HD), BF),
            pltpu.VMEM((padded, wide), F32),
            pltpu.VMEM((padded, wide), F32),
            pltpu.VMEM((padded, narrow), F32),
            pltpu.VMEM((padded, narrow), F32),
            pltpu.VMEM((2, MOVE, wide), BF),
            pltpu.VMEM((2, MOVE, wide), BF),
            pltpu.VMEM((2, MOVE, narrow), BF),
            pltpu.VMEM((2, MOVE, narrow), BF),
            pltpu.SemaphoreType.DMA((NDOC, KV)),
            pltpu.SemaphoreType.DMA((4, 2)),
        ],
        cost_estimate=pl.CostEstimate(flops=4_000_000_000, bytes_accessed=10_000_000, transcendentals=0),
        name="receive",
    )(sources, landings, recv, *outs)


def placement(codes):
    valid = codes > 0
    rank = jnp.sum((valid[None, :] & (codes[None, :] < codes[:, None])).astype(jnp.int32), axis=1)
    order = jnp.arange(NDOC, dtype=jnp.int32)
    chosen = valid[None, :] & (rank[None, :] == order[:, None])
    sources = jnp.sum(jnp.where(chosen, jnp.arange(NSLOT, dtype=jnp.int32)[None, :], 0), axis=1)
    landings = jnp.sum(jnp.where(chosen, (codes - 1)[None, :], 0), axis=1)
    return sources, landings


def codes_of(meta):
    pairs = meta.astype(F32).astype(jnp.int32)
    return pairs[:, 0] * 32 + pairs[:, S]


def swap(x, axis, size, mask):
    return lax.ppermute(x, axis, [(i, i ^ mask) for i in range(size)])


def add(*terms):
    total = terms[0].astype(F32)
    for term in terms[1:]:
        total = total + term.astype(F32)
    return total


def shifts(pieces, axis, size):
    return [lax.ppermute(pieces(step), axis, [(i, (i + step) % size) for i in range(size)]) for step in range(1, size)]


def reduce_cores(layer_grad):
    grad = layer_grad.reshape(2, 4, 2, 4, 64, layer_grad.shape[-1])
    core = lax.axis_index("core")
    mine = lax.dynamic_index_in_dim(grad, core, 2, keepdims=False)
    other = lax.dynamic_index_in_dim(grad, 1 - core, 2, keepdims=False)
    return add(mine, swap(other, "core", 2, 1)).astype(BF)


def reduce_ring(part, axis, dim):
    place = lax.axis_index(axis)

    def block(step):
        return lax.dynamic_index_in_dim(part, (place + step) % 4, dim, keepdims=False)

    return add(block(0), *shifts(block, axis, 4)).astype(BF)


def spread(total):
    place = lax.axis_index("z")
    held = jnp.stack([total] + shifts(lambda step: total, "z", 4))
    half = jnp.concatenate([lax.dynamic_index_in_dim(held, (place - b) % 4, 0, keepdims=False) for b in range(4)], axis=0)
    twin = swap(half, "core", 2, 1)
    core = lax.axis_index("core")
    first = jnp.where(core == 0, half, twin)
    second = jnp.where(core == 0, twin, half)
    return jnp.concatenate([first, second], axis=0).astype(F32)


def exchange(slots):
    return lax.all_to_all(slots, DP, split_axis=0, concat_axis=0, tiled=True)


def per_device(q, k, v, g, home_lengths, moved_lengths, moved_offsets, moved_owner, owner_offsets, layer_grad):
    table = jnp.concatenate([moved_lengths, moved_offsets, moved_owner, owner_offsets], axis=0)
    received = exchange(send(table, q, k, v, g))
    part = reduce_cores(layer_grad)
    part = reduce_ring(part, "x", 1)
    outs = home(home_lengths, q, k, v, g)
    part, outs = lax.optimization_barrier((part, outs))
    part = reduce_ring(part, "z", 1)
    part, received = lax.optimization_barrier((part, received))
    yhi = lax.axis_index("yhi")
    mine = lax.dynamic_index_in_dim(part, yhi, 0, keepdims=False)
    theirs = swap(lax.dynamic_index_in_dim(part, 1 - yhi, 0, keepdims=False), "yhi", 2, 1)
    sources, landings = placement(codes_of(received[:, KVROWS * KV, :]))
    outs = receive(sources, landings, received, outs)
    theirs, outs = lax.optimization_barrier((theirs, outs))
    total = add(mine, theirs).astype(BF)
    total = add(total, swap(total, "ylo", 2, 1)).astype(BF)
    return (*outs, spread(total))


def solution(mesh):
    fine = Mesh(mesh.devices.reshape(2, 4, 2, 2, 4), FINE)
    rows = P(FINE, None)
    return jax.shard_map(
        per_device,
        mesh=fine,
        in_specs=(rows,) * 9 + (P(DP, ("yhi", "x"), None, None),),
        out_specs=(rows, rows, rows, rows, P(("yhi", "x"), None)),
        check_vma=False,
    )
```

time: 180 us -> 155 us (0.86)
  waiting for transfers between devices: 91.7 us -> 67.3 us
  local copies, waits for them, and re-layouts: 15 us -> 5.52 us
  Pallas kernels: 34.4 us -> 38.5 us
  starting transfers between devices: 30.2 us -> 34.1 us
    all_to_all x1, waiting for transfers between devices: 47 us -> 8.47 us  [exchange(): return lax.all_to_all(slots, DP, split_axis=0, concat_axis=0, tiled=True)]
    ppermute x3 -> x9, waiting for transfers between devices: 25.6 us -> 50.3 us  [shifts(): lax.ppermute(pieces(step), axis, [(i, (i + step) % size) for i in range(s...]
    ppermute x3 -> x9, starting transfers between devices: 3.67 us -> 20.7 us  [shifts(): lax.ppermute(pieces(step), axis, [(i, (i + step) % size) for i in range(s...]
    ppermute x6 -> x4, starting transfers between devices: 18.6 us -> 5.52 us  [swap(): return lax.ppermute(x, axis, [(i, i ^ mask) for i in range(size)])]
    unnamed x20 -> x2, local copies, waits for them, and re-layouts: 11.8 us -> 1.34 us
    ppermute x6 -> x4, waiting for transfers between devices: 19.1 us -> 8.61 us  [swap(): return lax.ppermute(x, axis, [(i, i ^ mask) for i in range(size)])]
    dynamic_slice x0 -> x2, local copies, waits for them, and re-layouts: none -> 3.96 us  [the longest x1 2.51 us: reduce_cores(): mine = lax.dynamic_index_in_dim(grad, core, 2, keepdims=False)]
    pallas_call x2, Pallas kernels: 24.4 us -> 28.4 us  [the longest x1 16.4 us: send(): pl.pallas_call(send_kernel, out_shape=jax.ShapeDtypeStruct((NSLOT, KVROWS...]
  transfers between devices with their start and end apart: 10 -> 14, of which waited for: 7 -> 10; matrix products, arithmetic and copies ran while one was open for 5% -> 6% of each run, Pallas kernels for 10% -> 14%
where the time goes in v2:
time: 155 us; the launch traced here: 154 us
  waiting for transfers between devices  67.3 us (43%)
  Pallas kernels  38.5 us (25%)
  starting transfers between devices  34.1 us (22%)
  other arithmetic  8.1 us (5%)
  local copies, waits for them, and re-layouts  5.52 us (4%)
    ppermute x9, waiting for transfers between devices, shifts(): lax.ppermute(pieces(step), axis, [(i, (i + step) % size) for i in range(s...  50.3 us
    ppermute x9, starting transfers between devices, shifts(): lax.ppermute(pieces(step), axis, [(i, (i + step) % size) for i in range(s...  20.7 us
    pallas_call x1, Pallas kernels, send(): pl.pallas_call(send_kernel, out_shape=jax.ShapeDtypeStruct((NSLOT, KVROWS...  16.4 us
    pallas_call x1, Pallas kernels, receive(): pl.pallas_call(receive_kernel, out_shape=[jax.ShapeDtypeStruct(o.shape, o...  12 us
    pallas_call x1, Pallas kernels, home(): pl.pallas_call(home_kernel, out_shape=[jax.ShapeDtypeStruct((total, KV *...  10.1 us
    ppermute x4, waiting for transfers between devices, swap(): return lax.ppermute(x, axis, [(i, i ^ mask) for i in range(size)])  8.61 us
    all_to_all x1, waiting for transfers between devices, exchange(): return lax.all_to_all(slots, DP, split_axis=0, concat_axis=0, tiled=True)  8.47 us
    all_to_all x1, starting transfers between devices, exchange(): return lax.all_to_all(slots, DP, split_axis=0, concat_axis=0, tiled=True)  7.88 us
  transfers between devices with their start and end apart: 14, of which 10 were waited for; matrix products, arithmetic and copies ran while one was open for 6% of the time, Pallas kernels for 14%

profile of v2, /device:TPU:1, one launch (start us, length us, event | category | flops | bytes accessed | tf_op | source)
XLA Modules:
  0.0 154.3 jit_solution(147665783165836869)
XLA Ops:
  0.6 1.3 pad_add_fusion.table
  1.9 16.4 %send.1 = bf16[16,1544,128]{2,1,0:T(8,128)(2,1)} custom-call(s32[4,8]{1,0:T(4,128)} %pad_add_fusion.table, bf16[896,2048]{1,0:T(8,128)(2,1)} %q_hbm.1, bf16[896,512]{1,0:T(8,128)(2,1)} %k_hbm.1, bf16[896,512]{1,0:T(8,128)(2,1)} %v_hbm.1, bf16[896,2048]{1,0:T(8,128)(2,1)} %g_hbm.1), custom_call_target="tpu_custom_call" | custom-call | flops 4000000000 | bytes 10000000 | tf_op jit(solution)/shard_map/send/pallas_call | solution.py:130
  18.3 7.9 %all-to-all-start = ((bf16[16,1544,128]{2,1,0:T(8,128)(2,1)}), bf16[16,1544,128]{2,1,0:T(8,128)(2,1)}, u32[]{:S(2)}, u32[]{:S(2)}) async-start(bf16[16,1544,128]{2,1,0:T(8,128)(2,1)} %send.1), calls=%async_computation | async-start | bytes 12648448 | tf_op jit(solution)/shard_map/all_to_all | solution.py:374
  26.2 2.5 %constant_dynamic-slice_fusion.1 = (bf16[2,4,1,4,64,512]{5,4,3,2,1,0:T(8,128)(2,1)S(1)}, bf16[2,4,1,4,64,512]{5,4,3,2,1,0:T(8,128)(2,1)S(1)}) fusion(bf16[2,4,2,4,64,512]{5,4,3,2,1,0:T(8,128)(2,1)} %bitcast.45, s32[]{:T(128)S(6)} %select_n.119, s32[]{:T(128)S(6)} %select_n.120), kind=kLoop, calls=%fused_computation.40 | loop fusion | bytes 8388616 | tf_op jit(solution)/shard_map/jit(dynamic_index_in_dim)/dynamic_slice | solution.py:348
  28.7 1.5 copy.30
  30.4 4.3 %collective-permute-done = bf16[2,4,4,64,512]{4,3,0,2,1:T(8,128)(2,1)} collective-permute-done((bf16[2,4,4,64,512]{4,3,0,2,1:T(8,128)(2,1)}, bf16[2,4,4,64,512]{4,3,0,2,1:T(8,128)(2,1)}, u32[]{:S(2)}, u32[]{:S(2)}) %collective-permute-start) | collective-permute-done | bytes 2097184 | tf_op jit(solution)/shard_map/ppermute | solution.py:331
  34.7 2.3 %fusion = bf16[2,4,4,64,512]{4,3,0,2,1:T(8,128)(2,1)S(1)} fusion(bf16[2,4,4,64,512]{4,3,0,2,1:T(8,128)(2,1)} %collective-permute-done, bf16[2,4,1,4,64,512]{5,4,3,2,1,0:T(8,128)(2,1)S(1)} %get-tuple-element.47), kind=kLoop, calls=%fused_computation.1 | loop fusion | flops 4194304 | bytes 6291456 | tf_op jit(solution)/shard_map/convert_element_type | solution.py:350
  37.0 1.3 copy-done
  38.5 1.3 collective-permute-start.1
  39.8 2.5 %collective-permute-start.2 = (bf16[2,4,64,512]{3,2,0,1:T(8,128)(2,1)S(1)}, bf16[2,4,64,512]{3,2,0,1:T(8,128)(2,1)S(1)}, u32[]{:S(2)}, u32[]{:S(2)}) collective-permute-start(bf16[2,4,64,512]{3,2,0,1:T(8,128)(2,1)S(1)} %get-tuple-element.51), channel_id=1, source_target_pairs={{0,2},{1,3},{2,0},{3,1},{4,6},{5,7},{6,4},{7,5},{8,10},{9,11},{10,... | collective-permute-start | bytes 1572872 | tf_op jit(solution)/shard_map/ppermute | solution.py:342
  42.3 1.1 collective-permute-start.3
  43.4 10.1 %home.1 = (bf16[896,2048]{1,0:T(8,128)(2,1)}, bf16[896,2048]{1,0:T(8,128)(2,1)}, bf16[896,512]{1,0:T(8,128)(2,1)}, bf16[896,512]{1,0:T(8,128)(2,1)}) custom-call(s32[1,6]{1,0:T(1,128)} %lengths.1, bf16[896,2048]{1,0:T(8,128)(2,1)} %q_hbm.1, bf16[896,512]{1,0:T(8,128)(2,1)} %k_hbm.1, bf16[896,512]{1,0:T(8,128)(2,1)} %v_hbm.1, bf16[896,2048]{1,0:T(8,128)(2,1)} %g_hbm.1), custom_call_target="tpu_custom_call" | custom-call | flops 10000000000 | bytes 10000000 | tf_op jit(solution)/shard_map/home/pallas_call | solution.py:194
  53.5 12.0 %collective-permute-done.2 = bf16[2,4,64,512]{3,2,0,1:T(8,128)(2,1)S(1)} collective-permute-done((bf16[2,4,64,512]{3,2,0,1:T(8,128)(2,1)S(1)}, bf16[2,4,64,512]{3,2,0,1:T(8,128)(2,1)S(1)}, u32[]{:S(2)}, u32[]{:S(2)}) %collective-permute-start.2) | collective-permute-done | bytes 524320 | tf_op jit(solution)/shard_map/ppermute | solution.py:342
  65.5 1.3 fusion.3
  66.9 1.1 collective-permute-start.4
  68.0 2.5 %collective-permute-start.5 = (bf16[2,64,512]{2,1,0:T(8,128)(2,1)S(1)}, bf16[2,64,512]{2,1,0:T(8,128)(2,1)S(1)}, u32[]{:S(2)}, u32[]{:S(2)}) collective-permute-start(bf16[2,64,512]{2,1,0:T(8,128)(2,1)S(1)} %get-tuple-element.56), channel_id=1, source_target_pairs={{0,32},{16,48},{32,0},{48,16},{1,33},{17,49},{33,1},{49,17},{2,34}... | collective-permute-start | bytes 393224 | tf_op jit(solution)/shard_map/ppermute | solution.py:342
  70.5 1.1 collective-permute-start.6
  71.6 29.0 %collective-permute-done.4 = bf16[2,64,512]{2,1,0:T(8,128)(2,1)S(1)} collective-permute-done((bf16[2,64,512]{2,1,0:T(8,128)(2,1)S(1)}, bf16[2,64,512]{2,1,0:T(8,128)(2,1)S(1)}, u32[]{:S(2)}, u32[]{:S(2)}) %collective-permute-start.4) | collective-permute-done | bytes 131104 | tf_op jit(solution)/shard_map/ppermute | solution.py:342
  100.7 5.2 %collective-permute-done.5 = bf16[2,64,512]{2,1,0:T(8,128)(2,1)S(1)} collective-permute-done((bf16[2,64,512]{2,1,0:T(8,128)(2,1)S(1)}, bf16[2,64,512]{2,1,0:T(8,128)(2,1)S(1)}, u32[]{:S(2)}, u32[]{:S(2)}) %collective-permute-start.5) | collective-permute-done | bytes 131104 | tf_op jit(solution)/shard_map/ppermute | solution.py:342
  105.9 8.5 %all-to-all-done.recv = bf16[16,1544,128]{2,1,0:T(8,128)(2,1)} async-done(((bf16[16,1544,128]{2,1,0:T(8,128)(2,1)}), bf16[16,1544,128]{2,1,0:T(8,128)(2,1)}, u32[]{:S(2)}, u32[]{:S(2)}) %all-to-all-start) | async-done | bytes 6324256 | tf_op jit(solution)/shard_map/all_to_all | solution.py:374
  114.4 0.8 convert_convert_fusion
  115.6 2.7 %collective-permute-start.7 = (bf16[64,512]{1,0:T(8,128)(2,1)S(1)}, bf16[64,512]{1,0:T(8,128)(2,1)S(1)}, u32[]{:S(2)}, u32[]{:S(2)}) collective-permute-start(bf16[64,512]{1,0:T(8,128)(2,1)S(1)} %dynamic-slice_bitcast_fusion.10), channel_id=1, source_target_pairs={{0,4},{4,0},{1,5},{5,1},{2,6},{6,2},{3,7},{7,3},{8,12},{12,8},{9,1... | collective-permute-start | bytes 196616 | tf_op jit(solution)/shard_map/ppermute | solution.py:331
  118.3 0.7 select_reduce_fusion
  119.0 12.0 %receive.1 = (bf16[896,2048]{1,0:T(8,128)(2,1)}, bf16[896,2048]{1,0:T(8,128)(2,1)}, bf16[896,512]{1,0:T(8,128)(2,1)}, bf16[896,512]{1,0:T(8,128)(2,1)}) custom-call(s32[8]{0:T(128)} %get-tuple-element.46.sources, s32[8]{0:T(128)} %get-tuple-element.45.landings, ...), custom_call_target="tpu_custom_call", output_to_operand_aliasing={{0}: (3, {}), {1}: (4, {}), {2}: (5, {}), {3}: (6, {})} | custom-call | flops 4000000000 | bytes 10000000 | tf_op jit(solution)/shard_map/receive/pallas_call | solution.py:291
  131.1 3.1 %collective-permute-done.8 = bf16[64,512]{1,0:T(8,128)(2,1)S(1)} collective-permute-done((bf16[64,512]{1,0:T(8,128)(2,1)S(1)}, bf16[64,512]{1,0:T(8,128)(2,1)S(1)}, u32[]{:S(2)}, u32[]{:S(2)}) %collective-permute-start.8) | collective-permute-done | bytes 65568 | tf_op jit(solution)/shard_map/ppermute | solution.py:331
  134.2 6.7 %collective-permute-start.9 = (bf16[64,512]{1,0:T(8,128)(2,1)S(1)}, bf16[64,512]{1,0:T(8,128)(2,1)S(1)}, u32[]{:S(2)}, u32[]{:S(2)}) collective-permute-start(bf16[64,512]{1,0:T(8,128)(2,1)S(1)} %add_convert_fusion), channel_id=1, source_target_pairs={{0,16},{16,32},{32,48},{48,0},{1,17},{17,33},{33,49},{49,1},{2,18}... | collective-permute-start | bytes 196616 | tf_op jit(solution)/shard_map/ppermute | solution.py:342
  140.9 4.4 %collective-permute-start.10 = (bf16[64,512]{1,0:T(8,128)(2,1)S(1)}, bf16[64,512]{1,0:T(8,128)(2,1)S(1)}, u32[]{:S(2)}, u32[]{:S(2)}) collective-permute-start(bf16[64,512]{1,0:T(8,128)(2,1)S(1)} %add_convert_fusion), channel_id=1, source_target_pairs={{0,32},{16,48},{32,0},{48,16},{1,33},{17,49},{33,1},{49,17},{2,34}... | collective-permute-start | bytes 196616 | tf_op jit(solution)/shard_map/ppermute | solution.py:342
  145.8 2.0 %collective-permute-done.10 = bf16[64,512]{1,0:T(8,128)(2,1)S(1)} collective-permute-done((bf16[64,512]{1,0:T(8,128)(2,1)S(1)}, bf16[64,512]{1,0:T(8,128)(2,1)S(1)}, u32[]{:S(2)}, u32[]{:S(2)}) %collective-permute-start.10) | collective-permute-done | bytes 65568 | tf_op jit(solution)/shard_map/ppermute | solution.py:342
  147.8 1.5 collective-permute-done.11
  149.4 2.6 %collective-permute-start.12 = (bf16[256,512]{1,0:T(8,128)(2,1)S(1)}, bf16[256,512]{1,0:T(8,128)(2,1)S(1)}, u32[]{:S(2)}, u32[]{:S(2)}) collective-permute-start(bf16[256,512]{1,0:T(8,128)(2,1)S(1)} %pad_maximum_fusion.1), channel_id=1, source_target_pairs={{0,8},{8,0},{1,9},{9,1},{2,10},{10,2},{3,11},{11,3},{4,12},{12,4},... | collective-permute-start | bytes 786440 | tf_op jit(solution)/shard_map/ppermute | solution.py:331
  152.0 1.2 collective-permute-done.12
  153.2 1.1 maximum_convert_fusion
  (23 shorter events, 1.6 us)
Async XLA Ops:
  18.3 96.1 %all-to-all-start = ((bf16[16,1544,128]{2,1,0:T(8,128)(2,1)}), bf16[16,1544,128]{2,1,0:T(8,128)(2,1)}, u32[]{:S(2)}, u32[]{:S(2)}) async-start(bf16[16,1544,128]{2,1,0:T(8,128)(2,1)} %send.1), calls=%async_computation | async-start | bytes 12648448 | tf_op jit(solution)/shard_map/all_to_all | solution.py:374
  30.2 4.5 %collective-permute-start = (bf16[2,4,4,64,512]{4,3,0,2,1:T(8,128)(2,1)}, bf16[2,4,4,64,512]{4,3,0,2,1:T(8,128)(2,1)}, u32[]{:S(2)}, u32[]{:S(2)}) collective-permute-start(bf16[2,4,4,64,512]{4,3,0,2,1:T(8,128)(2,1)} %bitcast.44), channel_id=1, source_target_pairs={{0,8},{8,0},{1,9},{9,1},{2,10},{10,2},{3,11},{11,3},{4,12},{12,4},... | collective-permute-start | bytes 6291464 | tf_op jit(solution)/shard_map/ppermute | solution.py:331
  37.0 1.4 copy-start
  38.5 15.0 %collective-permute-start.1 = (bf16[2,4,64,512]{3,2,0,1:T(8,128)(2,1)S(1)}, bf16[2,4,64,512]{3,2,0,1:T(8,128)(2,1)S(1)}, u32[]{:S(2)}, u32[]{:S(2)}) collective-permute-start(bf16[2,4,64,512]{3,2,0,1:T(8,128)(2,1)S(1)} %get-tuple-element.49), channel_id=1, source_target_pairs={{0,1},{1,2},{2,3},{3,0},{4,5},{5,6},{6,7},{7,4},{8,9},{9,10},{10,1... | collective-permute-start | bytes 1572872 | tf_op jit(solution)/shard_map/ppermute | solution.py:342
  39.8 25.7 %collective-permute-start.2 = (bf16[2,4,64,512]{3,2,0,1:T(8,128)(2,1)S(1)}, bf16[2,4,64,512]{3,2,0,1:T(8,128)(2,1)S(1)}, u32[]{:S(2)}, u32[]{:S(2)}) collective-permute-start(bf16[2,4,64,512]{3,2,0,1:T(8,128)(2,1)S(1)} %get-tuple-element.51), channel_id=1, source_target_pairs={{0,2},{1,3},{2,0},{3,1},{4,6},{5,7},{6,4},{7,5},{8,10},{9,11},{10,... | collective-permute-start | bytes 1572872 | tf_op jit(solution)/shard_map/ppermute | solution.py:342
  42.3 23.3 %collective-permute-start.3 = (bf16[2,4,64,512]{3,2,0,1:T(8,128)(2,1)S(1)}, bf16[2,4,64,512]{3,2,0,1:T(8,128)(2,1)S(1)}, u32[]{:S(2)}, u32[]{:S(2)}) collective-permute-start(bf16[2,4,64,512]{3,2,0,1:T(8,128)(2,1)S(1)} %get-tuple-element.50), channel_id=1, source_target_pairs={{0,3},{1,0},{2,1},{3,2},{4,7},{5,4},{6,5},{7,6},{8,11},{9,8},{10,9... | collective-permute-start | bytes 1572872 | tf_op jit(solution)/shard_map/ppermute | solution.py:342
  66.9 33.8 %collective-permute-start.4 = (bf16[2,64,512]{2,1,0:T(8,128)(2,1)S(1)}, bf16[2,64,512]{2,1,0:T(8,128)(2,1)S(1)}, u32[]{:S(2)}, u32[]{:S(2)}) collective-permute-start(bf16[2,64,512]{2,1,0:T(8,128)(2,1)S(1)} %get-tuple-element.54), channel_id=1, source_target_pairs={{0,16},{16,32},{32,48},{48,0},{1,17},{17,33},{33,49},{49,1},{2,18}... | collective-permute-start | bytes 393224 | tf_op jit(solution)/shard_map/ppermute | solution.py:342
  68.0 37.8 %collective-permute-start.5 = (bf16[2,64,512]{2,1,0:T(8,128)(2,1)S(1)}, bf16[2,64,512]{2,1,0:T(8,128)(2,1)S(1)}, u32[]{:S(2)}, u32[]{:S(2)}) collective-permute-start(bf16[2,64,512]{2,1,0:T(8,128)(2,1)S(1)} %get-tuple-element.56), channel_id=1, source_target_pairs={{0,32},{16,48},{32,0},{48,16},{1,33},{17,49},{33,1},{49,17},{2,34}... | collective-permute-start | bytes 393224 | tf_op jit(solution)/shard_map/ppermute | solution.py:342
  70.5 35.3 %collective-permute-start.6 = (bf16[2,64,512]{2,1,0:T(8,128)(2,1)S(1)}, bf16[2,64,512]{2,1,0:T(8,128)(2,1)S(1)}, u32[]{:S(2)}, u32[]{:S(2)}) collective-permute-start(bf16[2,64,512]{2,1,0:T(8,128)(2,1)S(1)} %get-tuple-element.55), channel_id=1, source_target_pairs={{0,48},{16,0},{32,16},{48,32},{1,49},{17,1},{33,17},{49,33},{2,50}... | collective-permute-start | bytes 393224 | tf_op jit(solution)/shard_map/ppermute | solution.py:342
  115.6 15.4 %collective-permute-start.7 = (bf16[64,512]{1,0:T(8,128)(2,1)S(1)}, bf16[64,512]{1,0:T(8,128)(2,1)S(1)}, u32[]{:S(2)}, u32[]{:S(2)}) collective-permute-start(bf16[64,512]{1,0:T(8,128)(2,1)S(1)} %dynamic-slice_bitcast_fusion.10), channel_id=1, source_target_pairs={{0,4},{4,0},{1,5},{5,1},{2,6},{6,2},{3,7},{7,3},{8,12},{12,8},{9,1... | collective-permute-start | bytes 196616 | tf_op jit(solution)/shard_map/ppermute | solution.py:331
  131.0 3.2 %collective-permute-start.8 = (bf16[64,512]{1,0:T(8,128)(2,1)S(1)}, bf16[64,512]{1,0:T(8,128)(2,1)S(1)}, u32[]{:S(2)}, u32[]{:S(2)}) collective-permute-start(bf16[64,512]{1,0:T(8,128)(2,1)S(1)} %fusion.7), channel_id=1, source_target_pairs={{0,64},{64,0},{1,65},{65,1},{2,66},{66,2},{3,67},{67,3},{4,68},{68... | collective-permute-start | bytes 196616 | tf_op jit(solution)/shard_map/ppermute | solution.py:331
  134.2 11.6 %collective-permute-start.9 = (bf16[64,512]{1,0:T(8,128)(2,1)S(1)}, bf16[64,512]{1,0:T(8,128)(2,1)S(1)}, u32[]{:S(2)}, u32[]{:S(2)}) collective-permute-start(bf16[64,512]{1,0:T(8,128)(2,1)S(1)} %add_convert_fusion), channel_id=1, source_target_pairs={{0,16},{16,32},{32,48},{48,0},{1,17},{17,33},{33,49},{49,1},{2,18}... | collective-permute-start | bytes 196616 | tf_op jit(solution)/shard_map/ppermute | solution.py:342
  140.9 6.9 %collective-permute-start.10 = (bf16[64,512]{1,0:T(8,128)(2,1)S(1)}, bf16[64,512]{1,0:T(8,128)(2,1)S(1)}, u32[]{:S(2)}, u32[]{:S(2)}) collective-permute-start(bf16[64,512]{1,0:T(8,128)(2,1)S(1)} %add_convert_fusion), channel_id=1, source_target_pairs={{0,32},{16,48},{32,0},{48,16},{1,33},{17,49},{33,1},{49,17},{2,34}... | collective-permute-start | bytes 196616 | tf_op jit(solution)/shard_map/ppermute | solution.py:342
  145.3 4.0 %collective-permute-start.11 = (bf16[64,512]{1,0:T(8,128)(2,1)S(1)}, bf16[64,512]{1,0:T(8,128)(2,1)S(1)}, u32[]{:S(2)}, u32[]{:S(2)}) collective-permute-start(bf16[64,512]{1,0:T(8,128)(2,1)S(1)} %add_convert_fusion), channel_id=1, source_target_pairs={{0,48},{16,0},{32,16},{48,32},{1,49},{17,1},{33,17},{49,33},{2,50}... | collective-permute-start | bytes 196616 | tf_op jit(solution)/shard_map/ppermute | solution.py:342
  149.4 3.7 %collective-permute-start.12 = (bf16[256,512]{1,0:T(8,128)(2,1)S(1)}, bf16[256,512]{1,0:T(8,128)(2,1)S(1)}, u32[]{:S(2)}, u32[]{:S(2)}) collective-permute-start(bf16[256,512]{1,0:T(8,128)(2,1)S(1)} %pad_maximum_fusion.1), channel_id=1, source_target_pairs={{0,8},{8,0},{1,9},{9,1},{2,10},{10,2},{3,11},{11,3},{4,12},{12,4},... | collective-permute-start | bytes 786440 | tf_op jit(solution)/shard_map/ppermute | solution.py:331

commit v3 on v2

--- a/solution.py
+++ b/solution.py
@@ -18,6 +18,7 @@
 KV = 4
 WIN = 80
 NSLOT = 16
+NFAR = 8
 KVROWS = 6 * S
 META = 8
 SCALE = 1.0 / math.sqrt(HD)
@@ -52,7 +53,8 @@
 
 
 def send_kernel(table, q_hbm, k_hbm, v_hbm, g_hbm, *refs):
-    out, q, k, v, g, slot, meta, in_sem, out_sem, meta_sem = refs
+    near, far = refs[0], refs[1 : 1 + NFAR]
+    q, k, v, g, slot, meta, in_sem, out_sem, meta_sem = refs[1 + NFAR :]
     chunk = 128
     pairs = ((q_hbm, q), (g_hbm, g), (k_hbm, k), (v_hbm, v))
 
@@ -70,11 +72,28 @@
             code = code + jnp.where(table[2, d] == s, table[3, d] + 1, 0)
         meta[s] = jnp.where(lane < S, lax.shift_right_logical(code, 5), code & 31).astype(F32).astype(BF)
 
-    meta_copy = pltpu.make_async_copy(meta, out.at[:, pl.ds(KVROWS * KV, META), :], meta_sem)
-    meta_copy.start()
+    body, tail = pl.ds(0, KVROWS * KV), pl.ds(KVROWS * KV, META)
+    meta_copies = [pltpu.make_async_copy(meta.at[pl.ds(0, NFAR)], near.at[:, tail, :], meta_sem.at[NFAR])]
+    meta_copies += [pltpu.make_async_copy(meta.at[NFAR + m], far[m].at[tail, :], meta_sem.at[m]) for m in range(NFAR)]
+    for copy in meta_copies:
+        copy.start()
+
+    def store_near(d):
+        return pltpu.make_async_copy(slot.at[d % 2], near.at[table[2, d] & (NFAR - 1), body, :], out_sem.at[d % 2])
+
+    def store_far(d, m):
+        return pltpu.make_async_copy(slot.at[d % 2], far[m].at[body, :], out_sem.at[d % 2])
 
     def store(d):
-        return pltpu.make_async_copy(slot.at[d % 2], out.at[table[2, d], pl.ds(0, KVROWS * KV), :], out_sem.at[d % 2])
+        @pl.when(table[2, d] < NFAR)
+        def _():
+            store_near(d).start()
+
+        for m in range(NFAR):
+
+            @pl.when(table[2, d] == NFAR + m)
+            def _(m=m):
+                store_far(d, m).start()
 
     same = (lax.broadcasted_iota(jnp.int32, (HD, HD), 0) & (S - 1)) == (lax.broadcasted_iota(jnp.int32, (HD, HD), 1) & (S - 1))
     loaded = -1
@@ -97,41 +116,44 @@
         all_k = dot(pick, k[window, :], NN).astype(BF)
         all_v = dot(pick, v[window, :], NN).astype(BF)
         if d >= 2:
-            store(d - 2).wait()
+            store_far(d - 2, 0).wait()
         here = slot.at[d % 2]
-        for n in range(KV):
-            kd = all_k[:, HD * n : HD * (n + 1)]
-            vd = all_v[:, HD * n : HD * (n + 1)]
-            cols = slice(GROUP * HD * n, GROUP * HD * (n + 1))
-            qs = heads_to_rows(dot(pick, q[window, cols], NN).astype(BF))
-            gs = heads_to_rows(dot(pick, g[window, cols], NN).astype(BF))
-            weights = transposed_softmax(dot(kd, qs, NT), allowed, filled)
-            logits = dot(vd, gs, NT)
-            delta = jnp.sum(weights * logits, axis=0, keepdims=True)
-            grad = weights * (logits - delta)
-            dv = dot(weights.astype(BF), gs, NN).astype(BF)
-            dk = (dot(grad.astype(BF), qs, NN) * SCALE).astype(BF)
-            turned = jnp.concatenate([grad[:, :HD], grad[:, HD:]], axis=0).T
-            square = jnp.concatenate([weights[:, :HD], weights[:, HD:]], axis=0) + jnp.where(same, 0.0, turned)
+        each = range(KV)
+        wide = [slice(GROUP * HD * n, GROUP * HD * (n + 1)) for n in each]
+        kd = [all_k[:, HD * n : HD * (n + 1)] for n in each]
+        vd = [all_v[:, HD * n : HD * (n + 1)] for n in each]
+        qs = [heads_to_rows(dot(pick, q[window, wide[n]], NN).astype(BF)) for n in each]
+        gs = [heads_to_rows(dot(pick, g[window, wide[n]], NN).astype(BF)) for n in each]
+        scores = [dot(kd[n], qs[n], NT) for n in each]
+        logits = [dot(vd[n], gs[n], NT) for n in each]
+        weights = [transposed_softmax(scores[n], allowed, filled) for n in each]
+        delta = [jnp.sum(weights[n] * logits[n], axis=0, keepdims=True) for n in each]
+        grad = [weights[n] * (logits[n] - delta[n]) for n in each]
+        both = [jnp.concatenate([weights[n].astype(BF), grad[n].astype(BF)], axis=0) for n in each]
+        summed = [dot(both[n], jnp.concatenate([gs[n], qs[n]], axis=1), NN) for n in each]
+        for n in each:
+            turned = jnp.concatenate([grad[n][:, :HD], grad[n][:, HD:]], axis=0).T
+            square = jnp.concatenate([weights[n][:, :HD], weights[n][:, HD:]], axis=0) + jnp.where(same, 0.0, turned)
             base = KVROWS * n
             here[base : base + 2 * S, :] = square.astype(BF)
-            here[base + 2 * S : base + 3 * S, :] = kd
-            here[base + 3 * S : base + 4 * S, :] = vd
-            here[base + 4 * S : base + 5 * S, :] = dk
-            here[base + 5 * S : base + 6 * S, :] = dv
-        store(d).start()
-    store(NDOC - 2).wait()
-    store(NDOC - 1).wait()
-    meta_copy.wait()
+            here[base + 2 * S : base + 3 * S, :] = kd[n]
+            here[base + 3 * S : base + 4 * S, :] = vd[n]
+            here[base + 4 * S : base + 5 * S, :] = (summed[n][S:, HD:] * SCALE).astype(BF)
+            here[base + 5 * S : base + 6 * S, :] = summed[n][:S, :HD].astype(BF)
+        store(d)
+    store_far(NDOC - 2, 0).wait()
+    store_far(NDOC - 1, 0).wait()
+    for copy in meta_copies:
+        copy.wait()
 
 
 def send(table, q, k, v, g):
     hbm = pl.BlockSpec(memory_space=pltpu.HBM)
     return pl.pallas_call(
         send_kernel,
-        out_shape=jax.ShapeDtypeStruct((NSLOT, KVROWS * KV + META, HD), BF),
+        out_shape=[jax.ShapeDtypeStruct((NFAR, KVROWS * KV + META, HD), BF)] + [jax.ShapeDtypeStruct((KVROWS * KV + META, HD), BF)] * NFAR,
         in_specs=[pl.BlockSpec(memory_space=pltpu.SMEM)] + [hbm] * 4,
-        out_specs=hbm,
+        out_specs=[hbm] * (1 + NFAR),
         scratch_shapes=[
             pltpu.VMEM((MOVE, KV * GROUP * HD), BF),
             pltpu.VMEM((MOVE, KV * HD), BF),
@@ -141,7 +163,7 @@
             pltpu.VMEM((NSLOT, META, HD), BF),
             pltpu.SemaphoreType.DMA((4, 4)),
             pltpu.SemaphoreType.DMA((2,)),
-            pltpu.SemaphoreType.DMA,
+            pltpu.SemaphoreType.DMA((1 + NFAR,)),
         ],
         cost_estimate=pl.CostEstimate(flops=4_000_000_000, bytes_accessed=10_000_000, transcendentals=1_000_000),
         name="send",
@@ -208,17 +230,30 @@
     )(lengths, q, k, v, g)
 
 
-def receive_kernel(sources, landings, recv, *refs):
-    out, dq, dk, dv = refs[4:8]
-    slot, o_buf, q_buf, k_buf, v_buf, o_out, q_out, k_out, v_out, in_sem, out_sem = refs[8:]
-
-    def load(d, n):
+def receive_kernel(sources, landings, near, *refs):
+    far = refs[:NFAR]
+    out, dq, dk, dv = refs[NFAR + 4 : NFAR + 8]
+    slot, o_buf, q_buf, k_buf, v_buf, o_out, q_out, k_out, v_out, in_sem, out_sem = refs[NFAR + 8 :]
+
+    def load(d, n, m=0):
         rows = pl.ds(KVROWS * n, KVROWS)
-        return pltpu.make_async_copy(recv.at[sources[d], rows, :], slot.at[d, rows, :], in_sem.at[d, n])
-
-    for n in range(KV):
-        for d in range(NDOC):
-            load(d, n).start()
+        return pltpu.make_async_copy(far[m].at[rows, :], slot.at[d, rows, :], in_sem.at[d, n])
+
+    for d in range(NDOC):
+
+        @pl.when(sources[d] < NFAR)
+        def _(d=d):
+            for n in range(KV):
+                rows = pl.ds(KVROWS * n, KVROWS)
+                pltpu.make_async_copy(near.at[sources[d] & (NFAR - 1), rows, :], slot.at[d, rows, :], in_sem.at[d, n]).start()
+
+        for m in range(NFAR):
+
+            @pl.when(sources[d] == NFAR + m)
+            def _(d=d, m=m):
+                for n in range(KV):
+                    load(d, n, m).start()
+
 
     def stores(n):
         rows, wide, narrow = pl.ds(HOME, MOVE), pl.ds(GROUP * HD * n, GROUP * HD), pl.ds(HD * n, HD)
@@ -230,8 +265,10 @@
         ]
 
     zeros = jnp.zeros((S, HD), BF)
-    one = jnp.ones((S, HD), BF)
-    ones = jnp.concatenate([jnp.concatenate([one, zeros], axis=1), jnp.concatenate([zeros, one], axis=1)], axis=0)
+    lower = lax.broadcasted_iota(jnp.int32, (HD, HD), 0)
+    across = lax.broadcasted_iota(jnp.int32, (HD, HD), 1)
+    same = (lower & (S - 1)) == (across & (S - 1))
+    ones = jnp.where((lower < S) == (across < S), 1.0, 0.0).astype(BF)
 
     def twice(x):
         return jnp.concatenate([jnp.concatenate([x, zeros], axis=1), jnp.concatenate([zeros, x], axis=1)], axis=0)
@@ -244,33 +281,34 @@
     shared = 6 * S
     for buf in (o_buf, q_buf, k_buf, v_buf):
         buf[shared:, :] = jnp.zeros((MOVE + S - shared, buf.shape[1]), F32)
+    docs = range(NDOC)
+    landing = [landings[d] for d in docs]
+    shift = [landing[d] & (S - 1) for d in docs]
+    first = [pl.multiple_of(landing[d] - shift[d], S) for d in docs]
     for n in range(KV):
-        for d in range(NDOC):
+        for d in docs:
             load(d, n).wait()
-            landing = landings[d]
-            shift = landing & (S - 1)
-            first = pl.multiple_of(landing - shift, S)
-            causal = ((row - landing) & (S - 1)) <= ((column - landing) & (S - 1))
-            base = KVROWS * n
-            square = slot[d, base : base + 2 * S, :].astype(F32)
-            weights = jnp.where(causal, square, 0.0)
-            grad = (square - weights).astype(BF)
-            kd = slot[d, base + 2 * S : base + 3 * S, :]
-            vd = slot[d, base + 3 * S : base + 4 * S, :]
-            attended = dot(weights.T.astype(BF), twice(vd), NN)
-            k32 = kd.astype(F32)
-            k22 = jnp.concatenate([jnp.concatenate([k32, k32], axis=1)] * 2, axis=0)
-            query = (dot(grad, twice(kd), NN) - dot(grad, ones, NN) * k22) * SCALE
-
-            def put(buf, value):
-                kept = lax.broadcasted_iota(jnp.int32, value.shape, 0) >= shift
-                pltpu.store(buf.at[pl.ds(first, S), :], value, mask=kept)
-                pltpu.store(buf.at[pl.ds(first + S, S), :], value, mask=jnp.logical_not(kept))
-
-            put(o_buf, spread_heads(attended))
-            put(q_buf, spread_heads(query))
-            put(k_buf, slot[d, base + 4 * S : base + 5 * S, :].astype(F32))
-            put(v_buf, slot[d, base + 5 * S : base + 6 * S, :].astype(F32))
+        base = KVROWS * n
+        for half in (docs[: NDOC // 2], docs[NDOC // 2 :]):
+            causal = {d: ((row - landing[d]) & (S - 1)) <= ((column - landing[d]) & (S - 1)) for d in half}
+            square = {d: slot[d, base : base + 2 * S, :].astype(F32) for d in half}
+            weights = {d: jnp.where(causal[d], square[d], 0.0) for d in half}
+            grad = {d: square[d] - weights[d] for d in half}
+            sums = {d: dot(grad[d].astype(BF), ones, NN) for d in half}
+            attended = {d: dot(weights[d].T.astype(BF), twice(slot[d, base + 3 * S : base + 4 * S, :]), NN) for d in half}
+            grad = {d: jnp.where(same, -sums[d], grad[d]).astype(BF) for d in half}
+            query = {d: dot(grad[d], twice(slot[d, base + 2 * S : base + 3 * S, :]), NN) * SCALE for d in half}
+
+            def put(buf, d, value):
+                kept = lax.broadcasted_iota(jnp.int32, value.shape, 0) >= shift[d]
+                pltpu.store(buf.at[pl.ds(first[d], S), :], value, mask=kept)
+                pltpu.store(buf.at[pl.ds(first[d] + S, S), :], value, mask=jnp.logical_not(kept))
+
+            for d in half:
+                put(o_buf, d, spread_heads(attended[d]))
+                put(q_buf, d, spread_heads(query[d]))
+                put(k_buf, d, slot[d, base + 4 * S : base + 5 * S, :].astype(F32))
+                put(v_buf, d, slot[d, base + 5 * S : base + 6 * S, :].astype(F32))
         if n >= 2:
             for copy in stores(n - 2):
                 copy.wait()
@@ -283,7 +321,7 @@
             copy.wait()
 
 
-def receive(sources, landings, recv, outs):
+def receive(sources, landings, near, far, outs):
     hbm = pl.BlockSpec(memory_space=pltpu.HBM)
     smem = pl.BlockSpec(memory_space=pltpu.SMEM)
     padded = MOVE + S
@@ -291,9 +329,9 @@
     return pl.pallas_call(
         receive_kernel,
         out_shape=[jax.ShapeDtypeStruct(o.shape, o.dtype) for o in outs],
-        in_specs=[smem, smem] + [hbm] * 5,
+        in_specs=[smem, smem] + [hbm] * (1 + NFAR + 4),
         out_specs=[hbm] * 4,
-        input_output_aliases={3 + i: i for i in range(4)},
+        input_output_aliases={3 + NFAR + i: i for i in range(4)},
         scratch_shapes=[
             pltpu.VMEM((NDOC, KVROWS * KV, HD), BF),
             pltpu.VMEM((padded, wide), F32),
@@ -309,7 +347,7 @@
         ],
         cost_estimate=pl.CostEstimate(flops=4_000_000_000, bytes_accessed=10_000_000, transcendentals=0),
         name="receive",
-    )(sources, landings, recv, *outs)
+    )(sources, landings, near, *far, *outs)
 
 
 def placement(codes):
@@ -359,39 +397,59 @@
     return add(block(0), *shifts(block, axis, 4)).astype(BF)
 
 
-def spread(total):
-    place = lax.axis_index("z")
-    held = jnp.stack([total] + shifts(lambda step: total, "z", 4))
-    half = jnp.concatenate([lax.dynamic_index_in_dim(held, (place - b) % 4, 0, keepdims=False) for b in range(4)], axis=0)
+def after(value, *others):
+    return lax.optimization_barrier((value, *others))[0]
+
+
+FAR_ORDER = (0, 2, 4, 6, 5, 7, 3, 1)
+
+
+def per_device(q, k, v, g, home_lengths, moved_lengths, moved_offsets, moved_owner, owner_offsets, layer_grad):
+    core, z, yhi, me = lax.axis_index("core"), lax.axis_index("z"), lax.axis_index("yhi"), lax.axis_index(DP)
+    apart = moved_owner ^ me
+    goal = jnp.where(apart < NFAR, moved_owner & (NFAR - 1), apart)
+    table = jnp.concatenate([moved_lengths, moved_offsets, goal, owner_offsets], axis=0)
+
+    grad = layer_grad.reshape(8, 2, 256, layer_grad.shape[-1])
+    other = lax.dynamic_index_in_dim(grad, 1 - core, 1, keepdims=False)
+    mine = lax.dynamic_index_in_dim(grad, core, 1, keepdims=False)
+    table, other = lax.optimization_barrier((table, other))
+    near, *far = send(table, q, k, v, g)
+    part = add(mine, swap(other, "core", 2, 1)).astype(BF).reshape(2, 4, 4, 64, -1)
+    near = lax.all_to_all(near, ("z", "core"), split_axis=0, concat_axis=0, tiled=True)
+    part_x = reduce_ring(part, "x", 1)
+    outs = home(home_lengths, q, k, v, g)
+    part_x, *outs = lax.optimization_barrier((part_x, *outs))
+    needs = {3: (part,), 5: tuple(outs), 6: (part_x,)}
+    for place, m in enumerate(FAR_ORDER):
+        need = needs.get(place, ())
+        if place >= 3:
+            need = (far[FAR_ORDER[place - 3]], *need)
+        payload = after(far[m], *need) if need else far[m]
+        far[m] = lax.ppermute(payload, DP, [(i, i ^ (NFAR + m)) for i in range(NSLOT)])
+
+    def z_block(step):
+        return lax.dynamic_index_in_dim(part_x, (z + step) % 4, 1, keepdims=False)
+
+    from_z = shifts(z_block, "z", 4)
+    part_z = add(z_block(0), *from_z).astype(BF)
+    kept = lax.dynamic_index_in_dim(part_z, yhi, 0, keepdims=False)
+    given = lax.dynamic_index_in_dim(part_z, 1 - yhi, 0, keepdims=False)
+    from_y = [lax.ppermute(given if mask & 1 else kept, ("ylo", "yhi"), [(i, i ^ mask) for i in range(4)]) for mask in (1, 2, 3)]
+    total = add(kept, *from_y).astype(BF)
+    held = [total, *shifts(lambda step: total, "z", 4)]
+
+    meta = jnp.concatenate([near[:, KVROWS * KV, :], jnp.stack([f[KVROWS * KV, :] for f in far])], axis=0)
+    sources, landings = placement(codes_of(meta))
+    outs = receive(sources, landings, near, far, outs)
+    held, outs = lax.optimization_barrier((held, outs))
+
+    held = jnp.stack(held)
+    half = jnp.concatenate([lax.dynamic_index_in_dim(held, (z - b) % 4, 0, keepdims=False) for b in range(4)], axis=0)
     twin = swap(half, "core", 2, 1)
-    core = lax.axis_index("core")
     first = jnp.where(core == 0, half, twin)
     second = jnp.where(core == 0, twin, half)
-    return jnp.concatenate([first, second], axis=0).astype(F32)
-
-
-def exchange(slots):
-    return lax.all_to_all(slots, DP, split_axis=0, concat_axis=0, tiled=True)
-
-
-def per_device(q, k, v, g, home_lengths, moved_lengths, moved_offsets, moved_owner, owner_offsets, layer_grad):
-    table = jnp.concatenate([moved_lengths, moved_offsets, moved_owner, owner_offsets], axis=0)
-    received = exchange(send(table, q, k, v, g))
-    part = reduce_cores(layer_grad)
-    part = reduce_ring(part, "x", 1)
-    outs = home(home_lengths, q, k, v, g)
-    part, outs = lax.optimization_barrier((part, outs))
-    part = reduce_ring(part, "z", 1)
-    part, received = lax.optimization_barrier((part, received))
-    yhi = lax.axis_index("yhi")
-    mine = lax.dynamic_index_in_dim(part, yhi, 0, keepdims=False)
-    theirs = swap(lax.dynamic_index_in_dim(part, 1 - yhi, 0, keepdims=False), "yhi", 2, 1)
-    sources, landings = placement(codes_of(received[:, KVROWS * KV, :]))
-    outs = receive(sources, landings, received, outs)
-    theirs, outs = lax.optimization_barrier((theirs, outs))
-    total = add(mine, theirs).astype(BF)
-    total = add(total, swap(total, "ylo", 2, 1)).astype(BF)
-    return (*outs, spread(total))
+    return (*outs, jnp.concatenate([first, second], axis=0).astype(F32))
 
 
 def solution(mesh):

time: 155 us -> 132 us (0.85)
  waiting for transfers between devices: 67.3 us -> 31.6 us
  starting transfers between devices: 34.1 us -> 49.5 us
  Pallas kernels: 38.5 us -> 26.4 us
  local copies, waits for them, and re-layouts: 5.52 us -> 13.4 us
    ppermute x9, waiting for transfers between devices: 50.3 us -> 13.5 us  [shifts(): lax.ppermute(pieces(step), axis, [(i, (i + step) % size) for i in range(s...]
    ppermute x0 -> x11, starting transfers between devices: none -> 31.4 us  [the longest x8 21.5 us: per_device(): lax.ppermute(payload, DP, [(i, i ^ NFAR + m) for i in range(NSLOT)])]
    ppermute x0 -> x11, waiting for transfers between devices: none -> 16.8 us  [the longest x8 11.8 us: per_device(): lax.ppermute(payload, DP, [(i, i ^ NFAR + m) for i in range(NSLOT)])]
    ppermute x9, starting transfers between devices: 20.7 us -> 10.2 us  [shifts(): lax.ppermute(pieces(step), axis, [(i, (i + step) % size) for i in range(s...]
    all_to_all x1, waiting for transfers between devices: 8.47 us -> 0.01 us  [per_device(): lax.all_to_all(near, ('z', 'core'), split_axis=0, concat_axis=0, tiled=True)]
    pallas_call x1, Pallas kernels: 16.4 us -> 8.54 us  [send(): pl.pallas_call(send_kernel, out_shape=[jax.ShapeDtypeStruct((NFAR, KVROWS...]
    ppermute x4 -> x2, waiting for transfers between devices: 8.61 us -> 1.16 us  [swap(): return lax.ppermute(x, axis, [(i, i ^ mask) for i in range(size)])]
    slice x0 -> x9, local copies, waits for them, and re-layouts: none -> 5.28 us  [the longest x8 5.27 us: per_device(): f[KVROWS * KV, :]]
  transfers between devices with their start and end apart: 14 -> 23, of which waited for: 10 -> 7; matrix products, arithmetic and copies ran while one was open for 6% -> 12% of each run, Pallas kernels for 14% -> 14%
where the time goes in v3:
time: 132 us; the launch traced here: 131 us
  starting transfers between devices  49.5 us (38%)
  waiting for transfers between devices  31.6 us (24%)
  Pallas kernels  26.4 us (20%)
  local copies, waits for them, and re-layouts  13.4 us (10%)
  other arithmetic  9.37 us (7%)
    ppermute x8, starting transfers between devices, per_device(): lax.ppermute(payload, DP, [(i, i ^ NFAR + m) for i in range(NSLOT)])  21.5 us
    ppermute x9, waiting for transfers between devices, shifts(): lax.ppermute(pieces(step), axis, [(i, (i + step) % size) for i in range(s...  13.5 us
    ppermute x8, waiting for transfers between devices, per_device(): lax.ppermute(payload, DP, [(i, i ^ NFAR + m) for i in range(NSLOT)])  11.8 us
    ppermute x9, starting transfers between devices, shifts(): lax.ppermute(pieces(step), axis, [(i, (i + step) % size) for i in range(s...  10.2 us
    pallas_call x1, Pallas kernels, home(): pl.pallas_call(home_kernel, out_shape=[jax.ShapeDtypeStruct((total, KV *...  10.1 us
    ppermute x3, starting transfers between devices, per_device(): lax.ppermute(given if mask & 1 else kept, ('ylo', 'yhi'), [(i, i ^ mask)...  9.93 us
    pallas_call x1, Pallas kernels, send(): pl.pallas_call(send_kernel, out_shape=[jax.ShapeDtypeStruct((NFAR, KVROWS...  8.54 us
    pallas_call x1, Pallas kernels, receive(): pl.pallas_call(receive_kernel, out_shape=[jax.ShapeDtypeStruct(o.shape, o...  7.76 us
  transfers between devices with their start and end apart: 23, of which 7 were waited for; matrix products, arithmetic and copies ran while one was open for 12% of the time, Pallas kernels for 14%

profile of v3, /device:TPU:1, one launch (start us, length us, event | category | flops | bytes accessed | tf_op | source)
XLA Modules:
  0.0 131.1 jit_solution(11372513965022776578)
XLA Ops:
  1.3 3.0 %dynamic-slice_bitcast_fusion = bf16[8,256,512]{2,1,0:T(8,128)(2,1)} fusion(bf16[8,2,256,512]{3,2,1,0:T(8,128)(2,1)} %bitcast.50, s32[]{:T(128)S(6)} %select_n.125), kind=kLoop, calls=%fused_computation.2 | loop fusion | bytes 4194308 | tf_op jit(solution)/shard_map/jit(dynamic_index_in_dim)/squeeze | solution.py:414
  5.0 1.4 %collective-permute-start = (bf16[8,256,512]{2,1,0:T(8,128)(2,1)}, bf16[8,256,512]{2,1,0:T(8,128)(2,1)}, u32[]{:S(2)}, u32[]{:S(2)}) collective-permute-start(bf16[8,256,512]{2,1,0:T(8,128)(2,1)} %dynamic-slice_bitcast_fusion), channel_id=1, source_target_pairs={{0,8},{8,0},{1,9},{9,1},{2,10},{10,2},{3,11},{11,3},{4,12},{12,4},... | collective-permute-start | bytes 6291464 | tf_op jit(solution)/shard_map/ppermute | solution.py:369
  6.4 8.5 %send.1 = (bf16[8,1544,128]{2,1,0:T(8,128)(2,1)}, bf16[1544,128]{1,0:T(8,128)(2,1)}, bf16[1544,128]{1,0:T(8,128)(2,1)}, bf16[1544,128]{1,0:T(8,128)(2,1)}, bf16[...) custom-call(s32[4,8]{1,0:T(4,128)} %pad_add_fusion.table, ...), custom_call_target="tpu_custom_call" | custom-call | flops 4000000000 | bytes 10000000 | tf_op jit(solution)/shard_map/send/pallas_call | solution.py:152
  15.0 5.5 %all-to-all-start = ((bf16[8,1544,128]{2,1,0:T(8,128)(2,1)}), bf16[8,1544,128]{2,1,0:T(8,128)(2,1)S(1)}, u32[]{:S(2)}, u32[]{:S(2)}) async-start(bf16[8,1544,128]{2,1,0:T(8,128)(2,1)} %get-tuple-element.49), calls=%async_computation | async-start | bytes 6324224 | tf_op jit(solution)/shard_map/all_to_all | solution.py:419
  20.5 1.3 collective-permute-start.13
  21.8 1.3 collective-permute-start.14
  23.0 2.9 %fusion = bf16[8,256,512]{2,1,0:T(8,128)(2,1)S(1)} fusion(bf16[8,256,512]{2,1,0:T(8,128)(2,1)} %collective-permute-done, bf16[8,2,256,512]{3,2,1,0:T(8,128)(2,1)} %bitcast.51, s32[]{:T(128)S(6)} %select_n.123), kind=kLoop, calls=%fused_computation.1 | loop fusion | flops 4194304 | bytes 6291460 | tf_op jit(solution)/shard_map/convert_element_type | solution.py:418
  25.9 1.0 constant_dynamic-slice_fusion.3
  27.7 2.5 %collective-permute-start.3 = (bf16[2,4,64,512]{3,2,0,1:T(8,128)(2,1)}, bf16[2,4,64,512]{3,2,0,1:T(8,128)(2,1)}, u32[]{:S(2)}, u32[]{:S(2)}) collective-permute-start(bf16[2,4,64,512]{3,2,0,1:T(8,128)(2,1)} %bitcast.45), channel_id=1, source_target_pairs={{0,3},{1,0},{2,1},{3,2},{4,7},{5,4},{6,5},{7,6},{8,11},{9,8},{10,9... | collective-permute-start | bytes 1572872 | tf_op jit(solution)/shard_map/ppermute | solution.py:380
  30.2 0.8 copy.41
  33.0 10.1 %home.1 = (bf16[896,2048]{1,0:T(8,128)(2,1)}, bf16[896,2048]{1,0:T(8,128)(2,1)}, bf16[896,512]{1,0:T(8,128)(2,1)}, bf16[896,512]{1,0:T(8,128)(2,1)}) custom-call(s32[1,6]{1,0:T(1,128)} %lengths.1, bf16[896,2048]{1,0:T(8,128)(2,1)} %q_hbm.1, bf16[896,512]{1,0:T(8,128)(2,1)} %k_hbm.1, bf16[896,512]{1,0:T(8,128)(2,1)} %v_hbm.1, bf16[896,2048]{1,0:T(8,128)(2,1)} %g_hbm.1), custom_call_target="tpu_custom_call" | custom-call | flops 10000000000 | bytes 10000000 | tf_op jit(solution)/shard_map/home/pallas_call | solution.py:216
  43.1 3.5 %collective-permute-start.19 = (bf16[1544,128]{1,0:T(8,128)(2,1)}, bf16[1544,128]{1,0:T(8,128)(2,1)}, u32[]{:S(2)}, u32[]{:S(2)}) collective-permute-start(bf16[1544,128]{1,0:T(8,128)(2,1)} %get-tuple-element.60), channel_id=1, source_target_pairs={{0,96},{8,104},{16,112},{24,120},{32,64},{40,72},{48,80},{56,88},{... | collective-permute-start | bytes 1185800 | tf_op jit(solution)/shard_map/ppermute | solution.py:429
  46.6 2.4 %collective-permute-start.15 = (bf16[1544,128]{1,0:T(8,128)(2,1)}, bf16[1544,128]{1,0:T(8,128)(2,1)}, u32[]{:S(2)}, u32[]{:S(2)}) collective-permute-start(bf16[1544,128]{1,0:T(8,128)(2,1)} %get-tuple-element.54), channel_id=1, source_target_pairs={{0,104},{8,96},{16,120},{24,112},{32,72},{40,64},{48,88},{56,80},{... | collective-permute-start | bytes 1185800 | tf_op jit(solution)/shard_map/ppermute | solution.py:429
  49.0 2.8 %collective-permute-start.17 = (bf16[1544,128]{1,0:T(8,128)(2,1)}, bf16[1544,128]{1,0:T(8,128)(2,1)}, u32[]{:S(2)}, u32[]{:S(2)}) collective-permute-start(bf16[1544,128]{1,0:T(8,128)(2,1)} %get-tuple-element.58), channel_id=1, source_target_pairs={{0,112},{8,120},{16,96},{24,104},{32,80},{40,88},{48,64},{56,72},{... | collective-permute-start | bytes 1185800 | tf_op jit(solution)/shard_map/ppermute | solution.py:429
  51.8 6.1 %collective-permute-done.1 = bf16[2,4,64,512]{3,2,0,1:T(8,128)(2,1)} collective-permute-done((bf16[2,4,64,512]{3,2,0,1:T(8,128)(2,1)}, bf16[2,4,64,512]{3,2,0,1:T(8,128)(2,1)}, u32[]{:S(2)}, u32[]{:S(2)}) %collective-permute-start.1) | collective-permute-done | bytes 524320 | tf_op jit(solution)/shard_map/ppermute | solution.py:380
  57.9 1.8 %fusion.3 = bf16[2,4,64,512]{3,2,0,1:T(8,128)(2,1)S(1)} fusion(bf16[2,4,64,512]{3,2,0,1:T(8,128)(2,1)} %collective-permute-done.3, bf16[2,4,64,512]{3,2,0,1:T(8,128)(2,1)} %collective-permute-done.2, bf16[2,4,64,512]{3,2,0,1:T(8,128)(2,1)} %collective-permute-done.1, bf16[2,1,4,64,512]{4,3,2,1,0:T(8,128)(2,1)} %get-tuple-element.81), kind=kLoop, calls=%fused_computation.6 | loop fusion | flops 2097152 | bytes 2621440 | tf_op jit(solution)/shard_map/convert_element_type | solution.py:397
  61.2 1.8 %collective-permute-start.6 = (bf16[2,64,512]{2,1,0:T(8,128)(2,1)}, bf16[2,64,512]{2,1,0:T(8,128)(2,1)S(1)}, u32[]{:S(2)}, u32[]{:S(2)}) collective-permute-start(bf16[2,64,512]{2,1,0:T(8,128)(2,1)} %get-tuple-element.88), channel_id=1, source_target_pairs={{0,48},{16,0},{32,16},{48,32},{1,49},{17,1},{33,17},{49,33},{2,50}... | collective-permute-start | bytes 393224 | tf_op jit(solution)/shard_map/ppermute | solution.py:380
  63.6 4.5 %collective-permute-done.15.refs_5_ = bf16[1544,128]{1,0:T(8,128)(2,1)} collective-permute-done((bf16[1544,128]{1,0:T(8,128)(2,1)}, bf16[1544,128]{1,0:T(8,128)(2,1)}, u32[]{:S(2)}, u32[]{:S(2)}) %collective-permute-start.15) | collective-permute-done | bytes 395296 | tf_op jit(solution)/shard_map/ppermute | solution.py:429
  68.1 7.4 %collective-permute-done.17.refs_6_ = bf16[1544,128]{1,0:T(8,128)(2,1)} collective-permute-done((bf16[1544,128]{1,0:T(8,128)(2,1)}, bf16[1544,128]{1,0:T(8,128)(2,1)}, u32[]{:S(2)}, u32[]{:S(2)}) %collective-permute-start.17) | collective-permute-done | bytes 395296 | tf_op jit(solution)/shard_map/ppermute | solution.py:429
  75.5 5.8 %collective-permute-start.16 = (bf16[1544,128]{1,0:T(8,128)(2,1)}, bf16[1544,128]{1,0:T(8,128)(2,1)}, u32[]{:S(2)}, u32[]{:S(2)}) collective-permute-start(bf16[1544,128]{1,0:T(8,128)(2,1)} %get-tuple-element.55), channel_id=1, source_target_pairs={{0,72},{8,64},{16,88},{24,80},{32,104},{40,96},{48,120},{56,112},{... | collective-permute-start | bytes 1185800 | tf_op jit(solution)/shard_map/ppermute | solution.py:429
  81.3 7.4 %collective-permute-done.6 = bf16[2,64,512]{2,1,0:T(8,128)(2,1)S(1)} collective-permute-done((bf16[2,64,512]{2,1,0:T(8,128)(2,1)}, bf16[2,64,512]{2,1,0:T(8,128)(2,1)S(1)}, u32[]{:S(2)}, u32[]{:S(2)}) %collective-permute-start.6) | collective-permute-done | bytes 131104 | tf_op jit(solution)/shard_map/ppermute | solution.py:380
  88.7 4.4 %collective-permute-start.20 = (bf16[1544,128]{1,0:T(8,128)(2,1)}, bf16[1544,128]{1,0:T(8,128)(2,1)}, u32[]{:S(2)}, u32[]{:S(2)}) collective-permute-start(bf16[1544,128]{1,0:T(8,128)(2,1)} %get-tuple-element.66), channel_id=1, source_target_pairs={{0,120},{8,112},{16,104},{24,96},{32,88},{40,80},{48,72},{56,64},{... | collective-permute-start | bytes 1185800 | tf_op jit(solution)/shard_map/ppermute | solution.py:429
  93.1 1.1 fusion.6
  94.2 8.7 %collective-permute-start.9 = (bf16[64,512]{1,0:T(8,128)(2,1)S(1)}, bf16[64,512]{1,0:T(8,128)(2,1)S(1)}, u32[]{:S(2)}, u32[]{:S(2)}) collective-permute-start(bf16[64,512]{1,0:T(8,128)(2,1)S(1)} %get-tuple-element.95), channel_id=1, source_target_pairs={{0,68},{4,64},{64,4},{68,0},{1,69},{5,65},{65,5},{69,1},{2,70},{6,... | collective-permute-start | bytes 196616 | tf_op jit(solution)/shard_map/ppermute | solution.py:438
  102.9 1.3 collective-permute-start.7
  108.2 1.9 %collective-permute-done.8 = bf16[64,512]{1,0:T(8,128)(2,1)S(1)} collective-permute-done((bf16[64,512]{1,0:T(8,128)(2,1)S(1)}, bf16[64,512]{1,0:T(8,128)(2,1)S(1)}, u32[]{:S(2)}, u32[]{:S(2)}) %collective-permute-start.8) | collective-permute-done | bytes 65568 | tf_op jit(solution)/shard_map/ppermute | solution.py:438
  110.1 3.1 %collective-permute-done.7 = bf16[64,512]{1,0:T(8,128)(2,1)S(1)} collective-permute-done((bf16[64,512]{1,0:T(8,128)(2,1)S(1)}, bf16[64,512]{1,0:T(8,128)(2,1)S(1)}, u32[]{:S(2)}, u32[]{:S(2)}) %collective-permute-start.7) | collective-permute-done | bytes 65568 | tf_op jit(solution)/shard_map/ppermute | solution.py:438
  113.3 3.4 %collective-permute-start.11 = (bf16[64,512]{1,0:T(8,128)(2,1)S(1)}, bf16[64,512]{1,0:T(8,128)(2,1)S(1)}, u32[]{:S(2)}, u32[]{:S(2)}) collective-permute-start(bf16[64,512]{1,0:T(8,128)(2,1)S(1)} %add_convert_fusion), channel_id=1, source_target_pairs={{0,32},{16,48},{32,0},{48,16},{1,33},{17,49},{33,1},{49,17},{2,34}... | collective-permute-start | bytes 196616 | tf_op jit(solution)/shard_map/ppermute | solution.py:380
  119.9 7.8 %receive.1 = (bf16[896,2048]{1,0:T(8,128)(2,1)}, bf16[896,2048]{1,0:T(8,128)(2,1)}, bf16[896,512]{1,0:T(8,128)(2,1)}, bf16[896,512]{1,0:T(8,128)(2,1)}) custom-call(s32[8]{0:T(128)} %get-tuple-element.80.sources, s32[8]{0:T(128)} %get-tuple-element.79.landings, ...), custom_call_target="tpu_custom_call", output_to_operand_aliasing={{0}: (11, {}), {1}: (12, {}), {2}: (13, {}), {3}: (14, {})} | custom-call | flops 4000000000 | bytes 10000000 | tf_op jit(solution)/shard_map/receive/pallas_call | solution.py:329
  127.8 1.0 collective-permute-start.21
  128.8 1.2 collective-permute-done.21
  130.0 1.1 maximum_convert_fusion
  (62 shorter events, 13.6 us)
Async XLA Ops:
  0.6 3.8 %copy-start.2 = (s32[1,8]{1,0:T(1,128)S(1)}, s32[1,8]{1,0:T(1,128)}, u32[]{:S(2)}) copy-start(s32[1,8]{1,0:T(1,128)} %param.18) | copy-start | bytes 100
  0.6 3.7 %copy-start.3 = (s32[1,8]{1,0:T(1,128)S(1)}, s32[1,8]{1,0:T(1,128)}, u32[]{:S(2)}) copy-start(s32[1,8]{1,0:T(1,128)} %param.16) | copy-start | bytes 100
  0.7 3.7 %copy-start.4 = (s32[1,8]{1,0:T(1,128)S(1)}, s32[1,8]{1,0:T(1,128)}, u32[]{:S(2)}) copy-start(s32[1,8]{1,0:T(1,128)} %param.15) | copy-start | bytes 100
  5.0 18.1 %collective-permute-start = (bf16[8,256,512]{2,1,0:T(8,128)(2,1)}, bf16[8,256,512]{2,1,0:T(8,128)(2,1)}, u32[]{:S(2)}, u32[]{:S(2)}) collective-permute-start(bf16[8,256,512]{2,1,0:T(8,128)(2,1)} %dynamic-slice_bitcast_fusion), channel_id=1, source_target_pairs={{0,8},{8,0},{1,9},{9,1},{2,10},{10,2},{3,11},{11,3},{4,12},{12,4},... | collective-permute-start | bytes 6291464 | tf_op jit(solution)/shard_map/ppermute | solution.py:369
  15.0 93.2 %all-to-all-start = ((bf16[8,1544,128]{2,1,0:T(8,128)(2,1)}), bf16[8,1544,128]{2,1,0:T(8,128)(2,1)S(1)}, u32[]{:S(2)}, u32[]{:S(2)}) async-start(bf16[8,1544,128]{2,1,0:T(8,128)(2,1)} %get-tuple-element.49), calls=%async_computation | async-start | bytes 6324224 | tf_op jit(solution)/shard_map/all_to_all | solution.py:419
  20.5 26.1 %collective-permute-start.13 = (bf16[1544,128]{1,0:T(8,128)(2,1)}, bf16[1544,128]{1,0:T(8,128)(2,1)}, u32[]{:S(2)}, u32[]{:S(2)}) collective-permute-start(bf16[1544,128]{1,0:T(8,128)(2,1)} %get-tuple-element.50), channel_id=1, source_target_pairs={{0,64},{8,72},{16,80},{24,88},{32,96},{40,104},{48,112},{56,120},{... | collective-permute-start | bytes 1185800 | tf_op jit(solution)/shard_map/ppermute | solution.py:429
  21.8 21.3 %collective-permute-start.14 = (bf16[1544,128]{1,0:T(8,128)(2,1)}, bf16[1544,128]{1,0:T(8,128)(2,1)}, u32[]{:S(2)}, u32[]{:S(2)}) collective-permute-start(bf16[1544,128]{1,0:T(8,128)(2,1)} %get-tuple-element.53), channel_id=1, source_target_pairs={{0,80},{8,88},{16,64},{24,72},{32,112},{40,120},{48,96},{56,104},{... | collective-permute-start | bytes 1185800 | tf_op jit(solution)/shard_map/ppermute | solution.py:429
  27.7 21.3 %collective-permute-start.3 = (bf16[2,4,64,512]{3,2,0,1:T(8,128)(2,1)}, bf16[2,4,64,512]{3,2,0,1:T(8,128)(2,1)}, u32[]{:S(2)}, u32[]{:S(2)}) collective-permute-start(bf16[2,4,64,512]{3,2,0,1:T(8,128)(2,1)} %bitcast.45), channel_id=1, source_target_pairs={{0,3},{1,0},{2,1},{3,2},{4,7},{5,4},{6,5},{7,6},{8,11},{9,8},{10,9... | collective-permute-start | bytes 1572872 | tf_op jit(solution)/shard_map/ppermute | solution.py:380
  31.0 20.8 %collective-permute-start.2 = (bf16[2,4,64,512]{3,2,0,1:T(8,128)(2,1)}, bf16[2,4,64,512]{3,2,0,1:T(8,128)(2,1)}, u32[]{:S(2)}, u32[]{:S(2)}) collective-permute-start(bf16[2,4,64,512]{3,2,0,1:T(8,128)(2,1)} %bitcast.46), channel_id=1, source_target_pairs={{0,2},{1,3},{2,0},{3,1},{4,6},{5,7},{6,4},{7,5},{8,10},{9,11},{10,... | collective-permute-start | bytes 1572872 | tf_op jit(solution)/shard_map/ppermute | solution.py:380
  32.4 25.5 %collective-permute-start.1 = (bf16[2,4,64,512]{3,2,0,1:T(8,128)(2,1)}, bf16[2,4,64,512]{3,2,0,1:T(8,128)(2,1)}, u32[]{:S(2)}, u32[]{:S(2)}) collective-permute-start(bf16[2,4,64,512]{3,2,0,1:T(8,128)(2,1)} %bitcast.47), channel_id=1, source_target_pairs={{0,1},{1,2},{2,3},{3,0},{4,5},{5,6},{6,7},{7,4},{8,9},{9,10},{10,1... | collective-permute-start | bytes 1572872 | tf_op jit(solution)/shard_map/ppermute | solution.py:380
  43.1 38.2 %collective-permute-start.19 = (bf16[1544,128]{1,0:T(8,128)(2,1)}, bf16[1544,128]{1,0:T(8,128)(2,1)}, u32[]{:S(2)}, u32[]{:S(2)}) collective-permute-start(bf16[1544,128]{1,0:T(8,128)(2,1)} %get-tuple-element.60), channel_id=1, source_target_pairs={{0,96},{8,104},{16,112},{24,120},{32,64},{40,72},{48,80},{56,88},{... | collective-permute-start | bytes 1185800 | tf_op jit(solution)/shard_map/ppermute | solution.py:429
  46.6 21.5 %collective-permute-start.15 = (bf16[1544,128]{1,0:T(8,128)(2,1)}, bf16[1544,128]{1,0:T(8,128)(2,1)}, u32[]{:S(2)}, u32[]{:S(2)}) collective-permute-start(bf16[1544,128]{1,0:T(8,128)(2,1)} %get-tuple-element.54), channel_id=1, source_target_pairs={{0,104},{8,96},{16,120},{24,112},{32,72},{40,64},{48,88},{56,80},{... | collective-permute-start | bytes 1185800 | tf_op jit(solution)/shard_map/ppermute | solution.py:429
  49.0 26.5 %collective-permute-start.17 = (bf16[1544,128]{1,0:T(8,128)(2,1)}, bf16[1544,128]{1,0:T(8,128)(2,1)}, u32[]{:S(2)}, u32[]{:S(2)}) collective-permute-start(bf16[1544,128]{1,0:T(8,128)(2,1)} %get-tuple-element.58), channel_id=1, source_target_pairs={{0,112},{8,120},{16,96},{24,104},{32,80},{40,88},{48,64},{56,72},{... | collective-permute-start | bytes 1185800 | tf_op jit(solution)/shard_map/ppermute | solution.py:429
  59.8 0.8 copy-start.1
  61.2 27.5 %collective-permute-start.6 = (bf16[2,64,512]{2,1,0:T(8,128)(2,1)}, bf16[2,64,512]{2,1,0:T(8,128)(2,1)S(1)}, u32[]{:S(2)}, u32[]{:S(2)}) collective-permute-start(bf16[2,64,512]{2,1,0:T(8,128)(2,1)} %get-tuple-element.88), channel_id=1, source_target_pairs={{0,48},{16,0},{32,16},{48,32},{1,49},{17,1},{33,17},{49,33},{2,50}... | collective-permute-start | bytes 393224 | tf_op jit(solution)/shard_map/ppermute | solution.py:380
  63.0 30.1 %collective-permute-start.5 = (bf16[2,64,512]{2,1,0:T(8,128)(2,1)S(1)}, bf16[2,64,512]{2,1,0:T(8,128)(2,1)}, u32[]{:S(2)}, u32[]{:S(2)}) collective-permute-start(bf16[2,64,512]{2,1,0:T(8,128)(2,1)S(1)} %get-tuple-element.89), channel_id=1, source_target_pairs={{0,32},{16,48},{32,0},{48,16},{1,33},{17,49},{33,1},{49,17},{2,34}... | collective-permute-start | bytes 393224 | tf_op jit(solution)/shard_map/ppermute | solution.py:380
  68.1 25.0 %collective-permute-start.4 = (bf16[2,64,512]{2,1,0:T(8,128)(2,1)S(1)}, bf16[2,64,512]{2,1,0:T(8,128)(2,1)}, u32[]{:S(2)}, u32[]{:S(2)}) collective-permute-start(bf16[2,64,512]{2,1,0:T(8,128)(2,1)S(1)} %get-tuple-element.87), channel_id=1, source_target_pairs={{0,16},{16,32},{32,48},{48,0},{1,17},{17,33},{33,49},{49,1},{2,18}... | collective-permute-start | bytes 393224 | tf_op jit(solution)/shard_map/ppermute | solution.py:380
  75.5 27.4 %collective-permute-start.16 = (bf16[1544,128]{1,0:T(8,128)(2,1)}, bf16[1544,128]{1,0:T(8,128)(2,1)}, u32[]{:S(2)}, u32[]{:S(2)}) collective-permute-start(bf16[1544,128]{1,0:T(8,128)(2,1)} %get-tuple-element.55), channel_id=1, source_target_pairs={{0,72},{8,64},{16,88},{24,80},{32,104},{40,96},{48,120},{56,112},{... | collective-permute-start | bytes 1185800 | tf_op jit(solution)/shard_map/ppermute | solution.py:429
  81.3 36.2 %collective-permute-start.18 = (bf16[1544,128]{1,0:T(8,128)(2,1)}, bf16[1544,128]{1,0:T(8,128)(2,1)}, u32[]{:S(2)}, u32[]{:S(2)}) collective-permute-start(bf16[1544,128]{1,0:T(8,128)(2,1)} %get-tuple-element.59), channel_id=1, source_target_pairs={{0,88},{8,80},{16,72},{24,64},{32,120},{40,112},{48,104},{56,96},{... | collective-permute-start | bytes 1185800 | tf_op jit(solution)/shard_map/ppermute | solution.py:429
  88.7 29.5 %collective-permute-start.20 = (bf16[1544,128]{1,0:T(8,128)(2,1)}, bf16[1544,128]{1,0:T(8,128)(2,1)}, u32[]{:S(2)}, u32[]{:S(2)}) collective-permute-start(bf16[1544,128]{1,0:T(8,128)(2,1)} %get-tuple-element.66), channel_id=1, source_target_pairs={{0,120},{8,112},{16,104},{24,96},{32,88},{40,80},{48,72},{56,64},{... | collective-permute-start | bytes 1185800 | tf_op jit(solution)/shard_map/ppermute | solution.py:429
  94.2 14.0 %collective-permute-start.9 = (bf16[64,512]{1,0:T(8,128)(2,1)S(1)}, bf16[64,512]{1,0:T(8,128)(2,1)S(1)}, u32[]{:S(2)}, u32[]{:S(2)}) collective-permute-start(bf16[64,512]{1,0:T(8,128)(2,1)S(1)} %get-tuple-element.95), channel_id=1, source_target_pairs={{0,68},{4,64},{64,4},{68,0},{1,69},{5,65},{65,5},{69,1},{2,70},{6,... | collective-permute-start | bytes 196616 | tf_op jit(solution)/shard_map/ppermute | solution.py:438
  102.9 7.2 %collective-permute-start.8 = (bf16[64,512]{1,0:T(8,128)(2,1)S(1)}, bf16[64,512]{1,0:T(8,128)(2,1)S(1)}, u32[]{:S(2)}, u32[]{:S(2)}) collective-permute-start(bf16[64,512]{1,0:T(8,128)(2,1)S(1)} %get-tuple-element.94), channel_id=1, source_target_pairs={{0,64},{4,68},{64,0},{68,4},{1,65},{5,69},{65,1},{69,5},{2,66},{6,... | collective-permute-start | bytes 196616 | tf_op jit(solution)/shard_map/ppermute | solution.py:438
  102.9 10.3 %collective-permute-start.7 = (bf16[64,512]{1,0:T(8,128)(2,1)S(1)}, bf16[64,512]{1,0:T(8,128)(2,1)S(1)}, u32[]{:S(2)}, u32[]{:S(2)}) collective-permute-start(bf16[64,512]{1,0:T(8,128)(2,1)S(1)} %get-tuple-element.95), channel_id=1, source_target_pairs={{0,4},{4,0},{64,68},{68,64},{1,5},{5,1},{65,69},{69,65},{2,6},{6,2... | collective-permute-start | bytes 196616 | tf_op jit(solution)/shard_map/ppermute | solution.py:438
  108.2 11.7 %copy-start = (bf16[8,1544,128]{2,1,0:T(8,128)(2,1)}, bf16[8,1544,128]{2,1,0:T(8,128)(2,1)S(1)}, u32[]{:S(2)}) copy-start(bf16[8,1544,128]{2,1,0:T(8,128)(2,1)S(1)} %all-to-all-done.near) | copy-start | bytes 9486340
  113.3 14.4 %collective-permute-start.10 = (bf16[64,512]{1,0:T(8,128)(2,1)S(1)}, bf16[64,512]{1,0:T(8,128)(2,1)S(1)}, u32[]{:S(2)}, u32[]{:S(2)}) collective-permute-start(bf16[64,512]{1,0:T(8,128)(2,1)S(1)} %add_convert_fusion), channel_id=1, source_target_pairs={{0,16},{16,32},{32,48},{48,0},{1,17},{17,33},{33,49},{49,1},{2,18}... | collective-permute-start | bytes 196616 | tf_op jit(solution)/shard_map/ppermute | solution.py:380
  113.3 14.3 %collective-permute-start.11 = (bf16[64,512]{1,0:T(8,128)(2,1)S(1)}, bf16[64,512]{1,0:T(8,128)(2,1)S(1)}, u32[]{:S(2)}, u32[]{:S(2)}) collective-permute-start(bf16[64,512]{1,0:T(8,128)(2,1)S(1)} %add_convert_fusion), channel_id=1, source_target_pairs={{0,32},{16,48},{32,0},{48,16},{1,33},{17,49},{33,1},{49,17},{2,34}... | collective-permute-start | bytes 196616 | tf_op jit(solution)/shard_map/ppermute | solution.py:380
  116.8 10.9 %collective-permute-start.12 = (bf16[64,512]{1,0:T(8,128)(2,1)S(1)}, bf16[64,512]{1,0:T(8,128)(2,1)S(1)}, u32[]{:S(2)}, u32[]{:S(2)}) collective-permute-start(bf16[64,512]{1,0:T(8,128)(2,1)S(1)} %add_convert_fusion), channel_id=1, source_target_pairs={{0,48},{16,0},{32,16},{48,32},{1,49},{17,1},{33,17},{49,33},{2,50}... | collective-permute-start | bytes 196616 | tf_op jit(solution)/shard_map/ppermute | solution.py:380
  127.8 2.1 %collective-permute-start.21 = (bf16[256,512]{1,0:T(8,128)(2,1)S(1)}, bf16[256,512]{1,0:T(8,128)(2,1)S(1)}, u32[]{:S(2)}, u32[]{:S(2)}) collective-permute-start(bf16[256,512]{1,0:T(8,128)(2,1)S(1)} %pad_maximum_fusion.1), channel_id=1, source_target_pairs={{0,8},{8,0},{1,9},{9,1},{2,10},{10,2},{3,11},{11,3},{4,12},{12,4},... | collective-permute-start | bytes 786440 | tf_op jit(solution)/shard_map/ppermute | solution.py:369

commit v4 on v3

--- a/solution.py
+++ b/solution.py
@@ -216,10 +216,10 @@
     return pl.pallas_call(
         home_kernel,
         out_shape=[
-            jax.ShapeDtypeStruct((total, KV * GROUP * HD), BF),
-            jax.ShapeDtypeStruct((total, KV * GROUP * HD), BF),
-            jax.ShapeDtypeStruct((total, KV * HD), BF),
-            jax.ShapeDtypeStruct((total, KV * HD), BF),
+            pltpu.HBM((total, KV * GROUP * HD), BF),
+            pltpu.HBM((total, KV * GROUP * HD), BF),
+            pltpu.HBM((total, KV * HD), BF),
+            pltpu.HBM((total, KV * HD), BF),
         ],
         grid=(KV,),
         in_specs=[pl.BlockSpec(memory_space=pltpu.SMEM), wide, narrow, narrow, wide],
@@ -230,38 +230,64 @@
     )(lengths, q, k, v, g)
 
 
-def receive_kernel(sources, landings, near, *refs):
+def receive_kernel(kvs, near, *refs):
     far = refs[:NFAR]
     out, dq, dk, dv = refs[NFAR + 4 : NFAR + 8]
-    slot, o_buf, q_buf, k_buf, v_buf, o_out, q_out, k_out, v_out, in_sem, out_sem = refs[NFAR + 8 :]
-
-    def load(d, n, m=0):
-        rows = pl.ds(KVROWS * n, KVROWS)
-        return pltpu.make_async_copy(far[m].at[rows, :], slot.at[d, rows, :], in_sem.at[d, n])
+    slot, o_buf, q_buf, k_buf, v_buf, o_out, q_out, k_out, v_out, meta, sources, landings, in_sem, out_sem, meta_sem = refs[NFAR + 8 :]
+    tail = pl.ds(KVROWS * KV, META)
+    meta_copies = [pltpu.make_async_copy(near.at[:, tail, :], meta.at[pl.ds(0, NFAR)], meta_sem.at[NFAR])]
+    meta_copies += [pltpu.make_async_copy(far[m].at[tail, :], meta.at[NFAR + m], meta_sem.at[m]) for m in range(NFAR)]
+    for copy in meta_copies:
+        copy.start()
+    for copy in meta_copies:
+        copy.wait()
+    lane = lax.broadcasted_iota(jnp.int32, (META, HD), 1)
+    top = lax.broadcasted_iota(jnp.int32, (META, HD), 0) == 0
+    factor = jnp.where(top & (lane == 0), 32.0, jnp.where(top & (lane == S), 1.0, 0.0))
+    codes = [jnp.sum(meta[s].astype(F32) * factor).astype(jnp.int32) for s in range(NSLOT)]
+    for s in range(NSLOT):
+        rank = jnp.int32(0)
+        for t in range(NSLOT):
+            if t != s:
+                rank = rank + jnp.where((codes[t] > 0) & (codes[t] < codes[s]), 1, 0)
+
+        @pl.when(codes[s] > 0)
+        def _(s=s, rank=rank):
+            sources[rank] = jnp.int32(s)
+            landings[rank] = codes[s] - 1
+
+
+    def load(d, i, m=0):
+        source, rows = pl.ds(KVROWS * kvs[i], KVROWS), pl.ds(KVROWS * i, KVROWS)
+        return pltpu.make_async_copy(far[m].at[source, :], slot.at[d, rows, :], in_sem.at[d, i])
+
+    def load_near(d, i):
+        source, rows = pl.ds(KVROWS * kvs[i], KVROWS), pl.ds(KVROWS * i, KVROWS)
+        return pltpu.make_async_copy(near.at[sources[d] & (NFAR - 1), source, :], slot.at[d, rows, :], in_sem.at[d, i])
 
     for d in range(NDOC):
 
         @pl.when(sources[d] < NFAR)
         def _(d=d):
-            for n in range(KV):
-                rows = pl.ds(KVROWS * n, KVROWS)
-                pltpu.make_async_copy(near.at[sources[d] & (NFAR - 1), rows, :], slot.at[d, rows, :], in_sem.at[d, n]).start()
+            for i in range(len(kvs)):
+                load_near(d, i).start()
 
         for m in range(NFAR):
 
             @pl.when(sources[d] == NFAR + m)
             def _(d=d, m=m):
-                for n in range(KV):
-                    load(d, n, m).start()
-
-
-    def stores(n):
+                for i in range(len(kvs)):
+                    load(d, i, m).start()
+
+
+    def stores(i):
+        n = kvs[i]
         rows, wide, narrow = pl.ds(HOME, MOVE), pl.ds(GROUP * HD * n, GROUP * HD), pl.ds(HD * n, HD)
         return [
-            pltpu.make_async_copy(o_out.at[n % 2], out.at[rows, wide], out_sem.at[0, n % 2]),
-            pltpu.make_async_copy(q_out.at[n % 2], dq.at[rows, wide], out_sem.at[1, n % 2]),
-            pltpu.make_async_copy(k_out.at[n % 2], dk.at[rows, narrow], out_sem.at[2, n % 2]),
-            pltpu.make_async_copy(v_out.at[n % 2], dv.at[rows, narrow], out_sem.at[3, n % 2]),
+            pltpu.make_async_copy(o_out.at[i % 2], out.at[rows, wide], out_sem.at[0, i % 2]),
+            pltpu.make_async_copy(q_out.at[i % 2], dq.at[rows, wide], out_sem.at[1, i % 2]),
+            pltpu.make_async_copy(k_out.at[i % 2], dk.at[rows, narrow], out_sem.at[2, i % 2]),
+            pltpu.make_async_copy(v_out.at[i % 2], dv.at[rows, narrow], out_sem.at[3, i % 2]),
         ]
 
     zeros = jnp.zeros((S, HD), BF)
@@ -285,10 +311,10 @@
     landing = [landings[d] for d in docs]
     shift = [landing[d] & (S - 1) for d in docs]
     first = [pl.multiple_of(landing[d] - shift[d], S) for d in docs]
-    for n in range(KV):
+    for i in range(len(kvs)):
         for d in docs:
-            load(d, n).wait()
-        base = KVROWS * n
+            load(d, i).wait()
+        base = KVROWS * i
         for half in (docs[: NDOC // 2], docs[NDOC // 2 :]):
             causal = {d: ((row - landing[d]) & (S - 1)) <= ((column - landing[d]) & (S - 1)) for d in half}
             square = {d: slot[d, base : base + 2 * S, :].astype(F32) for d in half}
@@ -309,31 +335,30 @@
                 put(q_buf, d, spread_heads(query[d]))
                 put(k_buf, d, slot[d, base + 4 * S : base + 5 * S, :].astype(F32))
                 put(v_buf, d, slot[d, base + 5 * S : base + 6 * S, :].astype(F32))
-        if n >= 2:
-            for copy in stores(n - 2):
+        if i >= 2:
+            for copy in stores(i - 2):
                 copy.wait()
         for buf, final in ((o_buf, o_out), (q_buf, q_out), (k_buf, k_out), (v_buf, v_out)):
-            final[n % 2] = buf[:MOVE, :].astype(BF)
-        for copy in stores(n):
+            final[i % 2] = buf[:MOVE, :].astype(BF)
+        for copy in stores(i):
             copy.start()
-    for n in (KV - 2, KV - 1):
-        for copy in stores(n):
+    for i in range(max(0, len(kvs) - 2), len(kvs)):
+        for copy in stores(i):
             copy.wait()
 
 
-def receive(sources, landings, near, far, outs):
+def receive(near, far, outs, kvs):
     hbm = pl.BlockSpec(memory_space=pltpu.HBM)
-    smem = pl.BlockSpec(memory_space=pltpu.SMEM)
     padded = MOVE + S
     wide, narrow = GROUP * HD, HD
     return pl.pallas_call(
-        receive_kernel,
+        functools.partial(receive_kernel, kvs),
         out_shape=[jax.ShapeDtypeStruct(o.shape, o.dtype) for o in outs],
-        in_specs=[smem, smem] + [hbm] * (1 + NFAR + 4),
+        in_specs=[pl.BlockSpec(memory_space=pl.ANY)] + [hbm] * (NFAR + 4),
         out_specs=[hbm] * 4,
-        input_output_aliases={3 + NFAR + i: i for i in range(4)},
+        input_output_aliases={1 + NFAR + i: i for i in range(4)},
         scratch_shapes=[
-            pltpu.VMEM((NDOC, KVROWS * KV, HD), BF),
+            pltpu.VMEM((NDOC, KVROWS * len(kvs), HD), BF),
             pltpu.VMEM((padded, wide), F32),
             pltpu.VMEM((padded, wide), F32),
             pltpu.VMEM((padded, narrow), F32),
@@ -342,27 +367,16 @@
             pltpu.VMEM((2, MOVE, wide), BF),
             pltpu.VMEM((2, MOVE, narrow), BF),
             pltpu.VMEM((2, MOVE, narrow), BF),
-            pltpu.SemaphoreType.DMA((NDOC, KV)),
+            pltpu.VMEM((NSLOT, META, HD), BF),
+            pltpu.SMEM((NDOC,), jnp.int32),
+            pltpu.SMEM((NDOC,), jnp.int32),
+            pltpu.SemaphoreType.DMA((NDOC, len(kvs))),
             pltpu.SemaphoreType.DMA((4, 2)),
+            pltpu.SemaphoreType.DMA((1 + NFAR,)),
         ],
-        cost_estimate=pl.CostEstimate(flops=4_000_000_000, bytes_accessed=10_000_000, transcendentals=0),
+        cost_estimate=pl.CostEstimate(flops=1_000_000_000 * len(kvs), bytes_accessed=2_500_000 * len(kvs), transcendentals=0),
         name="receive",
-    )(sources, landings, near, *far, *outs)
-
-
-def placement(codes):
-    valid = codes > 0
-    rank = jnp.sum((valid[None, :] & (codes[None, :] < codes[:, None])).astype(jnp.int32), axis=1)
-    order = jnp.arange(NDOC, dtype=jnp.int32)
-    chosen = valid[None, :] & (rank[None, :] == order[:, None])
-    sources = jnp.sum(jnp.where(chosen, jnp.arange(NSLOT, dtype=jnp.int32)[None, :], 0), axis=1)
-    landings = jnp.sum(jnp.where(chosen, (codes - 1)[None, :], 0), axis=1)
-    return sources, landings
-
-
-def codes_of(meta):
-    pairs = meta.astype(F32).astype(jnp.int32)
-    return pairs[:, 0] * 32 + pairs[:, S]
+    )(near, *far, *outs)
 
 
 def swap(x, axis, size, mask):
@@ -415,9 +429,9 @@
     mine = lax.dynamic_index_in_dim(grad, core, 1, keepdims=False)
     table, other = lax.optimization_barrier((table, other))
     near, *far = send(table, q, k, v, g)
-    part = add(mine, swap(other, "core", 2, 1)).astype(BF).reshape(2, 4, 4, 64, -1)
+    part = add(mine, swap(other, "core", 2, 1)).astype(BF).reshape(2, 4, 256, -1)
     near = lax.all_to_all(near, ("z", "core"), split_axis=0, concat_axis=0, tiled=True)
-    part_x = reduce_ring(part, "x", 1)
+    part_x = reduce_ring(part, "x", 1).reshape(2, 4, 64, -1)
     outs = home(home_lengths, q, k, v, g)
     part_x, *outs = lax.optimization_barrier((part_x, *outs))
     needs = {3: (part,), 5: tuple(outs), 6: (part_x,)}
@@ -436,13 +450,14 @@
     kept = lax.dynamic_index_in_dim(part_z, yhi, 0, keepdims=False)
     given = lax.dynamic_index_in_dim(part_z, 1 - yhi, 0, keepdims=False)
     from_y = [lax.ppermute(given if mask & 1 else kept, ("ylo", "yhi"), [(i, i ^ mask) for i in range(4)]) for mask in (1, 2, 3)]
+    outs = receive(near, far, outs, (0, 1))
+    from_y, outs = lax.optimization_barrier((from_y, outs))
     total = add(kept, *from_y).astype(BF)
     held = [total, *shifts(lambda step: total, "z", 4)]
-
-    meta = jnp.concatenate([near[:, KVROWS * KV, :], jnp.stack([f[KVROWS * KV, :] for f in far])], axis=0)
-    sources, landings = placement(codes_of(meta))
-    outs = receive(sources, landings, near, far, outs)
+    *outs, total = lax.optimization_barrier((*outs, total))
+    outs = receive(near, far, outs, (2, 3))
     held, outs = lax.optimization_barrier((held, outs))
+
 
     held = jnp.stack(held)
     half = jnp.concatenate([lax.dynamic_index_in_dim(held, (z - b) % 4, 0, keepdims=False) for b in range(4)], axis=0)

time: 132 us -> 128 us (0.970)
  waiting for transfers between devices: 31.6 us -> 39.4 us
  starting transfers between devices: 49.5 us -> 42.1 us
  local copies, waits for them, and re-layouts: 13.4 us -> 6.4 us
  Pallas kernels: 26.4 us -> 30.4 us
    ppermute x9, waiting for transfers between devices: 13.5 us -> 21.7 us  [shifts(): lax.ppermute(pieces(step), axis, [(i, (i + step) % size) for i in range(s...]
    ppermute x3, starting transfers between devices: 9.93 us -> 3.77 us  [per_device(): lax.ppermute(given if mask & 1 else kept, ('ylo', 'yhi'), [(i, i ^ mask)...]
    slice x9 -> x0, local copies, waits for them, and re-layouts: 5.28 us -> none  [the longest x8 5.27 us: per_device(): f[KVROWS * KV, :]]
    ppermute x3, waiting for transfers between devices: 5 us -> 0.01 us  [per_device(): lax.ppermute(given if mask & 1 else kept, ('ylo', 'yhi'), [(i, i ^ mask)...]
    ppermute x8, waiting for transfers between devices: 11.8 us -> 16.5 us  [per_device(): lax.ppermute(payload, DP, [(i, i ^ NFAR + m) for i in range(NSLOT)])]
    pallas_call x2 -> x3, Pallas kernels: 17.9 us -> 21.8 us  [the longest x2 11.7 us: receive(): pl.pallas_call(functools.partial(receive_kernel, kvs), out_shape=[jax.Sha...]
    dynamic_slice x4 -> x0, local copies, waits for them, and re-layouts: 3.46 us -> none  [block(): lax.dynamic_index_in_dim(part, (place + step) % 4, dim, keepdims=False)]
    convert_element_type x2 -> x1, other arithmetic: 2.88 us -> 2.87 us  [per_device(): add(mine, swap(other, 'core', 2, 1)).astype(BF).reshape(2, 4, 256, -1)]
  transfers between devices with their start and end apart: 23 -> 23, of which waited for: 7 -> 7; matrix products, arithmetic and copies ran while one was open for 12% -> 5% of each run, Pallas kernels for 14% -> 17%
where the time goes in v4:
time: 128 us; the launch traced here: 127 us
  starting transfers between devices  42.1 us (33%)
  waiting for transfers between devices  39.4 us (31%)
  Pallas kernels  30.4 us (24%)
  other arithmetic  8.29 us (6%)
  local copies, waits for them, and re-layouts  6.4 us (5%)
    ppermute x9, waiting for transfers between devices, shifts(): lax.ppermute(pieces(step), axis, [(i, (i + step) % size) for i in range(s...  21.7 us
    ppermute x8, starting transfers between devices, per_device(): lax.ppermute(payload, DP, [(i, i ^ NFAR + m) for i in range(NSLOT)])  21.3 us
    ppermute x8, waiting for transfers between devices, per_device(): lax.ppermute(payload, DP, [(i, i ^ NFAR + m) for i in range(NSLOT)])  16.5 us
    pallas_call x2, Pallas kernels, receive(): pl.pallas_call(functools.partial(receive_kernel, kvs), out_shape=[jax.Sha...  11.7 us
    pallas_call x1, Pallas kernels, home(): pl.pallas_call(home_kernel, out_shape=[pltpu.HBM((total, KV * GROUP * HD)...  10.1 us
    ppermute x9, starting transfers between devices, shifts(): lax.ppermute(pieces(step), axis, [(i, (i + step) % size) for i in range(s...  9.64 us
    pallas_call x1, Pallas kernels, send(): pl.pallas_call(send_kernel, out_shape=[jax.ShapeDtypeStruct((NFAR, KVROWS...  8.54 us
    all_to_all x1, starting transfers between devices, per_device(): lax.all_to_all(near, ('z', 'core'), split_axis=0, concat_axis=0, tiled=True)  5.53 us
  transfers between devices with their start and end apart: 23, of which 7 were waited for; matrix products, arithmetic and copies ran while one was open for 5% of the time, Pallas kernels for 17%

profile of v4, /device:TPU:1, one launch (start us, length us, event | category | flops | bytes accessed | tf_op | source)
XLA Modules:
  0.0 127.5 jit_solution(2221175698907517875)
XLA Ops:
  1.3 3.0 %dynamic-slice_bitcast_fusion = bf16[8,256,512]{2,1,0:T(8,128)(2,1)} fusion(bf16[8,2,256,512]{3,2,1,0:T(8,128)(2,1)} %bitcast.44, s32[]{:T(128)S(6)} %select_n.118), kind=kLoop, calls=%fused_computation.2 | loop fusion | bytes 4194308 | tf_op jit(solution)/shard_map/jit(dynamic_index_in_dim)/squeeze | solution.py:428
  5.0 1.4 %collective-permute-start = (bf16[8,256,512]{2,1,0:T(8,128)(2,1)}, bf16[8,256,512]{2,1,0:T(8,128)(2,1)}, u32[]{:S(2)}, u32[]{:S(2)}) collective-permute-start(bf16[8,256,512]{2,1,0:T(8,128)(2,1)} %dynamic-slice_bitcast_fusion), channel_id=1, source_target_pairs={{0,8},{8,0},{1,9},{9,1},{2,10},{10,2},{3,11},{11,3},{4,12},{12,4},... | collective-permute-start | bytes 6291464 | tf_op jit(solution)/shard_map/ppermute | solution.py:383
  6.4 8.5 %send.1 = (bf16[8,1544,128]{2,1,0:T(8,128)(2,1)}, bf16[1544,128]{1,0:T(8,128)(2,1)}, bf16[1544,128]{1,0:T(8,128)(2,1)}, bf16[1544,128]{1,0:T(8,128)(2,1)}, bf16[...) custom-call(s32[4,8]{1,0:T(4,128)} %pad_add_fusion.table, ...), custom_call_target="tpu_custom_call" | custom-call | flops 4000000000 | bytes 10000000 | tf_op jit(solution)/shard_map/send/pallas_call | solution.py:152
  15.0 5.5 %all-to-all-start = ((bf16[8,1544,128]{2,1,0:T(8,128)(2,1)}), bf16[8,1544,128]{2,1,0:T(8,128)(2,1)S(1)}, u32[]{:S(2)}, u32[]{:S(2)}) async-start(bf16[8,1544,128]{2,1,0:T(8,128)(2,1)} %get-tuple-element.64), calls=%async_computation | async-start | bytes 6324224 | tf_op jit(solution)/shard_map/all_to_all | solution.py:433
  20.5 1.3 %collective-permute-start.10 = (bf16[1544,128]{1,0:T(8,128)(2,1)}, bf16[1544,128]{1,0:T(8,128)(2,1)}, u32[]{:S(2)}, u32[]{:S(2)}) collective-permute-start(bf16[1544,128]{1,0:T(8,128)(2,1)} %get-tuple-element.65), channel_id=1, source_target_pairs={{0,64},{8,72},{16,80},{24,88},{32,96},{40,104},{48,112},{56,120},{... | collective-permute-start | bytes 1185800 | tf_op jit(solution)/shard_map/ppermute | solution.py:443
  21.8 1.3 collective-permute-start.11
  23.1 2.9 %fusion = bf16[8,256,512]{2,1,0:T(8,128)(2,1)S(1)} fusion(bf16[8,256,512]{2,1,0:T(8,128)(2,1)} %collective-permute-done, bf16[8,2,256,512]{3,2,1,0:T(8,128)(2,1)} %bitcast.45, s32[]{:T(128)S(6)} %select_n.116), kind=kLoop, calls=%fused_computation.1 | loop fusion | flops 4194304 | bytes 6291460 | tf_op jit(solution)/shard_map/convert_element_type | solution.py:432
  25.9 1.3 %copy-done.1 = bf16[8,256,512]{2,1,0:T(8,128)(2,1)} copy-done((bf16[8,256,512]{2,1,0:T(8,128)(2,1)}, bf16[8,256,512]{2,1,0:T(8,128)(2,1)S(1)}, u32[]{:S(2)}) %copy-start.1) | copy-done | bytes 2097176
  27.3 1.2 dynamic-slice_bitcast_fusion.3
  28.4 2.5 %collective-permute-start.3 = (bf16[2,256,512]{2,1,0:T(8,128)(2,1)}, bf16[2,256,512]{2,1,0:T(8,128)(2,1)}, u32[]{:S(2)}, u32[]{:S(2)}) collective-permute-start(bf16[2,256,512]{2,1,0:T(8,128)(2,1)} %get-tuple-element.110), channel_id=1, source_target_pairs={{0,3},{1,0},{2,1},{3,2},{4,7},{5,4},{6,5},{7,6},{8,11},{9,8},{10,9... | collective-permute-start | bytes 1572872 | tf_op jit(solution)/shard_map/ppermute | solution.py:394
  32.0 10.1 %home.1 = (bf16[896,2048]{1,0:T(8,128)(2,1)}, bf16[896,2048]{1,0:T(8,128)(2,1)}, bf16[896,512]{1,0:T(8,128)(2,1)}, bf16[896,512]{1,0:T(8,128)(2,1)}) custom-call(s32[1,6]{1,0:T(1,128)} %lengths.1, bf16[896,2048]{1,0:T(8,128)(2,1)} %q_hbm.1, bf16[896,512]{1,0:T(8,128)(2,1)} %k_hbm.1, bf16[896,512]{1,0:T(8,128)(2,1)} %v_hbm.1, bf16[896,2048]{1,0:T(8,128)(2,1)} %g_hbm.1), custom_call_target="tpu_custom_call" | custom-call | flops 10000000000 | bytes 10000000 | tf_op jit(solution)/shard_map/home/pallas_call | solution.py:216
  42.2 3.5 %collective-permute-start.16 = (bf16[1544,128]{1,0:T(8,128)(2,1)}, bf16[1544,128]{1,0:T(8,128)(2,1)}, u32[]{:S(2)}, u32[]{:S(2)}) collective-permute-start(bf16[1544,128]{1,0:T(8,128)(2,1)} %get-tuple-element.75), channel_id=1, source_target_pairs={{0,96},{8,104},{16,112},{24,120},{32,64},{40,72},{48,80},{56,88},{... | collective-permute-start | bytes 1185800 | tf_op jit(solution)/shard_map/ppermute | solution.py:443
  45.7 2.4 %collective-permute-start.12 = (bf16[1544,128]{1,0:T(8,128)(2,1)}, bf16[1544,128]{1,0:T(8,128)(2,1)}, u32[]{:S(2)}, u32[]{:S(2)}) collective-permute-start(bf16[1544,128]{1,0:T(8,128)(2,1)} %get-tuple-element.69), channel_id=1, source_target_pairs={{0,104},{8,96},{16,120},{24,112},{32,72},{40,64},{48,88},{56,80},{... | collective-permute-start | bytes 1185800 | tf_op jit(solution)/shard_map/ppermute | solution.py:443
  48.1 2.8 %collective-permute-start.14 = (bf16[1544,128]{1,0:T(8,128)(2,1)}, bf16[1544,128]{1,0:T(8,128)(2,1)}, u32[]{:S(2)}, u32[]{:S(2)}) collective-permute-start(bf16[1544,128]{1,0:T(8,128)(2,1)} %get-tuple-element.73), channel_id=1, source_target_pairs={{0,112},{8,120},{16,96},{24,104},{32,80},{40,88},{48,64},{56,72},{... | collective-permute-start | bytes 1185800 | tf_op jit(solution)/shard_map/ppermute | solution.py:443
  50.9 6.9 %collective-permute-done.1 = bf16[2,256,512]{2,1,0:T(8,128)(2,1)} collective-permute-done((bf16[2,256,512]{2,1,0:T(8,128)(2,1)}, bf16[2,256,512]{2,1,0:T(8,128)(2,1)}, u32[]{:S(2)}, u32[]{:S(2)}) %collective-permute-start.1) | collective-permute-done | bytes 524320 | tf_op jit(solution)/shard_map/ppermute | solution.py:394
  57.8 1.8 %fusion.3 = bf16[2,256,512]{2,1,0:T(8,128)(2,1)S(1)} fusion(bf16[2,256,512]{2,1,0:T(8,128)(2,1)} %collective-permute-done.3, bf16[2,256,512]{2,1,0:T(8,128)(2,1)} %collective-permute-done.2, bf16[2,256,512]{2,1,0:T(8,128)(2,1)} %collective-permute-done.1, bf16[2,4,256,512]{3,2,1,0:T(8,128)(2,1)} %bitcast.43, s32[]{:T(128)S(6)} %select_n.120), kind=kLoop, calls=%fused_computation.6 | loop fusion | flops 2097152 | bytes 2621444 | tf_op jit(solution)/shard_map/convert_element_type | solution.py:411
  60.4 1.9 %collective-permute-start.6 = (bf16[2,64,512]{2,1,0:T(8,128)(2,1)S(1)}, bf16[2,64,512]{2,1,0:T(8,128)(2,1)S(1)}, u32[]{:S(2)}, u32[]{:S(2)}) collective-permute-start(bf16[2,64,512]{2,1,0:T(8,128)(2,1)S(1)} %get-tuple-element.115), channel_id=1, source_target_pairs={{0,48},{16,0},{32,16},{48,32},{1,49},{17,1},{33,17},{49,33},{2,50}... | collective-permute-start | bytes 393224 | tf_op jit(solution)/shard_map/ppermute | solution.py:394
  62.9 4.2 %collective-permute-done.12.refs_5_ = bf16[1544,128]{1,0:T(8,128)(2,1)} collective-permute-done((bf16[1544,128]{1,0:T(8,128)(2,1)}, bf16[1544,128]{1,0:T(8,128)(2,1)}, u32[]{:S(2)}, u32[]{:S(2)}) %collective-permute-start.12) | collective-permute-done | bytes 395296 | tf_op jit(solution)/shard_map/ppermute | solution.py:443
  67.1 6.4 %collective-permute-done.14.refs_6_ = bf16[1544,128]{1,0:T(8,128)(2,1)} collective-permute-done((bf16[1544,128]{1,0:T(8,128)(2,1)}, bf16[1544,128]{1,0:T(8,128)(2,1)}, u32[]{:S(2)}, u32[]{:S(2)}) %collective-permute-start.14) | collective-permute-done | bytes 395296 | tf_op jit(solution)/shard_map/ppermute | solution.py:443
  73.6 5.8 %collective-permute-start.13 = (bf16[1544,128]{1,0:T(8,128)(2,1)}, bf16[1544,128]{1,0:T(8,128)(2,1)}, u32[]{:S(2)}, u32[]{:S(2)}) collective-permute-start(bf16[1544,128]{1,0:T(8,128)(2,1)} %get-tuple-element.70), channel_id=1, source_target_pairs={{0,72},{8,64},{16,88},{24,80},{32,104},{40,96},{48,120},{56,112},{... | collective-permute-start | bytes 1185800 | tf_op jit(solution)/shard_map/ppermute | solution.py:443
  79.4 8.4 %collective-permute-done.6 = bf16[2,64,512]{2,1,0:T(8,128)(2,1)S(1)} collective-permute-done((bf16[2,64,512]{2,1,0:T(8,128)(2,1)S(1)}, bf16[2,64,512]{2,1,0:T(8,128)(2,1)S(1)}, u32[]{:S(2)}, u32[]{:S(2)}) %collective-permute-start.6) | collective-permute-done | bytes 131104 | tf_op jit(solution)/shard_map/ppermute | solution.py:394
  87.8 4.2 %collective-permute-start.17 = (bf16[1544,128]{1,0:T(8,128)(2,1)}, bf16[1544,128]{1,0:T(8,128)(2,1)}, u32[]{:S(2)}, u32[]{:S(2)}) collective-permute-start(bf16[1544,128]{1,0:T(8,128)(2,1)} %get-tuple-element.81), channel_id=1, source_target_pairs={{0,120},{8,112},{16,104},{24,96},{32,88},{40,80},{48,72},{56,64},{... | collective-permute-start | bytes 1185800 | tf_op jit(solution)/shard_map/ppermute | solution.py:443
  92.0 6.5 %collective-permute-done.4 = bf16[2,64,512]{2,1,0:T(8,128)(2,1)} collective-permute-done((bf16[2,64,512]{2,1,0:T(8,128)(2,1)S(1)}, bf16[2,64,512]{2,1,0:T(8,128)(2,1)}, u32[]{:S(2)}, u32[]{:S(2)}) %collective-permute-start.4) | collective-permute-done | bytes 131104 | tf_op jit(solution)/shard_map/ppermute | solution.py:394
  98.4 1.1 fusion.6
  99.6 3.0 %collective-permute-start.7 = (bf16[64,512]{1,0:T(8,128)(2,1)S(1)}, bf16[64,512]{1,0:T(8,128)(2,1)S(1)}, u32[]{:S(2)}, u32[]{:S(2)}) collective-permute-start(bf16[64,512]{1,0:T(8,128)(2,1)S(1)} %get-tuple-element.122), channel_id=1, source_target_pairs={{0,4},{4,0},{64,68},{68,64},{1,5},{5,1},{65,69},{69,65},{2,6},{6,2... | collective-permute-start | bytes 196616 | tf_op jit(solution)/shard_map/ppermute | solution.py:452
  102.5 0.8 collective-permute-start.9
  103.4 5.8 %collective-permute-done.17.refs_7_ = bf16[1544,128]{1,0:T(8,128)(2,1)} collective-permute-done((bf16[1544,128]{1,0:T(8,128)(2,1)}, bf16[1544,128]{1,0:T(8,128)(2,1)}, u32[]{:S(2)}, u32[]{:S(2)}) %collective-permute-start.17) | collective-permute-done | bytes 395296 | tf_op jit(solution)/shard_map/ppermute | solution.py:443
  109.2 5.9 %receive.2 = (bf16[896,2048]{1,0:T(8,128)(2,1)}, bf16[896,2048]{1,0:T(8,128)(2,1)}, bf16[896,512]{1,0:T(8,128)(2,1)}, bf16[896,512]{1,0:T(8,128)(2,1)}) custom-call(bf16[8,1544,128]{2,1,0:T(8,128)(2,1)} %copy-done, bf16[1544,128]{1,0:T(8,128)(2,1)} %collective-permute-done.10.refs_0_, ...), custom_call_target="tpu_custom_call", output_to_operand_aliasing={{0}: (9, {}), {1}: (10, {}), {2}: (11, {}), {3}: (12, {})} | custom-call | flops 2000000000 | bytes 5000000 | tf_op jit(solution)/shard_map/receive/pallas_call | solution.py:354
  115.6 3.0 %collective-permute-start.19 = (bf16[64,512]{1,0:T(8,128)(2,1)S(1)}, bf16[64,512]{1,0:T(8,128)(2,1)S(1)}, u32[]{:S(2)}, u32[]{:S(2)}) collective-permute-start(bf16[64,512]{1,0:T(8,128)(2,1)S(1)} %add_convert_fusion), channel_id=1, source_target_pairs={{0,32},{16,48},{32,0},{48,16},{1,33},{17,49},{33,1},{49,17},{2,34}... | collective-permute-start | bytes 196616 | tf_op jit(solution)/shard_map/ppermute | solution.py:394
  118.6 5.9 %receive.3 = (bf16[896,2048]{1,0:T(8,128)(2,1)}, bf16[896,2048]{1,0:T(8,128)(2,1)}, bf16[896,512]{1,0:T(8,128)(2,1)}, bf16[896,512]{1,0:T(8,128)(2,1)}) custom-call(bf16[8,1544,128]{2,1,0:T(8,128)(2,1)} %copy-done, bf16[1544,128]{1,0:T(8,128)(2,1)} %collective-permute-done.10.refs_0_, ...), custom_call_target="tpu_custom_call", output_to_operand_aliasing={{0}: (9, {}), {1}: (10, {}), {2}: (11, {}), {3}: (12, {})} | custom-call | flops 2000000000 | bytes 5000000 | tf_op jit(solution)/shard_map/receive/pallas_call | solution.py:354
  125.1 1.2 collective-permute-done.21
  126.4 1.1 maximum_convert_fusion
  (45 shorter events, 5.2 us)
Async XLA Ops:
  0.6 3.8 %copy-start.3 = (s32[1,8]{1,0:T(1,128)S(1)}, s32[1,8]{1,0:T(1,128)}, u32[]{:S(2)}) copy-start(s32[1,8]{1,0:T(1,128)} %param.18) | copy-start | bytes 100
  0.6 3.7 %copy-start.4 = (s32[1,8]{1,0:T(1,128)S(1)}, s32[1,8]{1,0:T(1,128)}, u32[]{:S(2)}) copy-start(s32[1,8]{1,0:T(1,128)} %param.16) | copy-start | bytes 100
  0.7 3.7 %copy-start.5 = (s32[1,8]{1,0:T(1,128)S(1)}, s32[1,8]{1,0:T(1,128)}, u32[]{:S(2)}) copy-start(s32[1,8]{1,0:T(1,128)} %param.15) | copy-start | bytes 100
  5.0 18.1 %collective-permute-start = (bf16[8,256,512]{2,1,0:T(8,128)(2,1)}, bf16[8,256,512]{2,1,0:T(8,128)(2,1)}, u32[]{:S(2)}, u32[]{:S(2)}) collective-permute-start(bf16[8,256,512]{2,1,0:T(8,128)(2,1)} %dynamic-slice_bitcast_fusion), channel_id=1, source_target_pairs={{0,8},{8,0},{1,9},{9,1},{2,10},{10,2},{3,11},{11,3},{4,12},{12,4},... | collective-permute-start | bytes 6291464 | tf_op jit(solution)/shard_map/ppermute | solution.py:383
  15.0 88.4 %all-to-all-start = ((bf16[8,1544,128]{2,1,0:T(8,128)(2,1)}), bf16[8,1544,128]{2,1,0:T(8,128)(2,1)S(1)}, u32[]{:S(2)}, u32[]{:S(2)}) async-start(bf16[8,1544,128]{2,1,0:T(8,128)(2,1)} %get-tuple-element.64), calls=%async_computation | async-start | bytes 6324224 | tf_op jit(solution)/shard_map/all_to_all | solution.py:433
  20.5 25.2 %collective-permute-start.10 = (bf16[1544,128]{1,0:T(8,128)(2,1)}, bf16[1544,128]{1,0:T(8,128)(2,1)}, u32[]{:S(2)}, u32[]{:S(2)}) collective-permute-start(bf16[1544,128]{1,0:T(8,128)(2,1)} %get-tuple-element.65), channel_id=1, source_target_pairs={{0,64},{8,72},{16,80},{24,88},{32,96},{40,104},{48,112},{56,120},{... | collective-permute-start | bytes 1185800 | tf_op jit(solution)/shard_map/ppermute | solution.py:443
  21.8 20.4 %collective-permute-start.11 = (bf16[1544,128]{1,0:T(8,128)(2,1)}, bf16[1544,128]{1,0:T(8,128)(2,1)}, u32[]{:S(2)}, u32[]{:S(2)}) collective-permute-start(bf16[1544,128]{1,0:T(8,128)(2,1)} %get-tuple-element.68), channel_id=1, source_target_pairs={{0,80},{8,88},{16,64},{24,72},{32,112},{40,120},{48,96},{56,104},{... | collective-permute-start | bytes 1185800 | tf_op jit(solution)/shard_map/ppermute | solution.py:443
  25.9 1.3 %copy-start.1 = (bf16[8,256,512]{2,1,0:T(8,128)(2,1)}, bf16[8,256,512]{2,1,0:T(8,128)(2,1)S(1)}, u32[]{:S(2)}) copy-start(bf16[8,256,512]{2,1,0:T(8,128)(2,1)S(1)} %fusion) | copy-start | bytes 6291460
  28.4 19.6 %collective-permute-start.3 = (bf16[2,256,512]{2,1,0:T(8,128)(2,1)}, bf16[2,256,512]{2,1,0:T(8,128)(2,1)}, u32[]{:S(2)}, u32[]{:S(2)}) collective-permute-start(bf16[2,256,512]{2,1,0:T(8,128)(2,1)} %get-tuple-element.110), channel_id=1, source_target_pairs={{0,3},{1,0},{2,1},{3,2},{4,7},{5,4},{6,5},{7,6},{8,11},{9,8},{10,9... | collective-permute-start | bytes 1572872 | tf_op jit(solution)/shard_map/ppermute | solution.py:394
  30.9 20.0 %collective-permute-start.2 = (bf16[2,256,512]{2,1,0:T(8,128)(2,1)}, bf16[2,256,512]{2,1,0:T(8,128)(2,1)}, u32[]{:S(2)}, u32[]{:S(2)}) collective-permute-start(bf16[2,256,512]{2,1,0:T(8,128)(2,1)} %get-tuple-element.111), channel_id=1, source_target_pairs={{0,2},{1,3},{2,0},{3,1},{4,6},{5,7},{6,4},{7,5},{8,10},{9,11},{10,... | collective-permute-start | bytes 1572872 | tf_op jit(solution)/shard_map/ppermute | solution.py:394
  31.4 26.4 %collective-permute-start.1 = (bf16[2,256,512]{2,1,0:T(8,128)(2,1)}, bf16[2,256,512]{2,1,0:T(8,128)(2,1)}, u32[]{:S(2)}, u32[]{:S(2)}) collective-permute-start(bf16[2,256,512]{2,1,0:T(8,128)(2,1)} %get-tuple-element.109), channel_id=1, source_target_pairs={{0,1},{1,2},{2,3},{3,0},{4,5},{5,6},{6,7},{7,4},{8,9},{9,10},{10,1... | collective-permute-start | bytes 1572872 | tf_op jit(solution)/shard_map/ppermute | solution.py:394
  42.2 37.2 %collective-permute-start.16 = (bf16[1544,128]{1,0:T(8,128)(2,1)}, bf16[1544,128]{1,0:T(8,128)(2,1)}, u32[]{:S(2)}, u32[]{:S(2)}) collective-permute-start(bf16[1544,128]{1,0:T(8,128)(2,1)} %get-tuple-element.75), channel_id=1, source_target_pairs={{0,96},{8,104},{16,112},{24,120},{32,64},{40,72},{48,80},{56,88},{... | collective-permute-start | bytes 1185800 | tf_op jit(solution)/shard_map/ppermute | solution.py:443
  45.7 21.5 %collective-permute-start.12 = (bf16[1544,128]{1,0:T(8,128)(2,1)}, bf16[1544,128]{1,0:T(8,128)(2,1)}, u32[]{:S(2)}, u32[]{:S(2)}) collective-permute-start(bf16[1544,128]{1,0:T(8,128)(2,1)} %get-tuple-element.69), channel_id=1, source_target_pairs={{0,104},{8,96},{16,120},{24,112},{32,72},{40,64},{48,88},{56,80},{... | collective-permute-start | bytes 1185800 | tf_op jit(solution)/shard_map/ppermute | solution.py:443
  48.1 25.5 %collective-permute-start.14 = (bf16[1544,128]{1,0:T(8,128)(2,1)}, bf16[1544,128]{1,0:T(8,128)(2,1)}, u32[]{:S(2)}, u32[]{:S(2)}) collective-permute-start(bf16[1544,128]{1,0:T(8,128)(2,1)} %get-tuple-element.73), channel_id=1, source_target_pairs={{0,112},{8,120},{16,96},{24,104},{32,80},{40,88},{48,64},{56,72},{... | collective-permute-start | bytes 1185800 | tf_op jit(solution)/shard_map/ppermute | solution.py:443
  59.6 0.8 copy-start.2
  60.4 27.4 %collective-permute-start.6 = (bf16[2,64,512]{2,1,0:T(8,128)(2,1)S(1)}, bf16[2,64,512]{2,1,0:T(8,128)(2,1)S(1)}, u32[]{:S(2)}, u32[]{:S(2)}) collective-permute-start(bf16[2,64,512]{2,1,0:T(8,128)(2,1)S(1)} %get-tuple-element.115), channel_id=1, source_target_pairs={{0,48},{16,0},{32,16},{48,32},{1,49},{17,1},{33,17},{49,33},{2,50}... | collective-permute-start | bytes 393224 | tf_op jit(solution)/shard_map/ppermute | solution.py:394
  62.2 29.7 %collective-permute-start.5 = (bf16[2,64,512]{2,1,0:T(8,128)(2,1)S(1)}, bf16[2,64,512]{2,1,0:T(8,128)(2,1)}, u32[]{:S(2)}, u32[]{:S(2)}) collective-permute-start(bf16[2,64,512]{2,1,0:T(8,128)(2,1)S(1)} %get-tuple-element.116), channel_id=1, source_target_pairs={{0,32},{16,48},{32,0},{48,16},{1,33},{17,49},{33,1},{49,17},{2,34}... | collective-permute-start | bytes 393224 | tf_op jit(solution)/shard_map/ppermute | solution.py:394
  67.1 31.3 %collective-permute-start.4 = (bf16[2,64,512]{2,1,0:T(8,128)(2,1)S(1)}, bf16[2,64,512]{2,1,0:T(8,128)(2,1)}, u32[]{:S(2)}, u32[]{:S(2)}) collective-permute-start(bf16[2,64,512]{2,1,0:T(8,128)(2,1)S(1)} %get-tuple-element.114), channel_id=1, source_target_pairs={{0,16},{16,32},{32,48},{48,0},{1,17},{17,33},{33,49},{49,1},{2,18}... | collective-permute-start | bytes 393224 | tf_op jit(solution)/shard_map/ppermute | solution.py:394
  73.6 29.8 %collective-permute-start.13 = (bf16[1544,128]{1,0:T(8,128)(2,1)}, bf16[1544,128]{1,0:T(8,128)(2,1)}, u32[]{:S(2)}, u32[]{:S(2)}) collective-permute-start(bf16[1544,128]{1,0:T(8,128)(2,1)} %get-tuple-element.70), channel_id=1, source_target_pairs={{0,72},{8,64},{16,88},{24,80},{32,104},{40,96},{48,120},{56,112},{... | collective-permute-start | bytes 1185800 | tf_op jit(solution)/shard_map/ppermute | solution.py:443
  79.4 23.9 %collective-permute-start.15 = (bf16[1544,128]{1,0:T(8,128)(2,1)}, bf16[1544,128]{1,0:T(8,128)(2,1)}, u32[]{:S(2)}, u32[]{:S(2)}) collective-permute-start(bf16[1544,128]{1,0:T(8,128)(2,1)} %get-tuple-element.74), channel_id=1, source_target_pairs={{0,88},{8,80},{16,72},{24,64},{32,120},{40,112},{48,104},{56,96},{... | collective-permute-start | bytes 1185800 | tf_op jit(solution)/shard_map/ppermute | solution.py:443
  87.8 21.4 %collective-permute-start.17 = (bf16[1544,128]{1,0:T(8,128)(2,1)}, bf16[1544,128]{1,0:T(8,128)(2,1)}, u32[]{:S(2)}, u32[]{:S(2)}) collective-permute-start(bf16[1544,128]{1,0:T(8,128)(2,1)} %get-tuple-element.81), channel_id=1, source_target_pairs={{0,120},{8,112},{16,104},{24,96},{32,88},{40,80},{48,72},{56,64},{... | collective-permute-start | bytes 1185800 | tf_op jit(solution)/shard_map/ppermute | solution.py:443
  99.6 15.5 %collective-permute-start.7 = (bf16[64,512]{1,0:T(8,128)(2,1)S(1)}, bf16[64,512]{1,0:T(8,128)(2,1)S(1)}, u32[]{:S(2)}, u32[]{:S(2)}) collective-permute-start(bf16[64,512]{1,0:T(8,128)(2,1)S(1)} %get-tuple-element.122), channel_id=1, source_target_pairs={{0,4},{4,0},{64,68},{68,64},{1,5},{5,1},{65,69},{69,65},{2,6},{6,2... | collective-permute-start | bytes 196616 | tf_op jit(solution)/shard_map/ppermute | solution.py:452
  102.5 12.6 %collective-permute-start.9 = (bf16[64,512]{1,0:T(8,128)(2,1)S(1)}, bf16[64,512]{1,0:T(8,128)(2,1)S(1)}, u32[]{:S(2)}, u32[]{:S(2)}) collective-permute-start(bf16[64,512]{1,0:T(8,128)(2,1)S(1)} %get-tuple-element.122), channel_id=1, source_target_pairs={{0,68},{4,64},{64,4},{68,0},{1,69},{5,65},{65,5},{69,1},{2,70},{6,... | collective-permute-start | bytes 196616 | tf_op jit(solution)/shard_map/ppermute | solution.py:452
  103.3 11.8 %collective-permute-start.8 = (bf16[64,512]{1,0:T(8,128)(2,1)S(1)}, bf16[64,512]{1,0:T(8,128)(2,1)S(1)}, u32[]{:S(2)}, u32[]{:S(2)}) collective-permute-start(bf16[64,512]{1,0:T(8,128)(2,1)S(1)} %get-tuple-element.121), channel_id=1, source_target_pairs={{0,64},{4,68},{64,0},{68,4},{1,65},{5,69},{65,1},{69,5},{2,66},{6,... | collective-permute-start | bytes 196616 | tf_op jit(solution)/shard_map/ppermute | solution.py:452
  103.3 5.9 %copy-start = (bf16[8,1544,128]{2,1,0:T(8,128)(2,1)}, bf16[8,1544,128]{2,1,0:T(8,128)(2,1)S(1)}, u32[]{:S(2)}) copy-start(bf16[8,1544,128]{2,1,0:T(8,128)(2,1)S(1)} %all-to-all-done.near) | copy-start | bytes 9486340
  115.1 9.4 %collective-permute-start.18 = (bf16[64,512]{1,0:T(8,128)(2,1)S(1)}, bf16[64,512]{1,0:T(8,128)(2,1)S(1)}, u32[]{:S(2)}, u32[]{:S(2)}) collective-permute-start(bf16[64,512]{1,0:T(8,128)(2,1)S(1)} %add_convert_fusion), channel_id=1, source_target_pairs={{0,16},{16,32},{32,48},{48,0},{1,17},{17,33},{33,49},{49,1},{2,18}... | collective-permute-start | bytes 196616 | tf_op jit(solution)/shard_map/ppermute | solution.py:394
  115.6 8.9 %collective-permute-start.19 = (bf16[64,512]{1,0:T(8,128)(2,1)S(1)}, bf16[64,512]{1,0:T(8,128)(2,1)S(1)}, u32[]{:S(2)}, u32[]{:S(2)}) collective-permute-start(bf16[64,512]{1,0:T(8,128)(2,1)S(1)} %add_convert_fusion), channel_id=1, source_target_pairs={{0,32},{16,48},{32,0},{48,16},{1,33},{17,49},{33,1},{49,17},{2,34}... | collective-permute-start | bytes 196616 | tf_op jit(solution)/shard_map/ppermute | solution.py:394
  118.6 5.9 %collective-permute-start.20 = (bf16[64,512]{1,0:T(8,128)(2,1)S(1)}, bf16[64,512]{1,0:T(8,128)(2,1)S(1)}, u32[]{:S(2)}, u32[]{:S(2)}) collective-permute-start(bf16[64,512]{1,0:T(8,128)(2,1)S(1)} %add_convert_fusion), channel_id=1, source_target_pairs={{0,48},{16,0},{32,16},{48,32},{1,49},{17,1},{33,17},{49,33},{2,50}... | collective-permute-start | bytes 196616 | tf_op jit(solution)/shard_map/ppermute | solution.py:394
  124.6 1.6 %collective-permute-start.21 = (bf16[256,512]{1,0:T(8,128)(2,1)S(1)}, bf16[256,512]{1,0:T(8,128)(2,1)S(1)}, u32[]{:S(2)}, u32[]{:S(2)}) collective-permute-start(bf16[256,512]{1,0:T(8,128)(2,1)S(1)} %pad_maximum_fusion.1), channel_id=1, source_target_pairs={{0,8},{8,0},{1,9},{9,1},{2,10},{10,2},{3,11},{11,3},{4,12},{12,4},... | collective-permute-start | bytes 786440 | tf_op jit(solution)/shard_map/ppermute | solution.py:383

commit v5 on v4

--- a/solution.py
+++ b/solution.py
@@ -427,7 +427,6 @@
     grad = layer_grad.reshape(8, 2, 256, layer_grad.shape[-1])
     other = lax.dynamic_index_in_dim(grad, 1 - core, 1, keepdims=False)
     mine = lax.dynamic_index_in_dim(grad, core, 1, keepdims=False)
-    table, other = lax.optimization_barrier((table, other))
     near, *far = send(table, q, k, v, g)
     part = add(mine, swap(other, "core", 2, 1)).astype(BF).reshape(2, 4, 256, -1)
     near = lax.all_to_all(near, ("z", "core"), split_axis=0, concat_axis=0, tiled=True)

time: 128 us -> 127 us (level)
  transfers between devices with their start and end apart: 23 -> 23, of which waited for: 7 -> 7; matrix products, arithmetic and copies ran while one was open for 5% -> 6% of each run, Pallas kernels for 17% -> 17%
where the time goes in v5:
time: 127 us
  starting transfers between devices  41.8 us (33%)
  waiting for transfers between devices  39.7 us (31%)
  Pallas kernels  30.4 us (24%)
  other arithmetic  7.63 us (6%)
  local copies, waits for them, and re-layouts  6.43 us (5%)
    ppermute x9, waiting for transfers between devices, shifts(): lax.ppermute(pieces(step), axis, [(i, (i + step) % size) for i in range(s...  21.6 us
    ppermute x8, starting transfers between devices, per_device(): lax.ppermute(payload, DP, [(i, i ^ NFAR + m) for i in range(NSLOT)])  21.1 us
    ppermute x8, waiting for transfers between devices, per_device(): lax.ppermute(payload, DP, [(i, i ^ NFAR + m) for i in range(NSLOT)])  16.8 us
    pallas_call x2, Pallas kernels, receive(): pl.pallas_call(functools.partial(receive_kernel, kvs), out_shape=[jax.Sha...  11.7 us
    pallas_call x1, Pallas kernels, home(): pl.pallas_call(home_kernel, out_shape=[pltpu.HBM((total, KV * GROUP * HD)...  10.1 us
    ppermute x9, starting transfers between devices, shifts(): lax.ppermute(pieces(step), axis, [(i, (i + step) % size) for i in range(s...  9.62 us
    pallas_call x1, Pallas kernels, send(): pl.pallas_call(send_kernel, out_shape=[jax.ShapeDtypeStruct((NFAR, KVROWS...  8.56 us
    all_to_all x1, starting transfers between devices, per_device(): lax.all_to_all(near, ('z', 'core'), split_axis=0, concat_axis=0, tiled=True)  5.48 us
  transfers between devices with their start and end apart: 23, of which 7 were waited for; matrix products, arithmetic and copies ran while one was open for 6% of the time, Pallas kernels for 17%

profile of v5, /device:TPU:1, one launch (start us, length us, event | category | flops | bytes accessed | tf_op | source)
XLA Modules:
  0.0 126.9 jit_solution(15800528569883445461)
XLA Ops:
  0.7 3.1 %dynamic-slice_bitcast_fusion = bf16[8,256,512]{2,1,0:T(8,128)(2,1)} fusion(bf16[8,2,256,512]{3,2,1,0:T(8,128)(2,1)} %bitcast.44, s32[]{:T(128)S(6)} %select_n.117), kind=kLoop, calls=%fused_computation.2 | loop fusion | bytes 4194308 | tf_op jit(solution)/shard_map/jit(dynamic_index_in_dim)/squeeze | solution.py:428
  3.7 1.4 %collective-permute-start = (bf16[8,256,512]{2,1,0:T(8,128)(2,1)}, bf16[8,256,512]{2,1,0:T(8,128)(2,1)}, u32[]{:S(2)}, u32[]{:S(2)}) collective-permute-start(bf16[8,256,512]{2,1,0:T(8,128)(2,1)} %dynamic-slice_bitcast_fusion), channel_id=1, source_target_pairs={{0,8},{8,0},{1,9},{9,1},{2,10},{10,2},{3,11},{11,3},{4,12},{12,4},... | collective-permute-start | bytes 6291464 | tf_op jit(solution)/shard_map/ppermute | solution.py:383
  5.8 8.6 %send.1 = (bf16[8,1544,128]{2,1,0:T(8,128)(2,1)}, bf16[1544,128]{1,0:T(8,128)(2,1)}, bf16[1544,128]{1,0:T(8,128)(2,1)}, bf16[1544,128]{1,0:T(8,128)(2,1)}, bf16[...) custom-call(s32[4,8]{1,0:T(4,128)} %pad_add_fusion.table, ...), custom_call_target="tpu_custom_call" | custom-call | flops 4000000000 | bytes 10000000 | tf_op jit(solution)/shard_map/send/pallas_call | solution.py:152
  14.4 5.5 %all-to-all-start = ((bf16[8,1544,128]{2,1,0:T(8,128)(2,1)}), bf16[8,1544,128]{2,1,0:T(8,128)(2,1)S(1)}, u32[]{:S(2)}, u32[]{:S(2)}) async-start(bf16[8,1544,128]{2,1,0:T(8,128)(2,1)} %get-tuple-element.60), calls=%async_computation | async-start | bytes 6324224 | tf_op jit(solution)/shard_map/all_to_all | solution.py:432
  19.8 1.3 %collective-permute-start.10 = (bf16[1544,128]{1,0:T(8,128)(2,1)}, bf16[1544,128]{1,0:T(8,128)(2,1)}, u32[]{:S(2)}, u32[]{:S(2)}) collective-permute-start(bf16[1544,128]{1,0:T(8,128)(2,1)} %get-tuple-element.61), channel_id=1, source_target_pairs={{0,64},{8,72},{16,80},{24,88},{32,96},{40,104},{48,112},{56,120},{... | collective-permute-start | bytes 1185800 | tf_op jit(solution)/shard_map/ppermute | solution.py:442
  21.1 1.3 collective-permute-start.11
  22.4 2.9 %fusion = bf16[8,256,512]{2,1,0:T(8,128)(2,1)S(1)} fusion(bf16[8,256,512]{2,1,0:T(8,128)(2,1)} %collective-permute-done, bf16[8,2,256,512]{3,2,1,0:T(8,128)(2,1)} %bitcast.45, s32[]{:T(128)S(6)} %select_n.116), kind=kLoop, calls=%fused_computation.1 | loop fusion | flops 4194304 | bytes 6291460 | tf_op jit(solution)/shard_map/convert_element_type | solution.py:431
  25.3 1.3 %copy-done.1 = bf16[8,256,512]{2,1,0:T(8,128)(2,1)} copy-done((bf16[8,256,512]{2,1,0:T(8,128)(2,1)}, bf16[8,256,512]{2,1,0:T(8,128)(2,1)S(1)}, u32[]{:S(2)}) %copy-start.1) | copy-done | bytes 2097176
  26.6 1.2 dynamic-slice_bitcast_fusion.3
  27.8 2.5 %collective-permute-start.3 = (bf16[2,256,512]{2,1,0:T(8,128)(2,1)}, bf16[2,256,512]{2,1,0:T(8,128)(2,1)}, u32[]{:S(2)}, u32[]{:S(2)}) collective-permute-start(bf16[2,256,512]{2,1,0:T(8,128)(2,1)} %get-tuple-element.106), channel_id=1, source_target_pairs={{0,3},{1,0},{2,1},{3,2},{4,7},{5,4},{6,5},{7,6},{8,11},{9,8},{10,9... | collective-permute-start | bytes 1572872 | tf_op jit(solution)/shard_map/ppermute | solution.py:394
  31.5 10.1 %home.1 = (bf16[896,2048]{1,0:T(8,128)(2,1)}, bf16[896,2048]{1,0:T(8,128)(2,1)}, bf16[896,512]{1,0:T(8,128)(2,1)}, bf16[896,512]{1,0:T(8,128)(2,1)}) custom-call(s32[1,6]{1,0:T(1,128)} %lengths.1, bf16[896,2048]{1,0:T(8,128)(2,1)} %q_hbm.1, bf16[896,512]{1,0:T(8,128)(2,1)} %k_hbm.1, bf16[896,512]{1,0:T(8,128)(2,1)} %v_hbm.1, bf16[896,2048]{1,0:T(8,128)(2,1)} %g_hbm.1), custom_call_target="tpu_custom_call" | custom-call | flops 10000000000 | bytes 10000000 | tf_op jit(solution)/shard_map/home/pallas_call | solution.py:216
  41.6 3.5 %collective-permute-start.16 = (bf16[1544,128]{1,0:T(8,128)(2,1)}, bf16[1544,128]{1,0:T(8,128)(2,1)}, u32[]{:S(2)}, u32[]{:S(2)}) collective-permute-start(bf16[1544,128]{1,0:T(8,128)(2,1)} %get-tuple-element.71), channel_id=1, source_target_pairs={{0,96},{8,104},{16,112},{24,120},{32,64},{40,72},{48,80},{56,88},{... | collective-permute-start | bytes 1185800 | tf_op jit(solution)/shard_map/ppermute | solution.py:442
  45.1 2.4 %collective-permute-start.12 = (bf16[1544,128]{1,0:T(8,128)(2,1)}, bf16[1544,128]{1,0:T(8,128)(2,1)}, u32[]{:S(2)}, u32[]{:S(2)}) collective-permute-start(bf16[1544,128]{1,0:T(8,128)(2,1)} %get-tuple-element.65), channel_id=1, source_target_pairs={{0,104},{8,96},{16,120},{24,112},{32,72},{40,64},{48,88},{56,80},{... | collective-permute-start | bytes 1185800 | tf_op jit(solution)/shard_map/ppermute | solution.py:442
  47.5 2.8 %collective-permute-start.14 = (bf16[1544,128]{1,0:T(8,128)(2,1)}, bf16[1544,128]{1,0:T(8,128)(2,1)}, u32[]{:S(2)}, u32[]{:S(2)}) collective-permute-start(bf16[1544,128]{1,0:T(8,128)(2,1)} %get-tuple-element.69), channel_id=1, source_target_pairs={{0,112},{8,120},{16,96},{24,104},{32,80},{40,88},{48,64},{56,72},{... | collective-permute-start | bytes 1185800 | tf_op jit(solution)/shard_map/ppermute | solution.py:442
  50.3 6.8 %collective-permute-done.1 = bf16[2,256,512]{2,1,0:T(8,128)(2,1)} collective-permute-done((bf16[2,256,512]{2,1,0:T(8,128)(2,1)}, bf16[2,256,512]{2,1,0:T(8,128)(2,1)}, u32[]{:S(2)}, u32[]{:S(2)}) %collective-permute-start.1) | collective-permute-done | bytes 524320 | tf_op jit(solution)/shard_map/ppermute | solution.py:394
  57.2 1.8 %fusion.3 = bf16[2,256,512]{2,1,0:T(8,128)(2,1)S(1)} fusion(bf16[2,256,512]{2,1,0:T(8,128)(2,1)} %collective-permute-done.3, bf16[2,256,512]{2,1,0:T(8,128)(2,1)} %collective-permute-done.2, bf16[2,256,512]{2,1,0:T(8,128)(2,1)} %collective-permute-done.1, bf16[2,4,256,512]{3,2,1,0:T(8,128)(2,1)} %bitcast.43, s32[]{:T(128)S(6)} %select_n.119), kind=kLoop, calls=%fused_computation.6 | loop fusion | flops 2097152 | bytes 2621444 | tf_op jit(solution)/shard_map/convert_element_type | solution.py:411
  59.8 1.9 %collective-permute-start.6 = (bf16[2,64,512]{2,1,0:T(8,128)(2,1)S(1)}, bf16[2,64,512]{2,1,0:T(8,128)(2,1)S(1)}, u32[]{:S(2)}, u32[]{:S(2)}) collective-permute-start(bf16[2,64,512]{2,1,0:T(8,128)(2,1)S(1)} %get-tuple-element.111), channel_id=1, source_target_pairs={{0,48},{16,0},{32,16},{48,32},{1,49},{17,1},{33,17},{49,33},{2,50}... | collective-permute-start | bytes 393224 | tf_op jit(solution)/shard_map/ppermute | solution.py:394
  62.3 4.3 %collective-permute-done.12.refs_5_ = bf16[1544,128]{1,0:T(8,128)(2,1)} collective-permute-done((bf16[1544,128]{1,0:T(8,128)(2,1)}, bf16[1544,128]{1,0:T(8,128)(2,1)}, u32[]{:S(2)}, u32[]{:S(2)}) %collective-permute-start.12) | collective-permute-done | bytes 395296 | tf_op jit(solution)/shard_map/ppermute | solution.py:442
  66.6 6.6 %collective-permute-done.14.refs_6_ = bf16[1544,128]{1,0:T(8,128)(2,1)} collective-permute-done((bf16[1544,128]{1,0:T(8,128)(2,1)}, bf16[1544,128]{1,0:T(8,128)(2,1)}, u32[]{:S(2)}, u32[]{:S(2)}) %collective-permute-start.14) | collective-permute-done | bytes 395296 | tf_op jit(solution)/shard_map/ppermute | solution.py:442
  73.2 5.7 %collective-permute-start.13 = (bf16[1544,128]{1,0:T(8,128)(2,1)}, bf16[1544,128]{1,0:T(8,128)(2,1)}, u32[]{:S(2)}, u32[]{:S(2)}) collective-permute-start(bf16[1544,128]{1,0:T(8,128)(2,1)} %get-tuple-element.66), channel_id=1, source_target_pairs={{0,72},{8,64},{16,88},{24,80},{32,104},{40,96},{48,120},{56,112},{... | collective-permute-start | bytes 1185800 | tf_op jit(solution)/shard_map/ppermute | solution.py:442
  79.0 8.3 %collective-permute-done.6 = bf16[2,64,512]{2,1,0:T(8,128)(2,1)S(1)} collective-permute-done((bf16[2,64,512]{2,1,0:T(8,128)(2,1)S(1)}, bf16[2,64,512]{2,1,0:T(8,128)(2,1)S(1)}, u32[]{:S(2)}, u32[]{:S(2)}) %collective-permute-start.6) | collective-permute-done | bytes 131104 | tf_op jit(solution)/shard_map/ppermute | solution.py:394
  87.2 4.1 %collective-permute-start.17 = (bf16[1544,128]{1,0:T(8,128)(2,1)}, bf16[1544,128]{1,0:T(8,128)(2,1)}, u32[]{:S(2)}, u32[]{:S(2)}) collective-permute-start(bf16[1544,128]{1,0:T(8,128)(2,1)} %get-tuple-element.77), channel_id=1, source_target_pairs={{0,120},{8,112},{16,104},{24,96},{32,88},{40,80},{48,72},{56,64},{... | collective-permute-start | bytes 1185800 | tf_op jit(solution)/shard_map/ppermute | solution.py:442
  91.4 6.5 %collective-permute-done.4 = bf16[2,64,512]{2,1,0:T(8,128)(2,1)} collective-permute-done((bf16[2,64,512]{2,1,0:T(8,128)(2,1)S(1)}, bf16[2,64,512]{2,1,0:T(8,128)(2,1)}, u32[]{:S(2)}, u32[]{:S(2)}) %collective-permute-start.4) | collective-permute-done | bytes 131104 | tf_op jit(solution)/shard_map/ppermute | solution.py:394
  97.9 1.1 fusion.6
  99.0 3.0 %collective-permute-start.7 = (bf16[64,512]{1,0:T(8,128)(2,1)S(1)}, bf16[64,512]{1,0:T(8,128)(2,1)S(1)}, u32[]{:S(2)}, u32[]{:S(2)}) collective-permute-start(bf16[64,512]{1,0:T(8,128)(2,1)S(1)} %get-tuple-element.118), channel_id=1, source_target_pairs={{0,4},{4,0},{64,68},{68,64},{1,5},{5,1},{65,69},{69,65},{2,6},{6,2... | collective-permute-start | bytes 196616 | tf_op jit(solution)/shard_map/ppermute | solution.py:451
  102.0 0.8 collective-permute-start.9
  102.8 6.0 %collective-permute-done.17.refs_7_ = bf16[1544,128]{1,0:T(8,128)(2,1)} collective-permute-done((bf16[1544,128]{1,0:T(8,128)(2,1)}, bf16[1544,128]{1,0:T(8,128)(2,1)}, u32[]{:S(2)}, u32[]{:S(2)}) %collective-permute-start.17) | collective-permute-done | bytes 395296 | tf_op jit(solution)/shard_map/ppermute | solution.py:442
  108.8 5.9 %receive.2 = (bf16[896,2048]{1,0:T(8,128)(2,1)}, bf16[896,2048]{1,0:T(8,128)(2,1)}, bf16[896,512]{1,0:T(8,128)(2,1)}, bf16[896,512]{1,0:T(8,128)(2,1)}) custom-call(bf16[8,1544,128]{2,1,0:T(8,128)(2,1)} %copy-done, bf16[1544,128]{1,0:T(8,128)(2,1)} %collective-permute-done.10.refs_0_, ...), custom_call_target="tpu_custom_call", output_to_operand_aliasing={{0}: (9, {}), {1}: (10, {}), {2}: (11, {}), {3}: (12, {})} | custom-call | flops 2000000000 | bytes 5000000 | tf_op jit(solution)/shard_map/receive/pallas_call | solution.py:354
  115.0 3.1 %collective-permute-start.19 = (bf16[64,512]{1,0:T(8,128)(2,1)S(1)}, bf16[64,512]{1,0:T(8,128)(2,1)S(1)}, u32[]{:S(2)}, u32[]{:S(2)}) collective-permute-start(bf16[64,512]{1,0:T(8,128)(2,1)S(1)} %add_convert_fusion), channel_id=1, source_target_pairs={{0,32},{16,48},{32,0},{48,16},{1,33},{17,49},{33,1},{49,17},{2,34}... | collective-permute-start | bytes 196616 | tf_op jit(solution)/shard_map/ppermute | solution.py:394
  118.1 5.9 %receive.3 = (bf16[896,2048]{1,0:T(8,128)(2,1)}, bf16[896,2048]{1,0:T(8,128)(2,1)}, bf16[896,512]{1,0:T(8,128)(2,1)}, bf16[896,512]{1,0:T(8,128)(2,1)}) custom-call(bf16[8,1544,128]{2,1,0:T(8,128)(2,1)} %copy-done, bf16[1544,128]{1,0:T(8,128)(2,1)} %collective-permute-done.10.refs_0_, ...), custom_call_target="tpu_custom_call", output_to_operand_aliasing={{0}: (9, {}), {1}: (10, {}), {2}: (11, {}), {3}: (12, {})} | custom-call | flops 2000000000 | bytes 5000000 | tf_op jit(solution)/shard_map/receive/pallas_call | solution.py:354
  124.5 1.2 collective-permute-done.21
  125.8 1.1 maximum_convert_fusion
  (47 shorter events, 4.3 us)
Async XLA Ops:
  0.6 4.5 %copy-start.6 = (s32[1,8]{1,0:T(1,128)S(1)}, s32[1,8]{1,0:T(1,128)}, u32[]{:S(2)}) copy-start(s32[1,8]{1,0:T(1,128)} %param.17) | copy-start | bytes 100
  0.6 4.5 %copy-start.3 = (s32[1,8]{1,0:T(1,128)S(1)}, s32[1,8]{1,0:T(1,128)}, u32[]{:S(2)}) copy-start(s32[1,8]{1,0:T(1,128)} %param.18) | copy-start | bytes 100
  0.7 4.5 %copy-start.4 = (s32[1,8]{1,0:T(1,128)S(1)}, s32[1,8]{1,0:T(1,128)}, u32[]{:S(2)}) copy-start(s32[1,8]{1,0:T(1,128)} %param.16) | copy-start | bytes 100
  0.7 4.5 %copy-start.5 = (s32[1,8]{1,0:T(1,128)S(1)}, s32[1,8]{1,0:T(1,128)}, u32[]{:S(2)}) copy-start(s32[1,8]{1,0:T(1,128)} %param.15) | copy-start | bytes 100
  3.7 18.7 %collective-permute-start = (bf16[8,256,512]{2,1,0:T(8,128)(2,1)}, bf16[8,256,512]{2,1,0:T(8,128)(2,1)}, u32[]{:S(2)}, u32[]{:S(2)}) collective-permute-start(bf16[8,256,512]{2,1,0:T(8,128)(2,1)} %dynamic-slice_bitcast_fusion), channel_id=1, source_target_pairs={{0,8},{8,0},{1,9},{9,1},{2,10},{10,2},{3,11},{11,3},{4,12},{12,4},... | collective-permute-start | bytes 6291464 | tf_op jit(solution)/shard_map/ppermute | solution.py:383
  14.4 88.4 %all-to-all-start = ((bf16[8,1544,128]{2,1,0:T(8,128)(2,1)}), bf16[8,1544,128]{2,1,0:T(8,128)(2,1)S(1)}, u32[]{:S(2)}, u32[]{:S(2)}) async-start(bf16[8,1544,128]{2,1,0:T(8,128)(2,1)} %get-tuple-element.60), calls=%async_computation | async-start | bytes 6324224 | tf_op jit(solution)/shard_map/all_to_all | solution.py:432
  19.8 25.3 %collective-permute-start.10 = (bf16[1544,128]{1,0:T(8,128)(2,1)}, bf16[1544,128]{1,0:T(8,128)(2,1)}, u32[]{:S(2)}, u32[]{:S(2)}) collective-permute-start(bf16[1544,128]{1,0:T(8,128)(2,1)} %get-tuple-element.61), channel_id=1, source_target_pairs={{0,64},{8,72},{16,80},{24,88},{32,96},{40,104},{48,112},{56,120},{... | collective-permute-start | bytes 1185800 | tf_op jit(solution)/shard_map/ppermute | solution.py:442
  21.1 20.5 %collective-permute-start.11 = (bf16[1544,128]{1,0:T(8,128)(2,1)}, bf16[1544,128]{1,0:T(8,128)(2,1)}, u32[]{:S(2)}, u32[]{:S(2)}) collective-permute-start(bf16[1544,128]{1,0:T(8,128)(2,1)} %get-tuple-element.64), channel_id=1, source_target_pairs={{0,80},{8,88},{16,64},{24,72},{32,112},{40,120},{48,96},{56,104},{... | collective-permute-start | bytes 1185800 | tf_op jit(solution)/shard_map/ppermute | solution.py:442
  25.3 1.3 %copy-start.1 = (bf16[8,256,512]{2,1,0:T(8,128)(2,1)}, bf16[8,256,512]{2,1,0:T(8,128)(2,1)S(1)}, u32[]{:S(2)}) copy-start(bf16[8,256,512]{2,1,0:T(8,128)(2,1)S(1)} %fusion) | copy-start | bytes 6291460
  27.8 19.7 %collective-permute-start.3 = (bf16[2,256,512]{2,1,0:T(8,128)(2,1)}, bf16[2,256,512]{2,1,0:T(8,128)(2,1)}, u32[]{:S(2)}, u32[]{:S(2)}) collective-permute-start(bf16[2,256,512]{2,1,0:T(8,128)(2,1)} %get-tuple-element.106), channel_id=1, source_target_pairs={{0,3},{1,0},{2,1},{3,2},{4,7},{5,4},{6,5},{7,6},{8,11},{9,8},{10,9... | collective-permute-start | bytes 1572872 | tf_op jit(solution)/shard_map/ppermute | solution.py:394
  30.3 20.1 %collective-permute-start.2 = (bf16[2,256,512]{2,1,0:T(8,128)(2,1)}, bf16[2,256,512]{2,1,0:T(8,128)(2,1)}, u32[]{:S(2)}, u32[]{:S(2)}) collective-permute-start(bf16[2,256,512]{2,1,0:T(8,128)(2,1)} %get-tuple-element.107), channel_id=1, source_target_pairs={{0,2},{1,3},{2,0},{3,1},{4,6},{5,7},{6,4},{7,5},{8,10},{9,11},{10,... | collective-permute-start | bytes 1572872 | tf_op jit(solution)/shard_map/ppermute | solution.py:394
  30.8 26.4 %collective-permute-start.1 = (bf16[2,256,512]{2,1,0:T(8,128)(2,1)}, bf16[2,256,512]{2,1,0:T(8,128)(2,1)}, u32[]{:S(2)}, u32[]{:S(2)}) collective-permute-start(bf16[2,256,512]{2,1,0:T(8,128)(2,1)} %get-tuple-element.105), channel_id=1, source_target_pairs={{0,1},{1,2},{2,3},{3,0},{4,5},{5,6},{6,7},{7,4},{8,9},{9,10},{10,1... | collective-permute-start | bytes 1572872 | tf_op jit(solution)/shard_map/ppermute | solution.py:394
  41.6 37.3 %collective-permute-start.16 = (bf16[1544,128]{1,0:T(8,128)(2,1)}, bf16[1544,128]{1,0:T(8,128)(2,1)}, u32[]{:S(2)}, u32[]{:S(2)}) collective-permute-start(bf16[1544,128]{1,0:T(8,128)(2,1)} %get-tuple-element.71), channel_id=1, source_target_pairs={{0,96},{8,104},{16,112},{24,120},{32,64},{40,72},{48,80},{56,88},{... | collective-permute-start | bytes 1185800 | tf_op jit(solution)/shard_map/ppermute | solution.py:442
  45.1 21.5 %collective-permute-start.12 = (bf16[1544,128]{1,0:T(8,128)(2,1)}, bf16[1544,128]{1,0:T(8,128)(2,1)}, u32[]{:S(2)}, u32[]{:S(2)}) collective-permute-start(bf16[1544,128]{1,0:T(8,128)(2,1)} %get-tuple-element.65), channel_id=1, source_target_pairs={{0,104},{8,96},{16,120},{24,112},{32,72},{40,64},{48,88},{56,80},{... | collective-permute-start | bytes 1185800 | tf_op jit(solution)/shard_map/ppermute | solution.py:442
  47.5 25.7 %collective-permute-start.14 = (bf16[1544,128]{1,0:T(8,128)(2,1)}, bf16[1544,128]{1,0:T(8,128)(2,1)}, u32[]{:S(2)}, u32[]{:S(2)}) collective-permute-start(bf16[1544,128]{1,0:T(8,128)(2,1)} %get-tuple-element.69), channel_id=1, source_target_pairs={{0,112},{8,120},{16,96},{24,104},{32,80},{40,88},{48,64},{56,72},{... | collective-permute-start | bytes 1185800 | tf_op jit(solution)/shard_map/ppermute | solution.py:442
  59.0 0.8 copy-start.2
  59.8 27.5 %collective-permute-start.6 = (bf16[2,64,512]{2,1,0:T(8,128)(2,1)S(1)}, bf16[2,64,512]{2,1,0:T(8,128)(2,1)S(1)}, u32[]{:S(2)}, u32[]{:S(2)}) collective-permute-start(bf16[2,64,512]{2,1,0:T(8,128)(2,1)S(1)} %get-tuple-element.111), channel_id=1, source_target_pairs={{0,48},{16,0},{32,16},{48,32},{1,49},{17,1},{33,17},{49,33},{2,50}... | collective-permute-start | bytes 393224 | tf_op jit(solution)/shard_map/ppermute | solution.py:394
  61.6 29.7 %collective-permute-start.5 = (bf16[2,64,512]{2,1,0:T(8,128)(2,1)S(1)}, bf16[2,64,512]{2,1,0:T(8,128)(2,1)}, u32[]{:S(2)}, u32[]{:S(2)}) collective-permute-start(bf16[2,64,512]{2,1,0:T(8,128)(2,1)S(1)} %get-tuple-element.112), channel_id=1, source_target_pairs={{0,32},{16,48},{32,0},{48,16},{1,33},{17,49},{33,1},{49,17},{2,34}... | collective-permute-start | bytes 393224 | tf_op jit(solution)/shard_map/ppermute | solution.py:394
  66.6 31.3 %collective-permute-start.4 = (bf16[2,64,512]{2,1,0:T(8,128)(2,1)S(1)}, bf16[2,64,512]{2,1,0:T(8,128)(2,1)}, u32[]{:S(2)}, u32[]{:S(2)}) collective-permute-start(bf16[2,64,512]{2,1,0:T(8,128)(2,1)S(1)} %get-tuple-element.110), channel_id=1, source_target_pairs={{0,16},{16,32},{32,48},{48,0},{1,17},{17,33},{33,49},{49,1},{2,18}... | collective-permute-start | bytes 393224 | tf_op jit(solution)/shard_map/ppermute | solution.py:394
  73.2 29.6 %collective-permute-start.13 = (bf16[1544,128]{1,0:T(8,128)(2,1)}, bf16[1544,128]{1,0:T(8,128)(2,1)}, u32[]{:S(2)}, u32[]{:S(2)}) collective-permute-start(bf16[1544,128]{1,0:T(8,128)(2,1)} %get-tuple-element.66), channel_id=1, source_target_pairs={{0,72},{8,64},{16,88},{24,80},{32,104},{40,96},{48,120},{56,112},{... | collective-permute-start | bytes 1185800 | tf_op jit(solution)/shard_map/ppermute | solution.py:442
  79.0 23.8 %collective-permute-start.15 = (bf16[1544,128]{1,0:T(8,128)(2,1)}, bf16[1544,128]{1,0:T(8,128)(2,1)}, u32[]{:S(2)}, u32[]{:S(2)}) collective-permute-start(bf16[1544,128]{1,0:T(8,128)(2,1)} %get-tuple-element.70), channel_id=1, source_target_pairs={{0,88},{8,80},{16,72},{24,64},{32,120},{40,112},{48,104},{56,96},{... | collective-permute-start | bytes 1185800 | tf_op jit(solution)/shard_map/ppermute | solution.py:442
  87.2 21.5 %collective-permute-start.17 = (bf16[1544,128]{1,0:T(8,128)(2,1)}, bf16[1544,128]{1,0:T(8,128)(2,1)}, u32[]{:S(2)}, u32[]{:S(2)}) collective-permute-start(bf16[1544,128]{1,0:T(8,128)(2,1)} %get-tuple-element.77), channel_id=1, source_target_pairs={{0,120},{8,112},{16,104},{24,96},{32,88},{40,80},{48,72},{56,64},{... | collective-permute-start | bytes 1185800 | tf_op jit(solution)/shard_map/ppermute | solution.py:442
  99.0 15.6 %collective-permute-start.7 = (bf16[64,512]{1,0:T(8,128)(2,1)S(1)}, bf16[64,512]{1,0:T(8,128)(2,1)S(1)}, u32[]{:S(2)}, u32[]{:S(2)}) collective-permute-start(bf16[64,512]{1,0:T(8,128)(2,1)S(1)} %get-tuple-element.118), channel_id=1, source_target_pairs={{0,4},{4,0},{64,68},{68,64},{1,5},{5,1},{65,69},{69,65},{2,6},{6,2... | collective-permute-start | bytes 196616 | tf_op jit(solution)/shard_map/ppermute | solution.py:451
  102.0 12.7 %collective-permute-start.9 = (bf16[64,512]{1,0:T(8,128)(2,1)S(1)}, bf16[64,512]{1,0:T(8,128)(2,1)S(1)}, u32[]{:S(2)}, u32[]{:S(2)}) collective-permute-start(bf16[64,512]{1,0:T(8,128)(2,1)S(1)} %get-tuple-element.118), channel_id=1, source_target_pairs={{0,68},{4,64},{64,4},{68,0},{1,69},{5,65},{65,5},{69,1},{2,70},{6,... | collective-permute-start | bytes 196616 | tf_op jit(solution)/shard_map/ppermute | solution.py:451
  102.8 11.9 %collective-permute-start.8 = (bf16[64,512]{1,0:T(8,128)(2,1)S(1)}, bf16[64,512]{1,0:T(8,128)(2,1)S(1)}, u32[]{:S(2)}, u32[]{:S(2)}) collective-permute-start(bf16[64,512]{1,0:T(8,128)(2,1)S(1)} %get-tuple-element.117), channel_id=1, source_target_pairs={{0,64},{4,68},{64,0},{68,4},{1,65},{5,69},{65,1},{69,5},{2,66},{6,... | collective-permute-start | bytes 196616 | tf_op jit(solution)/shard_map/ppermute | solution.py:451
  102.8 6.0 %copy-start = (bf16[8,1544,128]{2,1,0:T(8,128)(2,1)}, bf16[8,1544,128]{2,1,0:T(8,128)(2,1)S(1)}, u32[]{:S(2)}) copy-start(bf16[8,1544,128]{2,1,0:T(8,128)(2,1)S(1)} %all-to-all-done.near) | copy-start | bytes 9486340
  114.7 9.2 %collective-permute-start.18 = (bf16[64,512]{1,0:T(8,128)(2,1)S(1)}, bf16[64,512]{1,0:T(8,128)(2,1)S(1)}, u32[]{:S(2)}, u32[]{:S(2)}) collective-permute-start(bf16[64,512]{1,0:T(8,128)(2,1)S(1)} %add_convert_fusion), channel_id=1, source_target_pairs={{0,16},{16,32},{32,48},{48,0},{1,17},{17,33},{33,49},{49,1},{2,18}... | collective-permute-start | bytes 196616 | tf_op jit(solution)/shard_map/ppermute | solution.py:394
  115.0 9.0 %collective-permute-start.19 = (bf16[64,512]{1,0:T(8,128)(2,1)S(1)}, bf16[64,512]{1,0:T(8,128)(2,1)S(1)}, u32[]{:S(2)}, u32[]{:S(2)}) collective-permute-start(bf16[64,512]{1,0:T(8,128)(2,1)S(1)} %add_convert_fusion), channel_id=1, source_target_pairs={{0,32},{16,48},{32,0},{48,16},{1,33},{17,49},{33,1},{49,17},{2,34}... | collective-permute-start | bytes 196616 | tf_op jit(solution)/shard_map/ppermute | solution.py:394
  118.1 5.9 %collective-permute-start.20 = (bf16[64,512]{1,0:T(8,128)(2,1)S(1)}, bf16[64,512]{1,0:T(8,128)(2,1)S(1)}, u32[]{:S(2)}, u32[]{:S(2)}) collective-permute-start(bf16[64,512]{1,0:T(8,128)(2,1)S(1)} %add_convert_fusion), channel_id=1, source_target_pairs={{0,48},{16,0},{32,16},{48,32},{1,49},{17,1},{33,17},{49,33},{2,50}... | collective-permute-start | bytes 196616 | tf_op jit(solution)/shard_map/ppermute | solution.py:394
  124.1 1.6 %collective-permute-start.21 = (bf16[256,512]{1,0:T(8,128)(2,1)S(1)}, bf16[256,512]{1,0:T(8,128)(2,1)S(1)}, u32[]{:S(2)}, u32[]{:S(2)}) collective-permute-start(bf16[256,512]{1,0:T(8,128)(2,1)S(1)} %pad_maximum_fusion.1), channel_id=1, source_target_pairs={{0,8},{8,0},{1,9},{9,1},{2,10},{10,2},{3,11},{11,3},{4,12},{12,4},... | collective-permute-start | bytes 786440 | tf_op jit(solution)/shard_map/ppermute | solution.py:383
